TPU v7x, 32 devices: a whole 2x2x4 slice. The times are simulated.
32 devices in a mesh: seq: 16 (over z, x, core), fsdp: 2 (over y).
Axes of the slice: x: 2, y: 2, z: 4, core: 2. Of those that a mesh axis runs over, the one named last changes fastest.
Arguments:
- prompt: bfloat16 [2, 256, 4096], P('fsdp'), may hold values from -6 to 6
- lengths: int32 [2], P('fsdp'), may hold values from 1 to 256, 384 in all
- timesteps: int32 [2], P('fsdp'), may hold values from 0 to 999
- ref_errors: float32 [2, 2], P('fsdp'), may hold values from 4.2 to 4.45
- gain_ffn: float32 [4096], replicated, may hold values from 0.5 to 1.5
- w_in_gate: bfloat16 [4096, 8192], P('fsdp', 'seq'), may hold values from -0.09375 to 0.09375
- w_in_up: bfloat16 [4096, 8192], P('fsdp', 'seq'), may hold values from -0.09375 to 0.09375
- w_in_down: bfloat16 [8192, 4096], P('seq', 'fsdp'), may hold values from -0.0625 to 0.0625
- gain_final: float32 [4096], replicated, may hold values from 0.5 to 1.5
- w_context: bfloat16 [4096, 2048], P('fsdp', 'seq'), may hold values from -0.09375 to 0.09375
- image_q: bfloat16 [2, 2, 1024, 1024], P('fsdp', None, 'seq'), may hold values from -128 to 128
- image_k: bfloat16 [2, 2, 1024, 1024], P('fsdp', None, 'seq'), may hold values from -4 to 4
- image_v: bfloat16 [2, 2, 1024, 1024], P('fsdp', None, 'seq'), may hold values from -6 to 6
- w_out: bfloat16 [1024, 1280], P('fsdp'), may hold values from -0.1875 to 0.1875
- target: bfloat16 [2, 2, 1024, 1280], P('fsdp', None, 'seq'), may hold values from -12 to 12
Outputs:
- pair_loss: float32 [2], P('fsdp')
- grad_q: bfloat16 [2, 2, 1024, 1024], P('fsdp', None, None, 'seq')
- grad_k: bfloat16 [2, 2, 1024, 1024], P('fsdp', None, None, 'seq')
- grad_v: bfloat16 [2, 2, 1024, 1024], P('fsdp', None, None, 'seq')
All inputs are finite; a program needn't handle non-finite values. No bound on the sum of `lengths` on one device may be relied on, other than what follows from the above.
Results may differ from a plain program's by a relative error of at most 0.029.
Values may be sent and summed in bfloat16 or wider, within the bound.
No kernel may reach another device: no remote copies, remote signals or barrier semaphores. Data moves between devices by JAX's collectives and lax.ppermute only.
A program may use at most 128 MiB of HBM per device.

v0:
```python
import math

import jax
import jax.numpy as jnp
from jax import lax
from jax.sharding import PartitionSpec as P

PROMPT = 256
HEAD = 64
CH = 1280


dpo_beta = 20.0
norm_eps = 1e-06


def rms_gain(values, gain):
    mean_sq = jnp.mean(values * values, axis=-1, keepdims=True)
    return values * lax.rsqrt(mean_sq + norm_eps) * gain


def noise_level(step_index):
    fraction = (step_index.astype(jnp.float32) + 1.0) / 1000.0
    return 3.0 * fraction / (1.0 + 2.0 * fraction)


def softmax_rows(queries, key_rows, key_mask):
    scores = jnp.einsum("qh,kh->qk", queries, key_rows, preferred_element_type=jnp.float32) * (
        1.0 / math.sqrt(HEAD)
    )
    scores = jnp.where(key_mask[None, :], scores, -jnp.inf)
    top_score = jnp.max(scores, axis=-1, keepdims=True)
    weights = jnp.exp(scores - top_score)
    return (weights / jnp.sum(weights, axis=-1, keepdims=True)).astype(jnp.bfloat16)


def stream_forward(queries, key_rows, value_rows, key_mask):
    seq_len = queries.shape[0]
    block_rows = min(512, seq_len)
    query_blocks = queries.reshape(seq_len // block_rows, block_rows, HEAD)

    def one_block(query_block):
        probs_bf = softmax_rows(query_block, key_rows, key_mask)
        return jnp.dot(probs_bf, value_rows, preferred_element_type=jnp.float32).astype(
            jnp.bfloat16
        )

    return lax.map(one_block, query_blocks).reshape(seq_len, HEAD)


def stream_backward(queries, key_rows, value_rows, key_mask, attended, grad_out):
    seq_len = queries.shape[0]
    block_rows = min(512, seq_len)
    block_count = seq_len // block_rows

    def one_block(carried, pieces):
        key_acc, value_acc = carried
        query_block, out_block, grad_block = pieces
        probs_bf = softmax_rows(query_block, key_rows, key_mask)
        grad_prob = jnp.einsum(
            "qh,kh->qk", grad_block, value_rows, preferred_element_type=jnp.float32
        )
        row_delta = jnp.sum(
            grad_block.astype(jnp.float32) * out_block.astype(jnp.float32), axis=-1, keepdims=True
        )
        grad_score = (
            probs_bf.astype(jnp.float32) * (grad_prob - row_delta) * (1.0 / math.sqrt(HEAD))
        ).astype(jnp.bfloat16)
        grad_query = jnp.dot(grad_score, key_rows, preferred_element_type=jnp.float32).astype(
            jnp.bfloat16
        )
        key_acc = key_acc + jnp.einsum(
            "qk,qh->kh", grad_score[:, :seq_len], query_block, preferred_element_type=jnp.float32
        )
        value_acc = value_acc + jnp.einsum(
            "qk,qh->kh", probs_bf[:, :seq_len], grad_block, preferred_element_type=jnp.float32
        )
        return ((key_acc, value_acc), grad_query)

    zeros_acc = jnp.zeros((seq_len, HEAD), jnp.float32)
    shaped = (
        queries.reshape(block_count, block_rows, HEAD),
        attended.reshape(block_count, block_rows, HEAD),
        grad_out.reshape(block_count, block_rows, HEAD),
    )
    (key_acc, value_acc), grad_query = lax.scan(one_block, (zeros_acc, zeros_acc), shaped)
    return (
        grad_query.reshape(seq_len, HEAD),
        key_acc.astype(jnp.bfloat16),
        value_acc.astype(jnp.bfloat16),
    )


def on_device(
    prompt,
    lengths,
    timesteps,
    ref_errors,
    gain_ffn,
    w_in_gate,
    w_in_up,
    w_in_down,
    gain_final,
    w_context,
    image_q,
    image_k,
    image_v,
    w_out,
    target,
):
    gate_full, up_full, down_full, context_full, out_full = (
        lax.all_gather(w_in_gate, "fsdp", axis=0, tiled=True),
        lax.all_gather(w_in_up, "fsdp", axis=0, tiled=True),
        lax.all_gather(w_in_down, "fsdp", axis=1, tiled=True),
        lax.all_gather(w_context, "fsdp", axis=0, tiled=True),
        lax.all_gather(w_out, "fsdp", axis=0, tiled=True),
    )
    prompt_f32 = prompt[0].astype(jnp.float32)
    normed = rms_gain(prompt_f32, gain_ffn).astype(jnp.bfloat16)
    gate_act = jnp.dot(normed, gate_full, preferred_element_type=jnp.float32)
    up_act = jnp.dot(normed, up_full, preferred_element_type=jnp.float32)
    hidden = (jax.nn.gelu(gate_act, approximate=True) * up_act).astype(jnp.bfloat16)
    partial_value = jnp.dot(hidden, down_full, preferred_element_type=jnp.float32)
    summed = lax.psum(partial_value.astype(jnp.bfloat16), "seq").astype(jnp.float32)
    encoded = rms_gain(prompt_f32 + summed, gain_final).astype(jnp.bfloat16)
    context = jnp.dot(encoded, context_full, preferred_element_type=jnp.float32).astype(
        jnp.bfloat16
    )
    text_keys = context[:, :HEAD]
    text_values = context[:, HEAD:]
    q_heads, k_heads, v_heads = (
        lax.all_to_all(image_q, "seq", split_axis=3, concat_axis=2, tiled=True),
        lax.all_to_all(image_k, "seq", split_axis=3, concat_axis=2, tiled=True),
        lax.all_to_all(image_v, "seq", split_axis=3, concat_axis=2, tiled=True),
    )
    seq_len = q_heads.shape[2]
    key_mask = jnp.arange(seq_len + PROMPT) < seq_len + lengths[0]
    key_sets = []
    value_sets = []
    head_outs = []
    for stream in range(2):
        key_rows = jnp.concatenate([k_heads[0, stream], text_keys], axis=0)
        value_rows = jnp.concatenate([v_heads[0, stream], text_values], axis=0)
        key_sets.append(key_rows)
        value_sets.append(value_rows)
        head_outs.append(stream_forward(q_heads[0, stream], key_rows, value_rows, key_mask))
    attended = jnp.stack(head_outs)[None]
    tok_out = lax.all_to_all(attended, "seq", split_axis=2, concat_axis=3, tiled=True)
    predicted = jnp.einsum("sti,ic->stc", tok_out[0], out_full, preferred_element_type=jnp.float32)
    residual = predicted - target[0].astype(jnp.float32)
    partial_err = jnp.sum(residual * residual, axis=(1, 2))
    error_sums = lax.psum(partial_err, "seq")
    mean_errors = error_sums / (seq_len * CH)
    error_gap = mean_errors[0] - ref_errors[0, 0] - (mean_errors[1] - ref_errors[0, 1])
    sigma_t = noise_level(timesteps[0])
    logit_value = dpo_beta * sigma_t * error_gap
    pair_loss = jax.nn.softplus(logit_value)[None]
    coefficient = sigma_t * jax.nn.sigmoid(logit_value)
    stream_signs = jnp.stack([coefficient, -coefficient])
    grad_pred = (stream_signs[:, None, None] * residual).astype(jnp.bfloat16)
    grad_tok = jnp.einsum(
        "stc,ic->sti", grad_pred, out_full, preferred_element_type=jnp.float32
    ).astype(jnp.bfloat16)
    grad_heads = lax.all_to_all(grad_tok[None], "seq", split_axis=3, concat_axis=2, tiled=True)
    query_grads = []
    key_grads = []
    value_grads = []
    for stream in range(2):
        grad_query, grad_key, grad_value = stream_backward(
            q_heads[0, stream],
            key_sets[stream],
            value_sets[stream],
            key_mask,
            head_outs[stream],
            grad_heads[0, stream],
        )
        query_grads.append(grad_query)
        key_grads.append(grad_key)
        value_grads.append(grad_value)
    return (
        pair_loss,
        jnp.stack(query_grads)[None],
        jnp.stack(key_grads)[None],
        jnp.stack(value_grads)[None],
    )


def solution(mesh):
    return jax.shard_map(
        on_device,
        mesh=mesh,
        in_specs=(
            P("fsdp", None, None),
            P("fsdp"),
            P("fsdp"),
            P("fsdp", None),
            P(),
            P("fsdp", "seq"),
            P("fsdp", "seq"),
            P("seq", "fsdp"),
            P(),
            P("fsdp", "seq"),
            P("fsdp", None, "seq", None),
            P("fsdp", None, "seq", None),
            P("fsdp", None, "seq", None),
            P("fsdp", None),
            P("fsdp", None, "seq", None),
        ),
        out_specs=(
            P("fsdp"),
            P("fsdp", None, None, "seq"),
            P("fsdp", None, None, "seq"),
            P("fsdp", None, None, "seq"),
        ),
        check_vma=False,
    )
```

profile of v0, /device:TPU:0, one launch (start us, length us, event | category | flops | bytes accessed | tf_op | source)
XLA Modules:
  0.0 485.4 jit_solution(12774204976036497098)
XLA Ops:
  10.0 59.0 %all-gather.6.cloned.1.call-done = bf16[4096,512]{1,0:T(8,128)(2,1)} async-done(((bf16[2048,512]{1,0:T(8,128)(2,1)}), bf16[4096,512]{1,0:T(8,128)(2,1)}) %all-gather.6.cloned.1.call-update) | async-done | bytes 4194320 | tf_op jit(solution)/shard_map/all_gather | solution.py:112
  69.0 3.6 fusion.102
  72.6 54.7 %all-gather.10.cloned.1.call-done = bf16[512,4096]{1,0:T(8,128)(2,1)} async-done(((bf16[512,2048]{1,0:T(8,128)(2,1)}), bf16[512,4096]{1,0:T(8,128)(2,1)}) %all-gather.10.cloned.1.call-update) | async-done | bytes 4194320 | tf_op jit(solution)/shard_map/all_gather | solution.py:114
  127.3 58.3 %all-gather.8.cloned.1.call-done = bf16[4096,512]{1,0:T(8,128)(2,1)} async-done(((bf16[2048,512]{1,0:T(8,128)(2,1)}), bf16[4096,512]{1,0:T(8,128)(2,1)}) %all-gather.8.cloned.1.call-update) | async-done | bytes 4194320 | tf_op jit(solution)/shard_map/all_gather | solution.py:113
  185.6 7.3 %convolution_convert_fusion.2 = bf16[256,4096]{1,0:T(8,128)(2,1)} fusion(bf16[512,4096]{1,0:T(8,128)(2,1)} %all-gather.10.cloned.1.call-done, f32[256,512]{1,0:T(8,128)S(1)} %fusion.102, bf16[4096,512]{1,0:T(8,128)(2,1)} %all-gather.8.cloned.1.call-done, bf16[1,256,4096]{2,1,0:T(8,128)(2,1)S(1)} %copy-done.4, f32[4096]{0:T(1024)S(1)} %copy-done.15, ...), kind=kOutput, calls=%fused_computation.97 | convolution fusion | flops 2152988672 | bytes 13124608 | tf_op jit(solution)/shard_map/dot_general | solution.py:123
  194.3 1.1 reshape.73
  195.4 5.6 %all-to-all-start.2 = ((bf16[16,2,4096]{2,1,0:T(2,128)(2,1)}), bf16[16,2,4096]{2,1,0:T(2,128)(2,1)S(1)}, u32[]{:S(2)}, u32[]{:S(2)}) async-start(bf16[16,2,4096]{2,1,0:T(2,128)(2,1)} %reshape.73), calls=%async_computation.2 | async-start | bytes 524288 | tf_op jit(solution)/shard_map/all_to_all | solution.py:134
  201.4 1.1 reshape.71
  202.5 11.2 %all-to-all-done.2 = bf16[16,2,4096]{2,1,0:T(2,128)(2,1)S(1)} async-done(((bf16[16,2,4096]{2,1,0:T(2,128)(2,1)}), bf16[16,2,4096]{2,1,0:T(2,128)(2,1)S(1)}, u32[]{:S(2)}, u32[]{:S(2)}) %all-to-all-start.2) | async-done | bytes 262176 | tf_op jit(solution)/shard_map/all_to_all | solution.py:134
  213.7 3.5 all-to-all-start.1
  217.3 1.3 copy.69
  218.6 1.1 reshape.69
  219.7 10.4 %all-to-all-done.1 = bf16[16,2,4096]{2,1,0:T(2,128)(2,1)S(1)} async-done(((bf16[16,2,4096]{2,1,0:T(2,128)(2,1)}), bf16[16,2,4096]{2,1,0:T(2,128)(2,1)S(1)}, u32[]{:S(2)}, u32[]{:S(2)}) %all-to-all-start.1) | async-done | bytes 262176 | tf_op jit(solution)/shard_map/all_to_all | solution.py:133
  230.1 4.2 all-to-all-start
  236.4 2.2 reshape.72
  238.5 1.4 copy.72
  241.4 4.5 all-to-all-done
  246.0 1.3 reshape.70
  249.1 50.5 %all-reduce.2.cloned.1.call-done = bf16[256,4096]{1,0:T(8,128)(2,1)} async-done(((bf16[256,4096]{1,0:T(8,128)(2,1)}), bf16[256,4096]{1,0:T(8,128)(2,1)}) %all-reduce.2.cloned.1.call-update) | async-done | bytes 2097168 | tf_op jit(solution)/shard_map/psum | solution.py:124
  299.6 2.4 multiply_reduce_fusion
  302.0 19.6 %all-gather.12.cloned.1.call-done = bf16[4096,128]{1,0:T(8,128)(2,1)} async-done(((bf16[2048,128]{1,0:T(8,128)(2,1)}), bf16[4096,128]{1,0:T(8,128)(2,1)}) %all-gather.12.cloned.1.call-update) | async-done | bytes 1048592 | tf_op jit(solution)/shard_map/all_gather | solution.py:115
  321.6 3.0 fusion.91
  324.8 1.2 pad_maximum_fusion.1
  326.7 6.9 %while.52 = (s32[]{:T(128)}, bf16[2,512,64]{1,2,0:T(8,128)(2,1)}, bf16[2,512,64]{2,1,0:T(8,128)(2,1)}, bf16[1280,64]{1,0:T(8,128)(2,1)S(1)}, bf16[1280,64]{1,0:T(8,128)(2,1)S(1)}, /*index=5*/s32[]{:T(128)}, s32[]{:T(128)}) while((s32[]{:T(128)}, bf16[2,512,64]{1,2,0:T(8,128)(2,1)}, bf16[2,512,64]{2,1,0:T(8,128)(2,1)}, ...), condition=%wide.region_6.7_spmd.clone, body=%wide.region_3.6_spmd.clone.sunk | while | flops 173048064 | bytes 8402513 | solution.py:48
  326.7 1.5 fusion.172
  328.8 1.4 fusion.174
  330.1 1.5 fusion.172
  332.2 1.4 fusion.174
  333.6 1.2 copy.78
  334.8 3.9 while.53
  339.4 1.1 reshape.75
  340.5 5.6 %all-to-all-start.3 = ((bf16[16,2,4096]{2,1,0:T(2,128)(2,1)}), bf16[16,2,4096]{2,1,0:T(2,128)(2,1)S(1)}, u32[]{:S(2)}, u32[]{:S(2)}) async-start(bf16[16,2,4096]{2,1,0:T(2,128)(2,1)} %reshape.75), calls=%async_computation.3 | async-start | bytes 524288 | tf_op jit(solution)/shard_map/all_to_all | solution.py:148
  347.5 8.7 %all-to-all-done.3 = bf16[16,2,4096]{2,1,0:T(2,128)(2,1)S(1)} async-done(((bf16[16,2,4096]{2,1,0:T(2,128)(2,1)}), bf16[16,2,4096]{2,1,0:T(2,128)(2,1)S(1)}, u32[]{:S(2)}, u32[]{:S(2)}) %all-to-all-start.3) | async-done | bytes 262176 | tf_op jit(solution)/shard_map/all_to_all | solution.py:148
  357.9 4.1 all-gather.14.cloned.1.call-done
  362.0 3.4 multiply_reduce_fusion.1
  365.4 33.0 %psum.15 = f32[2]{0:T(128)S(1)} all-reduce(f32[2]{0:T(128)S(1)} %get-tuple-element.468), channel_id=1, replica_groups=mesh['seq'=16,'fsdp'=2] {'seq'}, use_global_device_ids=true, to_apply=%region_12.13 | all-reduce | flops 2 | bytes 16 | tf_op jit(solution)/shard_map/psum | solution.py:152
  401.7 2.8 fusion.88
  404.5 1.3 copy.86
  405.7 1.1 reshape.77
  406.8 3.8 all-to-all-start.4
  410.7 9.6 %all-to-all-done.4 = bf16[16,2,4096]{2,1,0:T(2,128)(2,1)S(1)} async-done(((bf16[16,2,4096]{2,1,0:T(2,128)(2,1)}), bf16[16,2,4096]{2,1,0:T(2,128)(2,1)S(1)}, u32[]{:S(2)}, u32[]{:S(2)}) %all-to-all-start.4) | async-done | bytes 262176 | tf_op jit(solution)/shard_map/all_to_all | solution.py:164
  423.6 22.8 %while.54 = (s32[]{:T(128)}, f32[1024,64]{0,1:T(8,128)}, f32[1024,64]{0,1:T(8,128)}, bf16[2,512,64]{1,2,0:T(8,128)(2,1)}, bf16[2,512,64]{2,1,0:T(8,128)(2,1)}, /...) while((s32[]{:T(128)}, f32[1024,64]{0,1:T(8,128)}, ...), condition=%wide.region_17.18_spmd.clone, body=%wide.region_13.17_spmd.clone.sunk | while | flops 394821376 | bytes 17910924 | solution.py:86
  423.6 1.5 fusion.189
  428.2 1.6 fusion.192
  429.8 1.9 convolution_add_fusion.8
  431.7 1.1 fusion.193
  432.9 1.9 convolution_add_fusion.9
  434.8 1.5 fusion.189
  439.4 1.6 fusion.192
  441.1 2.1 convolution_add_fusion.8
  443.1 1.2 fusion.193
  444.3 2.1 convolution_add_fusion.9
  446.3 1.6 convert_bitcast_fusion.1
  448.0 1.7 copy.99
  450.4 18.9 %while.55 = (s32[]{:T(128)}, f32[1024,64]{0,1:T(8,128)}, f32[1024,64]{0,1:T(8,128)}, bf16[2,512,64]{1,2,0:T(8,128)(2,1)}, bf16[2,512,64]{2,1,0:T(8,128)(2,1)S(1)...) while((s32[]{:T(128)}, f32[1024,64]{0,1:T(8,128)}, ...), condition=%wide.region_22.23_spmd.clone, body=%wide.region_18.22_spmd.clone.sunk | while | flops 394821376 | bytes 21187588 | solution.py:86
  453.6 1.5 fusion.206
  455.1 1.1 convolution_add_fusion.10
  456.2 1.1 fusion.207
  457.3 1.3 convolution_add_fusion.11
  462.6 1.5 fusion.206
  464.1 2.0 convolution_add_fusion.10
  466.1 1.1 fusion.207
  467.3 1.3 convolution_add_fusion.11
  474.4 1.6 maximum_bitcast_fusion.3
  (143 shorter events, 43.1 us)
Async XLA Ops:
  7.2 2.3 copy-start.4
  7.2 61.8 %all-gather.6.cloned.1.call-start = ((), (), s32[]{:S(2)}) async-start(), calls=%async_computation.5 | async-start | bytes 6291456 | tf_op jit(solution)/shard_map/all_gather | solution.py:112
  7.9 119.4 %all-gather.10.cloned.1.call-start = ((), (), s32[]{:S(2)}) async-start(), calls=%async_computation.7 | async-start | bytes 6291456 | tf_op jit(solution)/shard_map/all_gather | solution.py:114
  8.7 60.4 %copy-start.15 = (f32[4096]{0:T(1024)S(1)}, f32[4096]{0:T(1024)}, u32[]{:S(2)}) copy-start(f32[4096]{0:T(1024)} %param.27) | copy-start | bytes 49156
  8.7 176.9 %all-gather.8.cloned.1.call-start = ((), (), s32[]{:S(2)}) async-start(), calls=%async_computation.6 | async-start | bytes 6291456 | tf_op jit(solution)/shard_map/all_gather | solution.py:113
  9.4 290.2 %all-reduce.2.cloned.1.call-start = ((), (), s32[]{:S(2)}) async-start(), calls=%async_computation.8 | async-start | bytes 4194304 | tf_op jit(solution)/shard_map/psum | solution.py:124
  193.0 0.9 copy-start.10
  193.0 8.1 %copy-start.11 = (bf16[1,2,64,1024]{3,2,1,0:T(8,128)(2,1)S(1)}, bf16[1,2,64,1024]{3,2,1,0:T(8,128)(2,1)}, u32[]{:S(2)}) copy-start(bf16[1,2,64,1024]{3,2,1,0:T(8,128)(2,1)} %param.34) | copy-start | bytes 786436
  193.0 128.6 %all-gather.12.cloned.1.call-start = ((), (), s32[]{:S(2)}) async-start(), calls=%async_computation.9 | async-start | bytes 1572864 | tf_op jit(solution)/shard_map/all_gather | solution.py:115
  195.4 18.3 %all-to-all-start.2 = ((bf16[16,2,4096]{2,1,0:T(2,128)(2,1)}), bf16[16,2,4096]{2,1,0:T(2,128)(2,1)S(1)}, u32[]{:S(2)}, u32[]{:S(2)}) async-start(bf16[16,2,4096]{2,1,0:T(2,128)(2,1)} %reshape.73), calls=%async_computation.2 | async-start | bytes 524288 | tf_op jit(solution)/shard_map/all_to_all | solution.py:134
  213.7 16.3 %all-to-all-start.1 = ((bf16[16,2,4096]{2,1,0:T(2,128)(2,1)}), bf16[16,2,4096]{2,1,0:T(2,128)(2,1)S(1)}, u32[]{:S(2)}, u32[]{:S(2)}) async-start(bf16[16,2,4096]{2,1,0:T(2,128)(2,1)} %reshape.71), calls=%async_computation.1 | async-start | bytes 524288 | tf_op jit(solution)/shard_map/all_to_all | solution.py:133
  230.1 5.4 %copy-start.7 = (bf16[16,2,4096]{2,1,0:T(2,128)(2,1)}, bf16[16,2,4096]{2,1,0:T(2,128)(2,1)S(1)}, u32[]{:S(2)}) copy-start(bf16[16,2,4096]{2,1,0:T(2,128)(2,1)S(1)} %all-to-all-done.1) | copy-start | bytes 786436
  230.1 15.9 %all-to-all-start = ((bf16[16,2,4096]{2,1,0:T(2,128)(2,1)}), bf16[16,2,4096]{2,1,0:T(2,128)(2,1)}, u32[]{:S(2)}, u32[]{:S(2)}) async-start(bf16[16,2,4096]{2,1,0:T(2,128)(2,1)} %reshape.69), calls=%async_computation | async-start | bytes 524288 | tf_op jit(solution)/shard_map/all_to_all | solution.py:132
  234.3 127.7 %all-gather.14.cloned.1.call-start = ((), (), s32[]{:S(2)}) async-start(), calls=%async_computation.10 | async-start | bytes 3932160 | tf_op jit(solution)/shard_map/all_gather | solution.py:116
  248.0 73.5 %copy-start.16 = (f32[4096]{0:T(1024)S(1)}, f32[4096]{0:T(1024)}, u32[]{:S(2)}) copy-start(f32[4096]{0:T(1024)} %param.31) | copy-start | bytes 49156
  301.9 22.9 %copy-start.8 = (bf16[1024,64]{1,0:T(8,128)(2,1)S(1)}, bf16[1024,64]{1,0:T(8,128)(2,1)}, u32[]{:S(2)}) copy-start(bf16[1024,64]{1,0:T(8,128)(2,1)} %get-tuple-element.451) | copy-start | bytes 393220
  301.9 22.9 %copy-start.9 = (bf16[1024,64]{1,0:T(8,128)(2,1)S(1)}, bf16[1024,64]{1,0:T(8,128)(2,1)}, u32[]{:S(2)}) copy-start(bf16[1024,64]{1,0:T(8,128)(2,1)} %get-tuple-element.452) | copy-start | bytes 393220
  333.6 1.3 copy-start.3
  338.7 19.2 %copy-start.1 = (bf16[1280,64]{1,0:T(8,128)(2,1)}, bf16[1280,64]{1,0:T(8,128)(2,1)S(1)}, u32[]{:S(2)}) copy-start(bf16[1280,64]{1,0:T(8,128)(2,1)S(1)} %get-tuple-element.807) | copy-start | bytes 491524
  338.7 19.2 %copy-start.5 = (bf16[2,512,64]{1,2,0:T(8,128)(2,1)}, bf16[2,512,64]{1,2,0:T(8,128)(2,1)S(1)}, u32[]{:S(2)}) copy-start(bf16[2,512,64]{1,2,0:T(8,128)(2,1)S(1)} %get-tuple-element.734) | copy-start | bytes 393220
  338.7 8.1 %copy-start.14 = (f32[1,2]{1,0:T(1,128)S(1)}, f32[1,2]{1,0:T(1,128)}, u32[]{:S(2)}) copy-start(f32[1,2]{1,0:T(1,128)} %param.26) | copy-start | bytes 28
  340.5 15.6 %all-to-all-start.3 = ((bf16[16,2,4096]{2,1,0:T(2,128)(2,1)}), bf16[16,2,4096]{2,1,0:T(2,128)(2,1)S(1)}, u32[]{:S(2)}, u32[]{:S(2)}) async-start(bf16[16,2,4096]{2,1,0:T(2,128)(2,1)} %reshape.75), calls=%async_computation.3 | async-start | bytes 524288 | tf_op jit(solution)/shard_map/all_to_all | solution.py:148
  362.0 39.7 %copy-start = (bf16[1024,1280]{1,0:T(8,128)(2,1)S(1)}, bf16[1024,1280]{1,0:T(8,128)(2,1)}, u32[]{:S(2)}) copy-start(bf16[1024,1280]{1,0:T(8,128)(2,1)} %all-gather.14.cloned.1.call-done) | copy-start | bytes 7864324
  406.8 13.5 %all-to-all-start.4 = ((bf16[16,2,4096]{2,1,0:T(2,128)(2,1)}), bf16[16,2,4096]{2,1,0:T(2,128)(2,1)S(1)}, u32[]{:S(2)}, u32[]{:S(2)}) async-start(bf16[16,2,4096]{2,1,0:T(2,128)(2,1)} %reshape.77), calls=%async_computation.4 | async-start | bytes 524288 | tf_op jit(solution)/shard_map/all_to_all | solution.py:164
  451.5 0.9 copy-start.6
  451.5 2.1 copy-start.2
  455.1 2.2 copy-start.12
  458.6 0.7 copy-start.13
  460.5 0.9 copy-start.6
  460.5 2.1 copy-start.2
  464.1 3.2 copy-start.12
  468.5 0.7 copy-start.13
Sparse Core Ops, SparseCore 0:
  9.5 59.4 all-gather.5
  70.5 56.7 all-gather.9
  128.9 56.7 all-gather.7
  193.1 106.4 all-reduce.1
  301.0 20.5 all-gather.11
  323.0 38.9 all-gather.13
where the time goes:
time: 487 us; the launch traced here: 485 us
  waiting for transfers between devices  294 us (60%)
  matrix products  57.2 us (12%)
  local copies, waits for them, and re-layouts  36 us (7%)
  blocking collectives  33 us (7%)
  starting transfers between devices  23.1 us (5%)
  other arithmetic  22.4 us (5%)
  between operations  19.8 us (4%)
    all_gather x1, waiting for transfers between devices, on_device(): lax.all_gather(w_in_gate, 'fsdp', axis=0, tiled=True)  59 us
    all_gather x1, waiting for transfers between devices, on_device(): lax.all_gather(w_in_up, 'fsdp', axis=0, tiled=True)  58.3 us
    all_gather x1, waiting for transfers between devices, on_device(): lax.all_gather(w_in_down, 'fsdp', axis=1, tiled=True)  54.7 us
    psum x1, waiting for transfers between devices, on_device(): lax.psum(partial_value.astype(jnp.bfloat16), 'seq').astype(jnp.float32)  50.5 us
    psum x1, blocking collectives, on_device(): error_sums = lax.psum(partial_err, 'seq')  33 us
    all_gather x1, waiting for transfers between devices, on_device(): lax.all_gather(w_context, 'fsdp', axis=0, tiled=True)  19.6 us
    unnamed x43, local copies, waits for them, and re-layouts  16 us
    all_to_all x1, waiting for transfers between devices, on_device(): lax.all_to_all(image_v, 'seq', split_axis=3, concat_axis=2, tiled=True)  11.2 us
  transfers between devices with their start and end apart: 11, of which 11 were waited for; matrix products, arithmetic and copies ran while one was open for 9% of the time, Pallas kernels for 0%

commit v1 on v0

v1 whole, which is shorter than its diff:
```python
import math

import jax
import jax.numpy as jnp
from jax import lax
from jax.experimental import pallas as pl
from jax.experimental.pallas import tpu as pltpu
from jax.sharding import PartitionSpec as P

HEAD = 64
LANES = 128
f32 = jnp.float32
bf16 = jnp.bfloat16

dpo_beta = 20.0
norm_eps = 1e-06
inv_root = 1.0 / math.sqrt(HEAD)


def noise_level(step_index):
    fraction = (step_index.astype(f32) + 1.0) / 1000.0
    return 3.0 * fraction / (1.0 + 2.0 * fraction)


def dot(a, b):
    return jnp.dot(a, b, preferred_element_type=f32)


def dot_nt(a, b):
    return lax.dot_general(a, b, (((1,), (1,)), ((), ())), preferred_element_type=f32)


def dot_tn(a, b):
    return lax.dot_general(a, b, (((0,), (0,)), ((), ())), preferred_element_type=f32)


def swap(x, axis, size, mask):
    return lax.ppermute(x, axis, [(i, i ^ mask) for i in range(size)])


def vmem():
    return pl.BlockSpec(memory_space=pltpu.VMEM)


def smem():
    return pl.BlockSpec(memory_space=pltpu.SMEM)


params = pltpu.CompilerParams(vmem_limit_bytes=48 * 1024 * 1024)


def pack_kernel(q_ref, k_ref, v_ref, out_ref):
    tok = q_ref.shape[1]
    for n, ref in enumerate((q_ref, k_ref, v_ref)):
        for pair in range(ref.shape[2] // LANES):
            a = ref[0, :, pair * LANES : (pair + 1) * LANES]
            b = ref[1, :, pair * LANES : (pair + 1) * LANES]
            rows = slice(n * tok, (n + 1) * tok)
            out_ref[2 * pair, rows, :] = jnp.concatenate([a[:, :HEAD], b[:, :HEAD]], axis=1)
            out_ref[2 * pair + 1, rows, :] = jnp.concatenate([a[:, HEAD:], b[:, HEAD:]], axis=1)


def pack_heads(q, k, v):
    tok, inner = q.shape[1], q.shape[2]
    return pl.pallas_call(
        pack_kernel,
        out_shape=jax.ShapeDtypeStruct((inner // HEAD, 3 * tok, LANES), bf16),
        in_specs=[vmem()] * 3,
        out_specs=vmem(),
        compiler_params=params,
        name="pack_heads",
    )(q, k, v)


def down_kernel(idx_ref, hid_ref, w_ref, out_ref):
    hidden = hid_ref[...]
    for p in range(out_ref.shape[0]):
        start = pl.multiple_of(idx_ref[p] * LANES, LANES)
        out_ref[p] = dot(hidden, w_ref[:, pl.ds(start, LANES)]).astype(bf16)


def down_product(idx, hidden, w_down):
    blocks = w_down.shape[1] // LANES
    return pl.pallas_call(
        down_kernel,
        out_shape=jax.ShapeDtypeStruct((blocks, hidden.shape[0], LANES), bf16),
        in_specs=[smem(), vmem(), vmem()],
        out_specs=vmem(),
        compiler_params=params,
        name="down_product",
    )(idx, hidden, w_down)


def context_kernel(idx_ref, y_ref, pp_ref, gain_ref, w_ref, ctx_ref, sq_ref):
    blocks, rows = y_ref.shape[0], y_ref.shape[1]
    acc = jnp.zeros((rows, w_ref.shape[1]), f32)
    sq = jnp.zeros((rows, LANES), f32)
    for p in range(blocks):
        start = pl.multiple_of(idx_ref[p] * LANES, LANES)
        state = y_ref[p].astype(f32) + pp_ref[:, pl.ds(start, LANES)].astype(f32)
        sq = sq + state * state
        scaled = (state * gain_ref[:, pl.ds(start, LANES)]).astype(bf16)
        acc = acc + dot(scaled, w_ref[pl.ds(start, LANES), :])
    ctx_ref[...] = acc.astype(bf16)
    sq_ref[...] = jnp.sum(sq.T, axis=0, keepdims=True)


def context_product(idx, y, packed_prompt, gain, w_context):
    rows = y.shape[1]
    return pl.pallas_call(
        context_kernel,
        out_shape=(
            jax.ShapeDtypeStruct((rows, w_context.shape[1]), bf16),
            jax.ShapeDtypeStruct((1, rows), f32),
        ),
        in_specs=[smem(), vmem(), vmem(), vmem(), vmem()],
        out_specs=(vmem(), vmem()),
        compiler_params=params,
        name="context_product",
    )(idx, y, packed_prompt, gain, w_context)


def bit_reversed(size):
    bits = size.bit_length() - 1
    return [int(format(p, "b").zfill(bits)[::-1], 2) if bits else 0 for p in range(size)]


def seq_sum(x, size):
    masks = [1 << b for b in range(size.bit_length() - 1)]
    for mask in masks:
        half = x.shape[0] // 2
        got = swap(x[half:], "seq", size, mask)
        x = (x[:half].astype(f32) + got.astype(f32)).astype(bf16)
    for mask in reversed(masks):
        x = jnp.concatenate([x, swap(x, "seq", size, mask)], axis=0)
    return x


def encode_shared(
    S, prompt, lengths, gain_ffn, w_gate, w_up, w_down, gain_final, w_context
):
    s = lax.axis_index("seq")
    f = lax.axis_index("fsdp")
    own = prompt[0]
    rows, width = own.shape
    cols = width // 2
    half = rows // 2
    core = s & 1

    away = lax.dynamic_slice(own, (core * half, (1 - f) * cols), (half, cols))
    got_a = swap(away, "fsdp", 2, 1)
    other_len = swap(lengths, "fsdp", 2, 1)[0]
    own_f32 = own.astype(f32)
    scale = lax.rsqrt(jnp.mean(own_f32 * own_f32, axis=-1) + norm_eps)
    other_scale = swap(scale.reshape(-1, LANES), "fsdp", 2, 1).reshape(-1)
    got_b = swap(got_a, "seq", S, 1)
    gain = lax.dynamic_slice(gain_ffn, (f * cols,), (cols,))

    here = lax.dynamic_slice(own, (0, f * cols), (rows, cols))
    first = core * half
    scale_a = lax.dynamic_slice(other_scale, (first,), (half,))
    scale_b = lax.dynamic_slice(other_scale, (half - first,), (half,))

    def partial_of(raw, row_scale):
        normed = (raw.astype(f32) * row_scale[:, None] * gain[None, :]).astype(bf16)
        return jnp.concatenate(
            [dot(normed, w_gate).astype(bf16), dot(normed, w_up).astype(bf16)], axis=1
        )

    own_len = lengths[0]
    own_start = jnp.where(f == 0, 0, other_len)
    other_start = jnp.where(f == 0, own_len, 0)
    row = jnp.arange(half, dtype=jnp.int32)
    source = jnp.concatenate([row, row + half, row + first, row + half - first])
    is_own = jnp.arange(2 * rows) < rows
    place = source + jnp.where(is_own, own_start, other_start)
    place = jnp.where(source < jnp.where(is_own, own_len, other_len), place, -1)
    total = rows * 3 // 2
    select = (jnp.arange(total)[:, None] == place[None, :]).astype(bf16)

    parts = jnp.concatenate(
        [partial_of(here, scale), partial_of(got_a, scale_a), partial_of(got_b, scale_b)], axis=0
    )
    packed = dot(select, parts).astype(bf16)
    both = packed.astype(f32) + swap(packed, "fsdp", 2, 1).astype(f32)
    units = w_gate.shape[1]
    hidden = (jax.nn.gelu(both[:, :units], approximate=True) * both[:, units:]).astype(bf16)

    packed_prompt = dot(select, jnp.concatenate([here, got_a, got_b], axis=0)).astype(bf16)
    idx = jnp.array(bit_reversed(S), jnp.int32) ^ s
    y = down_product(idx, hidden, w_down)
    y = seq_sum(y, S)
    gain_here = lax.dynamic_slice(gain_final, (f * cols,), (cols,))[None]
    ctx, sq = context_product(idx, y, packed_prompt, gain_here, w_context)
    ctx_other = swap(ctx, "fsdp", 2, 1)
    sq_other = swap(sq, "fsdp", 2, 1)
    inv = lax.rsqrt((sq + sq_other)[0] / width + norm_eps)
    ctx = ((ctx.astype(f32) + ctx_other.astype(f32)) * inv[:, None]).astype(bf16)
    return dot_tn(select[:, :rows], ctx).astype(bf16)


def rms_gain(values, gain):
    mean_sq = jnp.mean(values * values, axis=-1, keepdims=True)
    return values * lax.rsqrt(mean_sq + norm_eps) * gain


def encode_gathered(prompt, gain_ffn, w_gate, w_up, w_down, gain_final, w_context):
    gate_full = lax.all_gather(w_gate, "fsdp", axis=0, tiled=True)
    up_full = lax.all_gather(w_up, "fsdp", axis=0, tiled=True)
    down_full = lax.all_gather(w_down, "fsdp", axis=1, tiled=True)
    context_full = lax.all_gather(w_context, "fsdp", axis=0, tiled=True)
    prompt_f32 = prompt[0].astype(f32)
    normed = rms_gain(prompt_f32, gain_ffn).astype(bf16)
    hidden = (
        jax.nn.gelu(dot(normed, gate_full), approximate=True) * dot(normed, up_full)
    ).astype(bf16)
    summed = lax.psum(dot(hidden, down_full).astype(bf16), "seq").astype(f32)
    encoded = rms_gain(prompt_f32 + summed, gain_final).astype(bf16)
    return dot(encoded, context_full).astype(bf16)


def lanes_of(stream):
    return slice(stream * HEAD, (stream + 1) * HEAD)


def rows_of(ref):
    value = ref[...]
    return value.reshape(-1, LANES)


def image_kernel(q_ref, k_ref, v_ref, e_ref, o_ref, m_ref, l_ref):
    q, k, v = rows_of(q_ref), rows_of(k_ref), rows_of(v_ref)
    rows = q.shape[0]
    outs, tops, sums = [], [], []
    for stream in range(2):
        at = lanes_of(stream)
        scores = dot_nt(q[:, at] * jnp.asarray(inv_root, bf16), k[:, at])
        top = jnp.max(scores, axis=-1, keepdims=True)
        e = jnp.exp(scores - top)
        eb = e.astype(bf16)
        e_ref[stream] = eb
        outs.append(dot(eb, v[:, at]))
        tops.append(jnp.broadcast_to(top, (rows, HEAD)))
        sums.append(jnp.broadcast_to(jnp.sum(e, axis=-1, keepdims=True), (rows, HEAD)))
    o_ref[...] = jnp.concatenate(outs, axis=1)
    m_ref[...] = jnp.concatenate(tops, axis=1)
    l_ref[...] = jnp.concatenate(sums, axis=1)


def q_blocks(S, tok):
    rows = min(256, S * tok)
    return rows // tok, S * tok // rows, rows


def image_part(qkv):
    S, _, tok, _ = qkv.shape
    group, steps, rows = q_blocks(S, tok)
    seq_len = S * tok
    whole = lambda n: pl.BlockSpec((S, None, tok, LANES), lambda i: (0, n, 0, 0))
    flat = pl.BlockSpec((rows, LANES), lambda i: (i, 0))
    return pl.pallas_call(
        image_kernel,
        grid=(steps,),
        out_shape=(jax.ShapeDtypeStruct((2, seq_len, seq_len), bf16),)
        + (jax.ShapeDtypeStruct((seq_len, LANES), f32),) * 3,
        in_specs=[
            pl.BlockSpec((group, None, tok, LANES), lambda i: (i, 0, 0, 0)),
            whole(1),
            whole(2),
        ],
        out_specs=(pl.BlockSpec((2, rows, seq_len), lambda i: (0, i, 0)), flat, flat, flat),
        compiler_params=params,
        name="image_part",
    )(qkv, qkv, qkv)


def text_kernel(len_ref, q_ref, ctx_ref, o_ref, m_ref, l_ref, out_ref, p_ref, c_ref):
    q = rows_of(q_ref)
    ctx = ctx_ref[...]
    keys, values = ctx[:, :HEAD], ctx[:, HEAD:]
    keep = lax.broadcasted_iota(jnp.int32, (q.shape[0], ctx.shape[0]), 1) < len_ref[0]
    outs, scales = [], []
    for stream in range(2):
        at = lanes_of(stream)
        scores = dot_nt(q[:, at] * jnp.asarray(inv_root, bf16), keys)
        scores = jnp.where(keep, scores, -jnp.inf)
        top_image = m_ref[:, stream * HEAD : stream * HEAD + 1]
        top = jnp.maximum(top_image, jnp.max(scores, axis=-1, keepdims=True))
        e = jnp.exp(scores - top)
        shrink = jnp.exp(top_image - top)
        total = l_ref[:, stream * HEAD : stream * HEAD + 1] * shrink + jnp.sum(
            e, axis=-1, keepdims=True
        )
        inv = 1.0 / total
        probs = (e * inv).astype(bf16)
        p_ref[stream] = probs
        scale = shrink * inv
        outs.append(o_ref[:, at] * scale + dot(probs, values))
        scales.append(jnp.broadcast_to(scale, (q.shape[0], HEAD)))
    out = jnp.concatenate(outs, axis=1).astype(bf16)
    out_ref[...] = out.reshape(out_ref.shape)
    c_ref[...] = jnp.concatenate(scales, axis=1)


def text_part(lengths, qkv, ctx, o_img, m_img, l_img):
    S, _, tok, _ = qkv.shape
    group, steps, rows = q_blocks(S, tok)
    seq_len = S * tok
    text = ctx.shape[0]
    flat = pl.BlockSpec((rows, LANES), lambda i: (i, 0))
    return pl.pallas_call(
        text_kernel,
        grid=(steps,),
        out_shape=(
            jax.ShapeDtypeStruct((S, tok, LANES), bf16),
            jax.ShapeDtypeStruct((2, seq_len, text), bf16),
            jax.ShapeDtypeStruct((seq_len, LANES), f32),
        ),
        in_specs=[
            smem(),
            pl.BlockSpec((group, None, tok, LANES), lambda i: (i, 0, 0, 0)),
            pl.BlockSpec((text, LANES), lambda i: (0, 0)),
            flat,
            flat,
            flat,
        ],
        out_specs=(
            pl.BlockSpec((group, tok, LANES), lambda i: (i, 0, 0)),
            pl.BlockSpec((2, rows, text), lambda i: (0, i, 0)),
            flat,
        ),
        compiler_params=params,
        name="text_part",
    )(lengths, qkv, ctx, o_img, m_img, l_img)


def project_kernel(idx_ref, o_ref, target_ref, *refs):
    counts = len(refs) - 3
    w_refs, out_ref, err_ref, a_ref = refs[:counts], refs[-3], refs[-2], refs[-1]
    heads, tok = o_ref.shape[0], o_ref.shape[1]
    blocks, _, block_rows = a_ref.shape
    pairs = block_rows // LANES
    for pair in range(heads // 2):
        a, b = o_ref[2 * pair], o_ref[2 * pair + 1]
        at = slice((pair % pairs) * LANES, (pair % pairs + 1) * LANES)
        a_ref[pair // pairs, :tok, at] = jnp.concatenate([a[:, :HEAD], b[:, :HEAD]], axis=1)
        a_ref[pair // pairs, tok:, at] = jnp.concatenate([a[:, HEAD:], b[:, HEAD:]], axis=1)
    slots = []
    for ref in w_refs:
        for n in range(ref.shape[0] // block_rows):
            slots.append((ref, n * block_rows))
    pred = None
    for slot, (ref, start) in enumerate(slots):
        term = dot(a_ref[idx_ref[slot]], ref[start : start + block_rows, :])
        pred = term if pred is None else pred + term
    target = target_ref[...].reshape(2 * tok, -1).astype(f32)
    residual = pred - target
    squares = residual * residual
    for stream in range(2):
        part = squares[stream * tok : (stream + 1) * tok]
        total = jnp.sum(jnp.sum(part, axis=0, keepdims=True), axis=1, keepdims=True)
        err_ref[stream : stream + 1, :] = jnp.broadcast_to(total, (1, LANES))
    grad = residual.astype(bf16)
    for slot, (ref, start) in enumerate(slots):
        g = dot_nt(grad, ref[start : start + block_rows, :]).astype(bf16)
        head = idx_ref[slot] * (2 * pairs)
        for pair in range(pairs):
            a = g[:tok, pair * LANES : (pair + 1) * LANES]
            b = g[tok:, pair * LANES : (pair + 1) * LANES]
            out_ref[head + 2 * pair] = jnp.concatenate([a[:, :HEAD], b[:, :HEAD]], axis=1)
            out_ref[head + 2 * pair + 1] = jnp.concatenate([a[:, HEAD:], b[:, HEAD:]], axis=1)


def project(idx, attended, target, weights):
    S, tok, _ = attended.shape
    blocks = idx.shape[0]
    block_rows = sum(w.shape[0] for w in weights) // blocks
    return pl.pallas_call(
        project_kernel,
        out_shape=(
            jax.ShapeDtypeStruct((S, tok, LANES), bf16),
            jax.ShapeDtypeStruct((2, LANES), f32),
        ),
        in_specs=[smem()] + [vmem()] * (2 + len(weights)),
        out_specs=(vmem(), vmem()),
        scratch_shapes=[pltpu.VMEM((blocks, 2 * tok, block_rows), bf16)],
        compiler_params=params,
        name="project",
    )(idx, attended, target, *weights)


def backward_kernel(
    coef_ref, q_ref, k_ref, v_ref, ctx_ref, e_ref, p_ref, c_ref, o_ref, g_ref,
    dq_ref, dk_ref, dv_ref, ka_ref, va_ref,
):
    step = pl.program_id(0)
    q, k, v = rows_of(q_ref), rows_of(k_ref), rows_of(v_ref)
    o, g = rows_of(o_ref), rows_of(g_ref)
    ctx = ctx_ref[...]
    keys, values = ctx[:, :HEAD], ctx[:, HEAD:]
    products = g.astype(f32) * o.astype(f32)

    @pl.when(step == 0)
    def _():
        ka_ref[...] = jnp.zeros_like(ka_ref)
        va_ref[...] = jnp.zeros_like(va_ref)

    for stream in range(2):
        at = lanes_of(stream)
        gs = g[:, at]
        delta = jnp.sum(products[:, at], axis=-1, keepdims=True)
        scale = c_ref[:, stream * HEAD : stream * HEAD + 1]
        e = e_ref[stream]
        probs = p_ref[stream]
        grad_image = dot_nt(gs, v[:, at])
        grad_text = dot_nt(gs, values)
        ds_image = (e.astype(f32) * ((grad_image - delta) * scale)).astype(bf16)
        ds_text = (probs.astype(f32) * (grad_text - delta)).astype(bf16)
        coef = coef_ref[stream]
        dq = dot(ds_image, k[:, at]) + dot(ds_text, keys)
        dq_ref[stream] = (dq * (coef * inv_root)).astype(bf16)
        ka_ref[stream] += dot_tn(ds_image, q[:, at])
        va_ref[stream] += dot_tn(e, (gs.astype(f32) * scale).astype(bf16))

    @pl.when(step == pl.num_programs(0) - 1)
    def _():
        for stream in range(2):
            coef = coef_ref[stream]
            dk_ref[stream] = (ka_ref[stream] * (coef * inv_root)).astype(bf16)
            dv_ref[stream] = (va_ref[stream] * coef).astype(bf16)


def backward_part(coef, qkv, ctx, e, probs, scale, attended, grads):
    S, _, tok, _ = qkv.shape
    group, steps, rows = q_blocks(S, tok)
    seq_len = S * tok
    text = ctx.shape[0]
    whole = lambda n: pl.BlockSpec((S, None, tok, LANES), lambda i: (0, n, 0, 0))
    block = pl.BlockSpec((group, tok, LANES), lambda i: (i, 0, 0))
    full = pl.BlockSpec((None, 2, seq_len, HEAD), lambda i: (0, 0, 0, 0))
    out = jax.ShapeDtypeStruct((1, 2, seq_len, HEAD), bf16)
    return pl.pallas_call(
        backward_kernel,
        grid=(steps,),
        out_shape=(out, out, out),
        in_specs=[
            smem(),
            pl.BlockSpec((group, None, tok, LANES), lambda i: (i, 0, 0, 0)),
            whole(1),
            whole(2),
            pl.BlockSpec((text, LANES), lambda i: (0, 0)),
            pl.BlockSpec((2, rows, seq_len), lambda i: (0, i, 0)),
            pl.BlockSpec((2, rows, text), lambda i: (0, i, 0)),
            pl.BlockSpec((rows, LANES), lambda i: (i, 0)),
            block,
            block,
        ],
        out_specs=(pl.BlockSpec((None, 2, rows, HEAD), lambda i: (0, 0, i, 0)), full, full),
        scratch_shapes=[pltpu.VMEM((2, seq_len, HEAD), f32)] * 2,
        compiler_params=params,
        name="backward_part",
    )(coef, qkv, qkv, qkv, ctx, e, probs, scale, attended, grads)


def exchange(x):
    return lax.all_to_all(x, "seq", split_axis=0, concat_axis=0, tiled=True)


def on_device(
    S, F, prompt, lengths, timesteps, ref_errors, gain_ffn, w_in_gate, w_in_up, w_in_down,
    gain_final, w_context, image_q, image_k, image_v, w_out, target,
):
    s = lax.axis_index("seq")
    f = lax.axis_index("fsdp")
    tok = image_q.shape[2]
    seq_len = S * tok
    qkv = exchange(pack_heads(image_q[0], image_k[0], image_v[0])).reshape(S, 3, tok, LANES)

    if F == 2 and w_in_down.shape[1] == S * LANES:
        ctx = encode_shared(
            S, prompt, lengths, gain_ffn, w_in_gate, w_in_up, w_in_down, gain_final, w_context
        )
    else:
        ctx = encode_gathered(
            prompt, gain_ffn, w_in_gate, w_in_up, w_in_down, gain_final, w_context
        )

    if F == 2:
        half = w_out.shape[0] // 2
        core = s & 1
        away = lax.dynamic_slice(w_out, (core * half, 0), (half, w_out.shape[1]))
        w_a = swap(away, "fsdp", 2, 1)
        w_b = swap(w_a, "seq", S, 1)
        weights = (w_out, w_a, w_b)
        there = 2 * (1 - f)
        w_idx = jnp.stack([2 * f, 2 * f + 1, there + core, there + 1 - core]).astype(jnp.int32)
    else:
        weights = (lax.all_gather(w_out, "fsdp", axis=0, tiled=True),)
        w_idx = jnp.arange(F, dtype=jnp.int32)

    e_img, o_img, m_img, l_img = image_part(qkv)
    attended, probs, scale = text_part(lengths, qkv, ctx, o_img, m_img, l_img)
    tokens = exchange(attended)
    grad_tok, partial_err = project(w_idx, tokens, target[0], weights)
    grads = exchange(grad_tok)
    error_sums = partial_err
    mask = 1
    while mask < S:
        error_sums = error_sums + swap(error_sums, "seq", S, mask)
        mask *= 2
    mean_errors = error_sums[:, 0] / (seq_len * target.shape[-1])
    error_gap = mean_errors[0] - ref_errors[0, 0] - (mean_errors[1] - ref_errors[0, 1])
    sigma_t = noise_level(timesteps[0])
    logit_value = dpo_beta * sigma_t * error_gap
    pair_loss = jax.nn.softplus(logit_value)[None]
    coefficient = sigma_t * jax.nn.sigmoid(logit_value)
    coef = jnp.stack([coefficient, -coefficient])
    grad_q, grad_k, grad_v = backward_part(
        coef, qkv, ctx, e_img, probs, scale, attended, grads
    )
    return pair_loss, grad_q, grad_k, grad_v


def solution(mesh):
    S, F = mesh.shape["seq"], mesh.shape["fsdp"]

    def body(*args):
        return on_device(S, F, *args)

    return jax.shard_map(
        body,
        mesh=mesh,
        in_specs=(
            P("fsdp", None, None),
            P("fsdp"),
            P("fsdp"),
            P("fsdp", None),
            P(),
            P("fsdp", "seq"),
            P("fsdp", "seq"),
            P("seq", "fsdp"),
            P(),
            P("fsdp", "seq"),
            P("fsdp", None, "seq", None),
            P("fsdp", None, "seq", None),
            P("fsdp", None, "seq", None),
            P("fsdp", None),
            P("fsdp", None, "seq", None),
        ),
        out_specs=(
            P("fsdp"),
            P("fsdp", None, None, "seq"),
            P("fsdp", None, None, "seq"),
            P("fsdp", None, None, "seq"),
        ),
        check_vma=False,
    )
```

time: 487 us -> 205 us (0.42)
  waiting for transfers between devices: 294 us -> 85.5 us
  matrix products: 57.2 us -> 10 us
  blocking collectives: 33 us -> 0 us
  Pallas kernels: 0 us -> 29.2 us
  starting transfers between devices: 23.1 us -> 40.4 us
  other arithmetic: 22.4 us -> 7.6 us
  between operations: 19.8 us -> 6.99 us
  local copies, waits for them, and re-layouts: 36 us -> 23.6 us
    all_gather x5 -> x0, waiting for transfers between devices: 196 us -> none  [the longest x1 59 us: on_device(): lax.all_gather(w_in_gate, 'fsdp', axis=0, tiled=True)]
    ppermute x0 -> x21, waiting for transfers between devices: none -> 75.6 us  [swap(): return lax.ppermute(x, axis, [(i, i ^ mask) for i in range(size)])]
    psum x1 -> x0, waiting for transfers between devices: 50.5 us -> none  [on_device(): lax.psum(partial_value.astype(jnp.bfloat16), 'seq').astype(jnp.float32)]
    dot_general x33 -> x9, matrix products: 57.2 us -> 10 us  [the longest x8 9.65 us: dot(): return jnp.dot(a, b, preferred_element_type=f32)]
    all_to_all x5 -> x3, waiting for transfers between devices: 44.5 us -> 9.93 us  [exchange(): return lax.all_to_all(x, 'seq', split_axis=0, concat_axis=0, tiled=True)]
    psum x1 -> x0, blocking collectives: 33 us -> none  [on_device(): error_sums = lax.psum(partial_err, 'seq')]
    pallas_call x0 -> x7, Pallas kernels: none -> 29.2 us  [the longest x1 9.52 us: backward_part(): pl.pallas_call(backward_kernel, grid=(steps,), out_shape=(out, out, out),...]
    ppermute x0 -> x21, starting transfers between devices: none -> 24.3 us  [swap(): return lax.ppermute(x, axis, [(i, i ^ mask) for i in range(size)])]
  transfers between devices with their start and end apart: 11 -> 24, of which waited for: 11 -> 14; matrix products, arithmetic and copies ran while one was open for 9% -> 9% of each run, Pallas kernels for 0% -> 7%
where the time goes in v1:
time: 205 us; the launch traced here: 203 us
  waiting for transfers between devices  85.5 us (42%)
  starting transfers between devices  40.4 us (20%)
  Pallas kernels  29.2 us (14%)
  local copies, waits for them, and re-layouts  23.6 us (12%)
  matrix products  10 us (5%)
  other arithmetic  7.6 us (4%)
  between operations  6.99 us (3%)
    ppermute x21, waiting for transfers between devices, swap(): return lax.ppermute(x, axis, [(i, i ^ mask) for i in range(size)])  75.6 us
    ppermute x21, starting transfers between devices, swap(): return lax.ppermute(x, axis, [(i, i ^ mask) for i in range(size)])  24.3 us
    unnamed x68, local copies, waits for them, and re-layouts  17.8 us
    all_to_all x3, starting transfers between devices, exchange(): return lax.all_to_all(x, 'seq', split_axis=0, concat_axis=0, tiled=True)  16.1 us
    all_to_all x3, waiting for transfers between devices, exchange(): return lax.all_to_all(x, 'seq', split_axis=0, concat_axis=0, tiled=True)  9.93 us
    dot_general x8, matrix products, dot(): return jnp.dot(a, b, preferred_element_type=f32)  9.65 us
    pallas_call x1, Pallas kernels, backward_part(): pl.pallas_call(backward_kernel, grid=(steps,), out_shape=(out, out, out),...  9.52 us
    pallas_call x1, Pallas kernels, text_part(): pl.pallas_call(text_kernel, grid=(steps,), out_shape=(jax.ShapeDtypeStruc...  6.62 us
  transfers between devices with their start and end apart: 24, of which 14 were waited for; matrix products, arithmetic and copies ran while one was open for 9% of the time, Pallas kernels for 7%

profile of v1, /device:TPU:0, one launch (start us, length us, event | category | flops | bytes accessed | tf_op | source)
XLA Modules:
  0.0 203.4 jit_solution(18249268248184331097)
XLA Ops:
  0.6 2.2 %multiply_reduce_fusion = f32[256]{0:T(256)S(1)} fusion(bf16[1,256,4096]{2,1,0:T(8,128)(2,1)} %param.16), kind=kLoop, calls=%fused_computation | loop fusion | flops 3145472 | bytes 2098176 | tf_op jit(solution)/shard_map/reduce_sum | solution.py:154
  2.9 3.1 %collective-permute-start.2 = (f32[2,128]{1,0:T(2,128)S(1)}, f32[2,128]{1,0:T(2,128)S(1)}, u32[]{:S(2)}, u32[]{:S(2)}) collective-permute-start(f32[2,128]{1,0:T(2,128)S(1)} %get-tuple-element.41), channel_id=1, source_target_pairs={{0,1},{1,0},{2,3},{3,2},{4,5},{5,4},{6,7},{7,6},{8,9},{9,8},{10,11... | collective-permute-start | bytes 3080 | tf_op jit(solution)/shard_map/ppermute | solution.py:38
  6.0 1.9 dynamic-slice_bitcast_fusion.1
  7.9 2.0 collective-permute-start
  10.6 1.3 dynamic-slice_bitcast_fusion
  12.0 1.5 convolution_convert_fusion.2
  14.0 1.5 convolution_convert_fusion.3
  15.4 6.2 %collective-permute-done = s32[1]{0:T(128)} collective-permute-done((s32[1]{0:T(128)}, s32[1]{0:T(128)}, u32[]{:S(2)}, u32[]{:S(2)}) %collective-permute-start) | collective-permute-done | bytes 36 | tf_op jit(solution)/shard_map/ppermute | solution.py:38
  22.3 0.8 add_select_fusion
  23.2 1.5 convolution_convert_fusion.6
  24.7 1.5 convolution_convert_fusion.7
  29.1 19.6 %collective-permute-done.4 = bf16[384,1024]{1,0:T(8,128)(2,1)S(1)} collective-permute-done((bf16[384,1024]{1,0:T(8,128)(2,1)S(1)}, bf16[384,1024]{1,0:T(8,128)(2,1)S(1)}, u32[]{:S(2)}, u32[]{:S(2)}) %collective-permute-start.4) | collective-permute-done | bytes 786464 | tf_op jit(solution)/shard_map/ppermute | solution.py:38
  49.3 2.4 %down_product.1 = bf16[16,384,128]{2,1,0:T(8,128)(2,1)S(1)} custom-call(s32[16]{0:T(128)S(1)} %broadcast_xor_fusion.idx_ref, bf16[384,512]{1,0:T(8,128)(2,1)S(1)} %fusion.24.hid_ref, bf16[512,2048]{1,0:T(8,128)(2,1)S(1)} %copy-done.3), custom_call_target="tpu_custom_call" | custom-call | tf_op jit(solution)/shard_map/down_product/pallas_call | solution.py:84
  51.8 2.3 %collective-permute-done.5 = bf16[8,384,128]{2,1,0:T(8,128)(2,1)S(1)} collective-permute-done((bf16[8,384,128]{2,1,0:T(8,128)(2,1)S(1)}, bf16[8,384,128]{2,1,0:T(8,128)(2,1)S(1)}, u32[]{:S(2)}, u32[]{:S(2)}) %collective-permute-start.5) | collective-permute-done | bytes 786464 | tf_op jit(solution)/shard_map/ppermute | solution.py:38
  54.4 1.5 collective-permute-start.6
  55.9 9.7 %collective-permute-done.6 = bf16[4,384,128]{2,1,0:T(8,128)(2,1)S(1)} collective-permute-done((bf16[4,384,128]{2,1,0:T(8,128)(2,1)S(1)}, bf16[4,384,128]{2,1,0:T(8,128)(2,1)S(1)}, u32[]{:S(2)}, u32[]{:S(2)}) %collective-permute-start.6) | collective-permute-done | bytes 393248 | tf_op jit(solution)/shard_map/ppermute | solution.py:38
  65.7 1.6 collective-permute-start.7
  67.4 4.5 %collective-permute-done.7 = bf16[2,384,128]{2,1,0:T(8,128)(2,1)S(1)} collective-permute-done((bf16[2,384,128]{2,1,0:T(8,128)(2,1)S(1)}, bf16[2,384,128]{2,1,0:T(8,128)(2,1)S(1)}, u32[]{:S(2)}, u32[]{:S(2)}) %collective-permute-start.7) | collective-permute-done | bytes 196640 | tf_op jit(solution)/shard_map/ppermute | solution.py:38
  72.0 2.7 %collective-permute-start.8 = (bf16[1,384,128]{2,1,0:T(8,128)(2,1)S(1)}, bf16[1,384,128]{2,1,0:T(8,128)(2,1)S(1)}, u32[]{:S(2)}, u32[]{:S(2)}) collective-permute-start(bf16[1,384,128]{2,1,0:T(8,128)(2,1)S(1)} %slice.76), channel_id=1, source_target_pairs={{0,16},{2,18},{4,20},{6,22},{8,24},{10,26},{12,28},{14,30},{16,0},... | collective-permute-start | bytes 294920 | tf_op jit(solution)/shard_map/ppermute | solution.py:38
  74.6 2.9 %collective-permute-done.8 = bf16[1,384,128]{2,1,0:T(8,128)(2,1)S(1)} collective-permute-done((bf16[1,384,128]{2,1,0:T(8,128)(2,1)S(1)}, bf16[1,384,128]{2,1,0:T(8,128)(2,1)S(1)}, u32[]{:S(2)}, u32[]{:S(2)}) %collective-permute-start.8) | collective-permute-done | bytes 98336 | tf_op jit(solution)/shard_map/ppermute | solution.py:38
  77.6 0.7 constant_dynamic-update-slice_fusion.4
  78.2 2.7 %collective-permute-start.9 = (bf16[1,384,128]{2,1,0:T(8,128)(2,1)S(1)}, bf16[1,384,128]{2,1,0:T(8,128)(2,1)S(1)}, u32[]{:S(2)}, u32[]{:S(2)}) collective-permute-start(bf16[1,384,128]{2,1,0:T(8,128)(2,1)S(1)} %get-tuple-element.37), channel_id=1, source_target_pairs={{0,16},{2,18},{4,20},{6,22},{8,24},{10,26},{12,28},{14,30},{16,0},... | collective-permute-start | bytes 294920 | tf_op jit(solution)/shard_map/ppermute | solution.py:38
  80.9 2.9 %collective-permute-done.9 = bf16[1,384,128]{2,1,0:T(8,128)(2,1)S(1)} collective-permute-done((bf16[1,384,128]{2,1,0:T(8,128)(2,1)S(1)}, bf16[1,384,128]{2,1,0:T(8,128)(2,1)S(1)}, u32[]{:S(2)}, u32[]{:S(2)}) %collective-permute-start.9) | collective-permute-done | bytes 98336 | tf_op jit(solution)/shard_map/ppermute | solution.py:38
  83.8 2.2 %collective-permute-start.10 = (bf16[2,384,128]{2,1,0:T(8,128)(2,1)S(1)}, bf16[2,384,128]{2,1,0:T(8,128)(2,1)S(1)}, u32[]{:S(2)}, u32[]{:S(2)}) collective-permute-start(bf16[2,384,128]{2,1,0:T(8,128)(2,1)S(1)} %pad_maximum_fusion.2), channel_id=1, source_target_pairs={{0,8},{2,10},{4,12},{6,14},{8,0},{10,2},{12,4},{14,6},{16,24},{18,... | collective-permute-start | bytes 589832 | tf_op jit(solution)/shard_map/ppermute | solution.py:38
  86.0 3.6 %collective-permute-done.10 = bf16[2,384,128]{2,1,0:T(8,128)(2,1)S(1)} collective-permute-done((bf16[2,384,128]{2,1,0:T(8,128)(2,1)S(1)}, bf16[2,384,128]{2,1,0:T(8,128)(2,1)S(1)}, u32[]{:S(2)}, u32[]{:S(2)}) %collective-permute-start.10) | collective-permute-done | bytes 196640 | tf_op jit(solution)/shard_map/ppermute | solution.py:38
  89.7 0.8 pad_maximum_fusion.1
  90.5 1.5 collective-permute-start.11
  92.2 0.9 copy-done.1
  93.1 6.3 %all-to-all-start = ((bf16[16,192,128]{2,1,0:T(8,128)(2,1)}), bf16[16,192,128]{2,1,0:T(8,128)(2,1)S(1)}, u32[]{:S(2)}, u32[]{:S(2)}) async-start(bf16[16,192,128]{2,1,0:T(8,128)(2,1)} %copy-done.1), calls=%async_computation | async-start | bytes 1572864 | tf_op jit(solution)/shard_map/all_to_all | solution.py:466
  99.4 1.2 pad_maximum_fusion
  101.1 1.1 constant_dynamic-slice_fusion
  102.2 0.6 collective-permute-start.15
  102.8 2.1 %convolution_convert_fusion.pp_ref = bf16[384,2048]{1,0:T(8,128)(2,1)S(1)} fusion(bf16[128,2048]{1,0:T(8,128)(2,1)S(1)} %copy-done.27, bf16[128,2048]{1,0:T(8,128)(2,1)} %collective-permute-done.1, bf16[256,2048]{1,0:T(8,128)(2,1)S(1)} %copy-done.19, s32[512]{0:T(512)S(1)} %add_select_fusion), kind=kOutput, calls=%fused_computation.1 | convolution fusion | flops 812580864 | bytes 3672064 | tf_op jit(solution)/shard_map/dot_general | solution.py:26
  105.1 1.1 constant_dynamic-update-slice_fusion.1
  106.3 1.4 context_product.1
  107.7 1.6 collective-permute-start.14
  109.3 0.8 iota_compare_fusion
  110.1 9.1 %collective-permute-done.15.refs_1_ = bf16[256,1280]{1,0:T(8,128)(2,1)} collective-permute-done((bf16[256,1280]{1,0:T(8,128)(2,1)S(1)}, bf16[256,1280]{1,0:T(8,128)(2,1)}, u32[]{:S(2)}, u32[]{:S(2)}) %collective-permute-start.15) | collective-permute-done | bytes 655392 | tf_op jit(solution)/shard_map/ppermute | solution.py:38
  119.2 6.2 %image_part.1 = (bf16[2,1024,1024]{2,1,0:T(8,128)(2,1)}, f32[1024,128]{1,0:T(8,128)S(1)}, f32[1024,128]{1,0:T(8,128)S(1)}, f32[1024,128]{1,0:T(8,128)S(1)}) custom-call(bf16[16,3,64,128]{3,2,1,0:T(8,128)(2,1)S(1)} %bitcast.32, bf16[16,3,64,128]{3,2,1,0:T(8,128)(2,1)S(1)} %bitcast.33, bf16[16,3,64,128]{3,2,1,0:T(8,128)(2,1)S(1)} %bitcast.34), custom_call_target="tpu_custom_call" | custom-call | tf_op jit(solution)/shard_map/image_part/pallas_call | solution.py:261
  125.9 4.6 %collective-permute-done.13 = bf16[384,128]{1,0:T(8,128)(2,1)S(1)} collective-permute-done((bf16[384,128]{1,0:T(8,128)(2,1)S(1)}, bf16[384,128]{1,0:T(8,128)(2,1)S(1)}, u32[]{:S(2)}, u32[]{:S(2)}) %collective-permute-start.13) | collective-permute-done | bytes 98336 | tf_op jit(solution)/shard_map/ppermute | solution.py:38
  131.0 6.6 %text_part.1 = (bf16[16,64,128]{2,1,0:T(8,128)(2,1)}, bf16[2,1024,256]{2,1,0:T(8,128)(2,1)S(1)}, f32[1024,128]{1,0:T(8,128)S(1)}) custom-call(s32[1]{0:T(128)} %copy.28.len_ref, bf16[16,3,64,128]{3,2,1,0:T(8,128)(2,1)S(1)} %bitcast.35, bf16[256,128]{1,0:T(8,128)(2,1)S(1)} %convolution_convert_fusion.8.ctx_ref, f32[1024,128]{1,0:T(8,128)S(1)} %get-tuple-element.20.o_ref, ...), custom_call_target="tpu_custom_call" | custom-call | tf_op jit(solution)/shard_map/text_part/pallas_call | solution.py:311
  137.6 1.0 copy-done.5
  138.6 0.8 copy-done.7
  139.4 6.3 %all-to-all-start.1 = ((bf16[16,64,128]{2,1,0:T(8,128)(2,1)}), bf16[16,64,128]{2,1,0:T(8,128)(2,1)S(1)}, u32[]{:S(2)}, u32[]{:S(2)}) async-start(bf16[16,64,128]{2,1,0:T(8,128)(2,1)} %get-tuple-element.23.o_ref), calls=%async_computation.1 | async-start | bytes 524288 | tf_op jit(solution)/shard_map/all_to_all | solution.py:466
  145.8 9.9 %all-to-all-done.1.o_ref = bf16[16,64,128]{2,1,0:T(8,128)(2,1)S(1)} async-done(((bf16[16,64,128]{2,1,0:T(8,128)(2,1)}), bf16[16,64,128]{2,1,0:T(8,128)(2,1)S(1)}, u32[]{:S(2)}, u32[]{:S(2)}) %all-to-all-start.1) | async-done | bytes 262176 | tf_op jit(solution)/shard_map/all_to_all | solution.py:466
  155.7 1.3 copy-done.2
  157.0 2.8 %project.1 = (bf16[16,64,128]{2,1,0:T(8,128)(2,1)S(1)}, f32[2,128]{1,0:T(2,128)S(1)}) custom-call(s32[4]{0:T(128)S(1)} %pad_add_fusion.1.idx_ref, bf16[16,64,128]{2,1,0:T(8,128)(2,1)S(1)} %all-to-all-done.1.o_ref, bf16[2,64,1280]{2,1,0:T(8,128)(2,1)S(1)} %bitcast.39, bf16[512,1280]{1,0:T(8,128)(2,1)S(1)} %copy-done.2, ...), custom_call_target="tpu_custom_call" | custom-call | tf_op jit(solution)/shard_map/project/pallas_call | solution.py:378
  159.8 0.7 copy-done.14
  160.5 1.2 collective-permute-done.17
  161.9 3.4 %collective-permute-done.18 = f32[2,128]{1,0:T(2,128)S(1)} collective-permute-done((f32[2,128]{1,0:T(2,128)S(1)}, f32[2,128]{1,0:T(2,128)S(1)}, u32[]{:S(2)}, u32[]{:S(2)}) %collective-permute-start.18) | collective-permute-done | bytes 1056 | tf_op jit(solution)/shard_map/ppermute | solution.py:38
  165.7 3.5 %all-to-all-start.2 = ((bf16[16,64,128]{2,1,0:T(8,128)(2,1)}), bf16[16,64,128]{2,1,0:T(8,128)(2,1)S(1)}, u32[]{:S(2)}, u32[]{:S(2)}) async-start(bf16[16,64,128]{2,1,0:T(8,128)(2,1)} %copy-done.14), calls=%async_computation.2 | async-start | bytes 524288 | tf_op jit(solution)/shard_map/all_to_all | solution.py:466
  169.2 2.9 %collective-permute-start.20 = (f32[2,128]{1,0:T(2,128)S(1)}, f32[2,128]{1,0:T(2,128)S(1)}, u32[]{:S(2)}, u32[]{:S(2)}) collective-permute-start(f32[2,128]{1,0:T(2,128)S(1)} %add.169), channel_id=1, source_target_pairs={{0,16},{2,18},{4,20},{6,22},{8,24},{10,26},{12,28},{14,30},{16,0},... | collective-permute-start | bytes 3080 | tf_op jit(solution)/shard_map/ppermute | solution.py:38
  172.1 0.6 fusion.34
  173.4 5.5 %collective-permute-done.20 = f32[2,128]{1,0:T(2,128)S(1)} collective-permute-done((f32[2,128]{1,0:T(2,128)S(1)}, f32[2,128]{1,0:T(2,128)S(1)}, u32[]{:S(2)}, u32[]{:S(2)}) %collective-permute-start.20) | collective-permute-done | bytes 1056 | tf_op jit(solution)/shard_map/ppermute | solution.py:38
  178.9 0.6 fusion.32
  182.2 1.2 copy-done.6
  183.4 1.0 copy-done.8
  184.5 9.5 %backward_part.1 = (bf16[1,2,1024,64]{3,2,1,0:T(8,128)(2,1)S(1)}, bf16[1,2,1024,64]{3,2,1,0:T(8,128)(2,1)S(1)}, bf16[1,2,1024,64]{3,2,1,0:T(8,128)(2,1)S(1)}) custom-call(f32[2]{0:T(128)S(1)} %pad_maximum_fusion.3.coef_ref, bf16[16,3,64,128]{3,2,1,0:T(8,128)(2,1)S(1)} %bitcast.36, bf16[16,3,64,128]{3,2,1,0:T(8,128)(2,1)S(1)} %bitcast.37, ...), custom_call_target="tpu_custom_call" | custom-call | tf_op jit(solution)/shard_map/backward_part/pallas_call | solution.py:442
  194.0 0.8 copy-done.9
  194.8 0.8 copy-done.10
  195.6 0.8 copy-done.11
  196.4 1.9 copy.20
  198.4 1.9 copy.21
  200.3 1.9 copy.22
  (106 shorter events, 7.2 us)
Async XLA Ops:
  0.6 11.3 %copy-start = (bf16[2048,512]{1,0:T(8,128)(2,1)S(1)}, bf16[2048,512]{1,0:T(8,128)(2,1)}, u32[]{:S(2)}) copy-start(bf16[2048,512]{1,0:T(8,128)(2,1)} %param.22) | copy-start | bytes 6291460
  2.9 9.0 %copy-start.21 = (f32[4096]{0:T(1024)S(1)}, f32[4096]{0:T(1024)}, u32[]{:S(2)}) copy-start(f32[4096]{0:T(1024)} %param.20) | copy-start | bytes 49156
  2.9 20.2 %collective-permute-start.2 = (f32[2,128]{1,0:T(2,128)S(1)}, f32[2,128]{1,0:T(2,128)S(1)}, u32[]{:S(2)}, u32[]{:S(2)}) collective-permute-start(f32[2,128]{1,0:T(2,128)S(1)} %get-tuple-element.41), channel_id=1, source_target_pairs={{0,1},{1,0},{2,3},{3,2},{4,5},{5,4},{6,7},{7,6},{8,9},{9,8},{10,11... | collective-permute-start | bytes 3080 | tf_op jit(solution)/shard_map/ppermute | solution.py:38
  7.9 15.3 %collective-permute-start.1 = (bf16[128,2048]{1,0:T(8,128)(2,1)}, bf16[128,2048]{1,0:T(8,128)(2,1)}, u32[]{:S(2)}, u32[]{:S(2)}) collective-permute-start(bf16[128,2048]{1,0:T(8,128)(2,1)} %dynamic-slice_bitcast_fusion.1), channel_id=1, source_target_pairs={{0,1},{1,0},{2,3},{3,2},{4,5},{5,4},{6,7},{7,6},{8,9},{9,8},{10,11... | collective-permute-start | bytes 1572872 | tf_op jit(solution)/shard_map/ppermute | solution.py:38
  7.9 13.8 %collective-permute-start = (s32[1]{0:T(128)}, s32[1]{0:T(128)}, u32[]{:S(2)}, u32[]{:S(2)}) collective-permute-start(s32[1]{0:T(128)} %param.17), channel_id=1, source_target_pairs={{0,1},{1,0},{2,3},{3,2},{4,5},{5,4},{6,7},{7,6},{8,9},{9,8},{10,11... | collective-permute-start | bytes 20 | tf_op jit(solution)/shard_map/ppermute | solution.py:38
  11.9 1.5 copy-start.18
  11.9 2.0 %copy-start.24 = (bf16[2048,512]{1,0:T(8,128)(2,1)S(1)}, bf16[2048,512]{1,0:T(8,128)(2,1)}, u32[]{:S(2)}) copy-start(bf16[2048,512]{1,0:T(8,128)(2,1)} %param.21) | copy-start | bytes 6291460
  22.3 2.5 %copy-start.25 = (bf16[2048,512]{1,0:T(8,128)(2,1)S(1)}, bf16[2048,512]{1,0:T(8,128)(2,1)}, u32[]{:S(2)}) copy-start(bf16[2048,512]{1,0:T(8,128)(2,1)} %param.21) | copy-start | bytes 6291460
  23.2 3.1 %collective-permute-start.3 = (bf16[128,2048]{1,0:T(8,128)(2,1)}, bf16[128,2048]{1,0:T(8,128)(2,1)S(1)}, u32[]{:S(2)}, u32[]{:S(2)}) collective-permute-start(bf16[128,2048]{1,0:T(8,128)(2,1)} %collective-permute-done.1), channel_id=1, source_target_pairs={{0,2},{2,0},{4,6},{6,4},{8,10},{10,8},{12,14},{14,12},{16,18},{18,... | collective-permute-start | bytes 1572872 | tf_op jit(solution)/shard_map/ppermute | solution.py:38
  26.3 0.8 copy-start.26
  27.1 0.9 copy-start.29
  27.1 1.0 copy-start.30
  28.1 1.0 copy-start.28
  28.7 20.0 %collective-permute-start.4 = (bf16[384,1024]{1,0:T(8,128)(2,1)S(1)}, bf16[384,1024]{1,0:T(8,128)(2,1)S(1)}, u32[]{:S(2)}, u32[]{:S(2)}) collective-permute-start(bf16[384,1024]{1,0:T(8,128)(2,1)S(1)} %convolution_convert_fusion.1), channel_id=1, source_target_pairs={{0,1},{1,0},{2,3},{3,2},{4,5},{5,4},{6,7},{7,6},{8,9},{9,8},{10,11... | collective-permute-start | bytes 2359304 | tf_op jit(solution)/shard_map/ppermute | solution.py:38
  29.1 20.2 %copy-start.3 = (bf16[512,2048]{1,0:T(8,128)(2,1)S(1)}, bf16[512,2048]{1,0:T(8,128)(2,1)}, u32[]{:S(2)}) copy-start(bf16[512,2048]{1,0:T(8,128)(2,1)} %w_ref.2) | copy-start | bytes 6291460
  51.8 2.4 %collective-permute-start.5 = (bf16[8,384,128]{2,1,0:T(8,128)(2,1)S(1)}, bf16[8,384,128]{2,1,0:T(8,128)(2,1)S(1)}, u32[]{:S(2)}, u32[]{:S(2)}) collective-permute-start(bf16[8,384,128]{2,1,0:T(8,128)(2,1)S(1)} %slice.70), channel_id=1, source_target_pairs={{0,2},{2,0},{4,6},{6,4},{8,10},{10,8},{12,14},{14,12},{16,18},{18,... | collective-permute-start | bytes 2359304 | tf_op jit(solution)/shard_map/ppermute | solution.py:38
  54.3 37.6 %copy-start.15 = (bf16[1,2,64,1024]{3,2,1,0:T(8,128)(2,1)S(1)}, bf16[1,2,64,1024]{3,2,1,0:T(8,128)(2,1)}, u32[]{:S(2)}) copy-start(bf16[1,2,64,1024]{3,2,1,0:T(8,128)(2,1)} %param.26) | copy-start | bytes 786436
  54.4 37.6 %copy-start.16 = (bf16[1,2,64,1024]{3,2,1,0:T(8,128)(2,1)S(1)}, bf16[1,2,64,1024]{3,2,1,0:T(8,128)(2,1)}, u32[]{:S(2)}) copy-start(bf16[1,2,64,1024]{3,2,1,0:T(8,128)(2,1)} %param.27) | copy-start | bytes 786436
  54.4 37.6 %copy-start.17 = (bf16[1,2,64,1024]{3,2,1,0:T(8,128)(2,1)S(1)}, bf16[1,2,64,1024]{3,2,1,0:T(8,128)(2,1)}, u32[]{:S(2)}) copy-start(bf16[1,2,64,1024]{3,2,1,0:T(8,128)(2,1)} %param.28) | copy-start | bytes 786436
  54.4 11.2 %collective-permute-start.6 = (bf16[4,384,128]{2,1,0:T(8,128)(2,1)S(1)}, bf16[4,384,128]{2,1,0:T(8,128)(2,1)S(1)}, u32[]{:S(2)}, u32[]{:S(2)}) collective-permute-start(bf16[4,384,128]{2,1,0:T(8,128)(2,1)S(1)} %slice.72), channel_id=1, source_target_pairs={{0,4},{2,6},{4,0},{6,2},{8,12},{10,14},{12,8},{14,10},{16,20},{18,... | collective-permute-start | bytes 1179656 | tf_op jit(solution)/shard_map/ppermute | solution.py:38
  65.7 6.2 %collective-permute-start.7 = (bf16[2,384,128]{2,1,0:T(8,128)(2,1)S(1)}, bf16[2,384,128]{2,1,0:T(8,128)(2,1)S(1)}, u32[]{:S(2)}, u32[]{:S(2)}) collective-permute-start(bf16[2,384,128]{2,1,0:T(8,128)(2,1)S(1)} %slice.74), channel_id=1, source_target_pairs={{0,8},{2,10},{4,12},{6,14},{8,0},{10,2},{12,4},{14,6},{16,24},{18,... | collective-permute-start | bytes 589832 | tf_op jit(solution)/shard_map/ppermute | solution.py:38
  72.0 5.6 %collective-permute-start.8 = (bf16[1,384,128]{2,1,0:T(8,128)(2,1)S(1)}, bf16[1,384,128]{2,1,0:T(8,128)(2,1)S(1)}, u32[]{:S(2)}, u32[]{:S(2)}) collective-permute-start(bf16[1,384,128]{2,1,0:T(8,128)(2,1)S(1)} %slice.76), channel_id=1, source_target_pairs={{0,16},{2,18},{4,20},{6,22},{8,24},{10,26},{12,28},{14,30},{16,0},... | collective-permute-start | bytes 294920 | tf_op jit(solution)/shard_map/ppermute | solution.py:38
  78.2 5.6 %collective-permute-start.9 = (bf16[1,384,128]{2,1,0:T(8,128)(2,1)S(1)}, bf16[1,384,128]{2,1,0:T(8,128)(2,1)S(1)}, u32[]{:S(2)}, u32[]{:S(2)}) collective-permute-start(bf16[1,384,128]{2,1,0:T(8,128)(2,1)S(1)} %get-tuple-element.37), channel_id=1, source_target_pairs={{0,16},{2,18},{4,20},{6,22},{8,24},{10,26},{12,28},{14,30},{16,0},... | collective-permute-start | bytes 294920 | tf_op jit(solution)/shard_map/ppermute | solution.py:38
  83.8 5.8 %collective-permute-start.10 = (bf16[2,384,128]{2,1,0:T(8,128)(2,1)S(1)}, bf16[2,384,128]{2,1,0:T(8,128)(2,1)S(1)}, u32[]{:S(2)}, u32[]{:S(2)}) collective-permute-start(bf16[2,384,128]{2,1,0:T(8,128)(2,1)S(1)} %pad_maximum_fusion.2), channel_id=1, source_target_pairs={{0,8},{2,10},{4,12},{6,14},{8,0},{10,2},{12,4},{14,6},{16,24},{18,... | collective-permute-start | bytes 589832 | tf_op jit(solution)/shard_map/ppermute | solution.py:38
  90.5 9.0 %collective-permute-start.11 = (bf16[4,384,128]{2,1,0:T(8,128)(2,1)}, bf16[4,384,128]{2,1,0:T(8,128)(2,1)}, u32[]{:S(2)}, u32[]{:S(2)}) collective-permute-start(bf16[4,384,128]{2,1,0:T(8,128)(2,1)} %pad_maximum_fusion.1), channel_id=1, source_target_pairs={{0,4},{2,6},{4,0},{6,2},{8,12},{10,14},{12,8},{14,10},{16,20},{18,... | collective-permute-start | bytes 1179656 | tf_op jit(solution)/shard_map/ppermute | solution.py:38
  92.2 0.9 copy-start.1
  93.1 9.7 %copy-start.22 = (f32[4096]{0:T(1024)S(1)}, f32[4096]{0:T(1024)}, u32[]{:S(2)}) copy-start(f32[4096]{0:T(1024)} %param.24) | copy-start | bytes 49156
  93.1 26.1 %all-to-all-start = ((bf16[16,192,128]{2,1,0:T(8,128)(2,1)}), bf16[16,192,128]{2,1,0:T(8,128)(2,1)S(1)}, u32[]{:S(2)}, u32[]{:S(2)}) async-start(bf16[16,192,128]{2,1,0:T(8,128)(2,1)} %copy-done.1), calls=%async_computation | async-start | bytes 1572864 | tf_op jit(solution)/shard_map/all_to_all | solution.py:466
  99.4 3.4 %copy-start.19 = (bf16[256,2048]{1,0:T(8,128)(2,1)S(1)}, bf16[256,2048]{1,0:T(8,128)(2,1)}, u32[]{:S(2)}) copy-start(bf16[256,2048]{1,0:T(8,128)(2,1)} %copy-done.18) | copy-start | bytes 3145732
  99.4 3.4 %copy-start.27 = (bf16[128,2048]{1,0:T(8,128)(2,1)S(1)}, bf16[128,2048]{1,0:T(8,128)(2,1)}, u32[]{:S(2)}) copy-start(bf16[128,2048]{1,0:T(8,128)(2,1)} %copy-done.26) | copy-start | bytes 1572868
  100.6 5.5 %collective-permute-start.12 = (bf16[8,384,128]{2,1,0:T(8,128)(2,1)S(1)}, bf16[8,384,128]{2,1,0:T(8,128)(2,1)S(1)}, u32[]{:S(2)}, u32[]{:S(2)}) collective-permute-start(bf16[8,384,128]{2,1,0:T(8,128)(2,1)S(1)} %pad_maximum_fusion), channel_id=1, source_target_pairs={{0,2},{2,0},{4,6},{6,4},{8,10},{10,8},{12,14},{14,12},{16,18},{18,... | collective-permute-start | bytes 2359304 | tf_op jit(solution)/shard_map/ppermute | solution.py:38
  102.2 16.9 %collective-permute-start.15 = (bf16[256,1280]{1,0:T(8,128)(2,1)S(1)}, bf16[256,1280]{1,0:T(8,128)(2,1)}, u32[]{:S(2)}, u32[]{:S(2)}) collective-permute-start(bf16[256,1280]{1,0:T(8,128)(2,1)S(1)} %constant_dynamic-slice_fusion), channel_id=1, source_target_pairs={{0,1},{1,0},{2,3},{3,2},{4,5},{5,4},{6,7},{7,6},{8,9},{9,8},{10,11... | collective-permute-start | bytes 1966088 | tf_op jit(solution)/shard_map/ppermute | solution.py:38
  102.8 2.2 %copy-start.4 = (bf16[16,384,128]{2,1,0:T(8,128)(2,1)S(1)}, bf16[16,384,128]{2,1,0:T(8,128)(2,1)}, u32[]{:S(2)}) copy-start(bf16[16,384,128]{2,1,0:T(8,128)(2,1)} %get-tuple-element.36) | copy-start | bytes 4718596
  105.0 1.3 copy-start.12
  107.7 18.2 %collective-permute-start.14 = (f32[1,384]{1,0:T(1,128)S(1)}, f32[1,384]{1,0:T(1,128)S(1)}, u32[]{:S(2)}, u32[]{:S(2)}) collective-permute-start(f32[1,384]{1,0:T(1,128)S(1)} %get-tuple-element.19), channel_id=1, source_target_pairs={{0,1},{1,0},{2,3},{3,2},{4,5},{5,4},{6,7},{7,6},{8,9},{9,8},{10,11... | collective-permute-start | bytes 4616 | tf_op jit(solution)/shard_map/ppermute | solution.py:38
  119.2 26.6 %collective-permute-start.16 = (bf16[256,1280]{1,0:T(8,128)(2,1)}, bf16[256,1280]{1,0:T(8,128)(2,1)}, u32[]{:S(2)}, u32[]{:S(2)}) collective-permute-start(bf16[256,1280]{1,0:T(8,128)(2,1)} %collective-permute-done.15.refs_1_), channel_id=1, source_target_pairs={{0,2},{2,0},{4,6},{6,4},{8,10},{10,8},{12,14},{14,12},{16,18},{18,... | collective-permute-start | bytes 1966088 | tf_op jit(solution)/shard_map/ppermute | solution.py:38
  119.2 11.4 %copy-start.20 = (pred[384,512]{1,0:T(32,128)(4,1)S(1)}, pred[384,512]{1,0:T(32,128)(4,1)}, u32[]{:S(2)}) copy-start(pred[384,512]{1,0:T(32,128)(4,1)} %iota_compare_fusion) | copy-start | bytes 589828
  125.4 30.3 %copy-start.13 = (bf16[1,2,64,1280]{3,2,1,0:T(8,128)(2,1)S(1)}, bf16[1,2,64,1280]{3,2,1,0:T(8,128)(2,1)}, u32[]{:S(2)}) copy-start(bf16[1,2,64,1280]{3,2,1,0:T(8,128)(2,1)} %param.30) | copy-start | bytes 983044
  125.4 5.2 %collective-permute-start.13 = (bf16[384,128]{1,0:T(8,128)(2,1)S(1)}, bf16[384,128]{1,0:T(8,128)(2,1)S(1)}, u32[]{:S(2)}, u32[]{:S(2)}) collective-permute-start(bf16[384,128]{1,0:T(8,128)(2,1)S(1)} %get-tuple-element.18), channel_id=1, source_target_pairs={{0,1},{1,0},{2,3},{3,2},{4,5},{5,4},{6,7},{7,6},{8,9},{9,8},{10,11... | collective-permute-start | bytes 294920 | tf_op jit(solution)/shard_map/ppermute | solution.py:38
  137.6 1.0 copy-start.5
  138.6 0.8 copy-start.7
  139.4 32.7 %copy-start.23 = (f32[1,2]{1,0:T(1,128)S(1)}, f32[1,2]{1,0:T(1,128)}, u32[]{:S(2)}) copy-start(f32[1,2]{1,0:T(1,128)} %param.19) | copy-start | bytes 28
  139.4 16.3 %all-to-all-start.1 = ((bf16[16,64,128]{2,1,0:T(8,128)(2,1)}), bf16[16,64,128]{2,1,0:T(8,128)(2,1)S(1)}, u32[]{:S(2)}, u32[]{:S(2)}) async-start(bf16[16,64,128]{2,1,0:T(8,128)(2,1)} %get-tuple-element.23.o_ref), calls=%async_computation.1 | async-start | bytes 524288 | tf_op jit(solution)/shard_map/all_to_all | solution.py:466
  155.7 1.3 copy-start.2
  159.8 0.7 copy-start.14
  160.5 1.2 collective-permute-start.17
  161.7 3.6 %collective-permute-start.18 = (f32[2,128]{1,0:T(2,128)S(1)}, f32[2,128]{1,0:T(2,128)S(1)}, u32[]{:S(2)}, u32[]{:S(2)}) collective-permute-start(f32[2,128]{1,0:T(2,128)S(1)} %add.167), channel_id=1, source_target_pairs={{0,4},{2,6},{4,0},{6,2},{8,12},{10,14},{12,8},{14,10},{16,20},{18,... | collective-permute-start | bytes 3080 | tf_op jit(solution)/shard_map/ppermute | solution.py:38
  165.3 3.9 %collective-permute-start.19 = (f32[2,128]{1,0:T(2,128)S(1)}, f32[2,128]{1,0:T(2,128)S(1)}, u32[]{:S(2)}, u32[]{:S(2)}) collective-permute-start(f32[2,128]{1,0:T(2,128)S(1)} %add.168), channel_id=1, source_target_pairs={{0,8},{2,10},{4,12},{6,14},{8,0},{10,2},{12,4},{14,6},{16,24},{18,... | collective-permute-start | bytes 3080 | tf_op jit(solution)/shard_map/ppermute | solution.py:38
  165.7 16.5 %all-to-all-start.2 = ((bf16[16,64,128]{2,1,0:T(8,128)(2,1)}), bf16[16,64,128]{2,1,0:T(8,128)(2,1)S(1)}, u32[]{:S(2)}, u32[]{:S(2)}) async-start(bf16[16,64,128]{2,1,0:T(8,128)(2,1)} %copy-done.14), calls=%async_computation.2 | async-start | bytes 524288 | tf_op jit(solution)/shard_map/all_to_all | solution.py:466
  169.2 9.6 %collective-permute-start.20 = (f32[2,128]{1,0:T(2,128)S(1)}, f32[2,128]{1,0:T(2,128)S(1)}, u32[]{:S(2)}, u32[]{:S(2)}) collective-permute-start(f32[2,128]{1,0:T(2,128)S(1)} %add.169), channel_id=1, source_target_pairs={{0,16},{2,18},{4,20},{6,22},{8,24},{10,26},{12,28},{14,30},{16,0},... | collective-permute-start | bytes 3080 | tf_op jit(solution)/shard_map/ppermute | solution.py:38
  182.2 1.2 copy-start.6
  183.4 1.0 copy-start.8
  194.0 0.8 copy-start.9
  194.8 0.8 copy-start.10
  195.6 0.8 copy-start.11

commit v2 on v1

v2 whole, which is shorter than its diff:
```python
import functools
import math

import jax
import jax.numpy as jnp
from jax import lax
from jax.experimental import pallas as pl
from jax.experimental.pallas import tpu as pltpu
from jax.sharding import PartitionSpec as P


HEAD = 64
LANES = 128
CHUNKS = 2
PARTS = 3
EXTRA = 8
f32 = jnp.float32
bf16 = jnp.bfloat16

dpo_beta = 20.0
norm_eps = 1e-06
inv_root = 1.0 / math.sqrt(HEAD)


def noise_level(step_index):
    fraction = (step_index.astype(f32) + 1.0) / 1000.0
    return 3.0 * fraction / (1.0 + 2.0 * fraction)


def dot(a, b):
    return jnp.dot(a, b, preferred_element_type=f32)


def dot_nt(a, b):
    return lax.dot_general(a, b, (((1,), (1,)), ((), ())), preferred_element_type=f32)


def dot_tn(a, b):
    return lax.dot_general(a, b, (((0,), (0,)), ((), ())), preferred_element_type=f32)


def swap(x, axis, size, mask):
    return lax.ppermute(x, axis, [(i, i ^ mask) for i in range(size)])


barrier = lax.optimization_barrier


def cost(flops, *arrays, exps=0):
    moved = sum(math.prod(a.shape) * a.dtype.itemsize for a in arrays)
    return pl.CostEstimate(flops=int(flops), bytes_accessed=moved, transcendentals=int(exps))


def vmem():
    return pl.BlockSpec(memory_space=pltpu.VMEM)


def in_hbm(x):
    return pltpu.with_memory_space_constraint(x, pltpu.HBM)


def hbm():
    return pl.BlockSpec(memory_space=pltpu.HBM)


def smem():
    return pl.BlockSpec(memory_space=pltpu.SMEM)


params = pltpu.CompilerParams(vmem_limit_bytes=20 * 1024 * 1024)


def exchange(x):
    return lax.all_to_all(x, "seq", split_axis=0, concat_axis=0, tiled=True)


def pack_kernel(q_ref, k_ref, v_ref, out_ref):
    tok = q_ref.shape[1]
    for n, ref in enumerate((q_ref, k_ref, v_ref)):
        for pair in range(ref.shape[2] // LANES):
            a = ref[0, :, pair * LANES : (pair + 1) * LANES]
            b = ref[1, :, pair * LANES : (pair + 1) * LANES]
            rows = slice(n * tok, (n + 1) * tok)
            out_ref[2 * pair, rows, :] = jnp.concatenate([a[:, :HEAD], b[:, :HEAD]], axis=1)
            out_ref[2 * pair + 1, rows, :] = jnp.concatenate([a[:, HEAD:], b[:, HEAD:]], axis=1)


def pack_heads(q, k, v):
    tok, inner = q.shape[1], q.shape[2]
    return pl.pallas_call(
        pack_kernel,
        out_shape=jax.ShapeDtypeStruct((inner // HEAD, 3 * tok, LANES), bf16),
        in_specs=[vmem()] * 3,
        out_specs=vmem(),
        compiler_params=params,
        cost_estimate=cost(0, q, k, v, q, k, v),
        name="pack_heads",
    )(q, k, v)


def down_kernel(idx_ref, mine_ref, got_ref, w_ref, out_ref, wide_ref):
    units = w_ref.shape[0]
    both = mine_ref[...].astype(f32) + got_ref[...].astype(f32)
    gate = both[:, :units]
    hidden = (jax.nn.gelu(gate, approximate=True) * both[:, units:]).astype(bf16)
    wide_ref[...] = dot(hidden, w_ref[...]).astype(bf16)
    for p in range(out_ref.shape[0]):
        start = pl.multiple_of(idx_ref[p] * LANES, LANES)
        out_ref[p] = wide_ref[:, pl.ds(start, LANES)]


def down_product(idx, mine, got, w_down):
    blocks, rows = w_down.shape[1] // LANES, mine.shape[0]
    return pl.pallas_call(
        down_kernel,
        out_shape=jax.ShapeDtypeStruct((blocks, rows, LANES), bf16),
        in_specs=[smem(), vmem(), vmem(), vmem()],
        out_specs=vmem(),
        scratch_shapes=[pltpu.VMEM((rows, w_down.shape[1]), bf16)],
        compiler_params=params,
        cost_estimate=cost(2 * rows * w_down.size, mine, got, w_down, exps=mine.size // 2),
        name="down_product",
    )(idx, mine, got, w_down)


def context_kernel(idx_ref, pp_ref, gain_ref, w_ref, *refs):
    y_refs, ctx_ref, sq_ref = refs[:-2], refs[-2], refs[-1]
    rows = pp_ref.shape[0]
    acc = jnp.zeros((rows, w_ref.shape[1]), f32)
    sq = jnp.zeros((rows, LANES), f32)
    p = 0
    for ref in y_refs:
        for n in range(ref.shape[0]):
            start = pl.multiple_of(idx_ref[p] * LANES, LANES)
            state = ref[n].astype(f32) + pp_ref[:, pl.ds(start, LANES)].astype(f32)
            sq = sq + state * state
            scaled = (state * gain_ref[:, pl.ds(start, LANES)]).astype(bf16)
            acc = acc + dot(scaled, w_ref[pl.ds(start, LANES), :])
            p += 1
    ctx_ref[...] = acc.astype(bf16)
    sq_ref[...] = jnp.sum(sq.T, axis=0, keepdims=True)


def context_product(idx, packed_prompt, gain, w_context, pieces):
    rows = packed_prompt.shape[0]
    return pl.pallas_call(
        context_kernel,
        out_shape=(
            jax.ShapeDtypeStruct((rows, w_context.shape[1]), bf16),
            jax.ShapeDtypeStruct((1, rows), f32),
        ),
        in_specs=[smem()] + [vmem()] * (3 + len(pieces)),
        out_specs=(vmem(), vmem()),
        compiler_params=params,
        cost_estimate=cost(4 * rows * w_context.size, packed_prompt, w_context, *pieces),
        name="context_product",
    )(idx, packed_prompt, gain, w_context, *pieces)


def column(row):
    return jnp.broadcast_to(row, (LANES, row.shape[1])).T


def corner_kernel(at_ref, in_ref, out_ref, sem):
    rows, cols = out_ref.shape
    row = pl.multiple_of(at_ref[0] * rows, 16)
    col = pl.multiple_of(at_ref[1] * cols, LANES)
    copy = pltpu.make_async_copy(in_ref.at[pl.ds(row, rows), pl.ds(col, cols)], out_ref, sem)
    copy.start()
    copy.wait()


def corner(at, array, rows, cols):
    out = jax.ShapeDtypeStruct((rows, cols), array.dtype)
    return pl.pallas_call(
        corner_kernel,
        out_shape=out,
        in_specs=[smem(), hbm()],
        out_specs=vmem(),
        scratch_shapes=[pltpu.SemaphoreType.DMA(())],
        compiler_params=params,
        cost_estimate=cost(0, out, out),
        name="corner",
    )(at, in_hbm(array))


def weight_copies(w_refs, buf_ref, sems):
    copies = []
    rows = w_refs[0].shape[0] // CHUNKS
    for n, ref in enumerate(w_refs):
        for chunk in range(CHUNKS):
            at = pl.ds(chunk * rows, rows)
            copies.append(
                pltpu.make_async_copy(ref.at[at], buf_ref.at[n, at], sems.at[n * CHUNKS + chunk])
            )
    for copy in copies:
        copy.start()
    return copies


def two_products(normed, buf_ref, copies, out_ref):
    units = buf_ref.shape[2]
    rows = buf_ref.shape[1] // CHUNKS
    for n in range(2):
        acc = None
        for chunk in range(CHUNKS):
            copies[n * CHUNKS + chunk].wait()
            at = slice(chunk * rows, (chunk + 1) * rows)
            term = dot(normed[:, at], buf_ref[n, at, :])
            acc = term if acc is None else acc + term
        out_ref[:, n * units : (n + 1) * units] = acc.astype(bf16)


def weight_scratch(w):
    return [pltpu.VMEM((2, *w.shape), bf16), pltpu.SemaphoreType.DMA((2 * CHUNKS,))]


def gate_up_own_kernel(
    at_ref, prompt_hbm, gain_ref, wg_ref, wu_ref, out_ref, scale_ref, here_ref,
    buf_ref, sems, prompt_ref, prompt_sem,
):
    prompt_copy = pltpu.make_async_copy(prompt_hbm, prompt_ref, prompt_sem)
    prompt_copy.start()
    copies = weight_copies((wg_ref, wu_ref), buf_ref, sems)
    prompt_copy.wait()
    value = prompt_ref[...].astype(f32)
    scale = lax.rsqrt(jnp.mean(value * value, axis=-1, keepdims=True) + norm_eps)
    cols = wg_ref.shape[0]
    start = pl.multiple_of(at_ref[0] * cols, LANES)
    here_ref[...] = prompt_ref[:, pl.ds(start, cols)]
    here = here_ref[...].astype(f32)
    normed = (here * scale * gain_ref[:, pl.ds(start, cols)]).astype(bf16)
    scale_ref[...] = jnp.broadcast_to(scale, (scale.shape[0], LANES)).T[:1]
    two_products(normed, buf_ref, copies, out_ref)


def gate_up_own(at, prompt, gain, w_gate, w_up):
    rows = prompt.shape[0]
    return pl.pallas_call(
        gate_up_own_kernel,
        out_shape=(
            pltpu.HBM((rows, 2 * w_gate.shape[1]), bf16),
            jax.ShapeDtypeStruct((1, rows), f32),
            pltpu.HBM((rows, w_gate.shape[0]), bf16),
        ),
        in_specs=[smem(), hbm(), vmem(), hbm(), hbm()],
        out_specs=(vmem(), vmem(), vmem()),
        scratch_shapes=weight_scratch(w_gate)
        + [pltpu.VMEM(prompt.shape, bf16), pltpu.SemaphoreType.DMA(())],
        compiler_params=params,
        cost_estimate=cost(4 * prompt.shape[0] * w_gate.size, prompt, w_gate, w_up),
        name="gate_up_own",
    )(at, in_hbm(prompt), gain, in_hbm(w_gate), in_hbm(w_up))


def gate_up_other_kernel(
    at_ref, a_hbm, b_ref, scale_ref, gain_ref, wg_ref, wu_ref, own_hbm, select_ref, out_ref,
    parts_ref, buf_ref, sems, a_ref, own_ref, more_sems,
):
    a_copy = pltpu.make_async_copy(a_hbm, a_ref, more_sems.at[0])
    own_copy = pltpu.make_async_copy(own_hbm, own_ref, more_sems.at[1])
    a_copy.start()
    copies = weight_copies((wg_ref, wu_ref), buf_ref, sems)
    own_copy.start()
    cols = wg_ref.shape[0]
    half = a_ref.shape[0]
    rows = own_ref.shape[0]
    start = pl.multiple_of(at_ref[0] * cols, LANES)
    gain = gain_ref[:, pl.ds(start, cols)]
    scales = column(scale_ref[...])
    swapped = at_ref[1] == 1
    low, high = scales[:half, :1], scales[half:, :1]
    scale_a = jnp.where(swapped, high, low)
    scale_b = jnp.where(swapped, low, high)
    a_copy.wait()
    normed = jnp.concatenate(
        [
            (a_ref[...].astype(f32) * scale_a * gain).astype(bf16),
            (b_ref[...].astype(f32) * scale_b * gain).astype(bf16),
        ],
        axis=0,
    )
    select = select_ref[...]
    two_products(normed, buf_ref, copies, parts_ref)
    own_copy.wait()
    packed = dot(select[:, :rows], own_ref[...]) + dot(select[:, rows:], parts_ref[...])
    out_ref[...] = packed.astype(bf16)


def gate_up_other(at, a, b, scale, gain, w_gate, w_up, own, select):
    return pl.pallas_call(
        gate_up_other_kernel,
        out_shape=jax.ShapeDtypeStruct((select.shape[0], own.shape[1]), bf16),
        in_specs=[smem(), hbm()] + [vmem()] * 3 + [hbm()] * 3 + [vmem()],
        out_specs=vmem(),
        scratch_shapes=[pltpu.VMEM(own.shape, bf16)]
        + weight_scratch(w_gate)
        + [pltpu.VMEM(a.shape, bf16), pltpu.VMEM(own.shape, bf16), pltpu.SemaphoreType.DMA((2,))],
        compiler_params=params,
        cost_estimate=cost(6 * own.shape[0] * w_gate.size, a, b, w_gate, w_up, own, own),
        name="gate_up_other",
    )(at, in_hbm(a), b, scale, gain, in_hbm(w_gate), in_hbm(w_up), in_hbm(own), select)


def bit_reversed(size):
    bits = size.bit_length() - 1
    return [int(format(p, "b").zfill(bits)[::-1], 2) if bits else 0 for p in range(size)]


def encode_shared(
    S, prompt, lengths, gain_ffn, w_gate, w_up, w_down, gain_final, w_context, w_out, qkv_in
):
    s = lax.axis_index("seq")
    f = lax.axis_index("fsdp")
    own = prompt[0]
    rows, width = own.shape
    cols = width // 2
    half = rows // 2
    core = s & 1

    away = corner(jnp.stack([core, 1 - f]).astype(jnp.int32), own, half, cols)
    got_a = swap(away, "fsdp", 2, 1)
    other_len = swap(lengths, "fsdp", 2, 1)[0]
    away, own = barrier((away, own))
    at = jnp.stack([f, core]).astype(jnp.int32)
    parts_own, scale, here = gate_up_own(at, own, gain_ffn[None], w_gate, w_up)
    other_scale = swap(scale, "fsdp", 2, 1)

    first = core * half
    own_len = lengths[0]
    own_start = jnp.where(f == 0, 0, other_len)
    other_start = jnp.where(f == 0, own_len, 0)
    row = jnp.arange(half, dtype=jnp.int32)
    source = jnp.concatenate([row, row + half, row + first, row + half - first])
    is_own = jnp.arange(2 * rows) < rows
    place = source + jnp.where(is_own, own_start, other_start)
    place = jnp.where(source < jnp.where(is_own, own_len, other_len), place, -1)
    total = rows * 3 // 2
    select = (jnp.arange(total)[:, None] == place[None, :]).astype(bf16)
    got_a, parts_own, other_scale, select, here = barrier(
        (got_a, parts_own, other_scale, select, here)
    )
    got_b = swap(got_a, "seq", S, 1)

    packed = gate_up_other(
        at, got_a, got_b, other_scale, gain_ffn[None], w_gate, w_up, parts_own, select
    )
    received = swap(packed, "fsdp", 2, 1)
    packed, got_a, got_b, here, select, *qkv_in = barrier(
        (packed, got_a, got_b, here, select, *qkv_in)
    )
    blocks = pack_heads(*qkv_in)
    qkv = exchange(blocks)
    packed_prompt = dot(select, jnp.concatenate([here, got_a, got_b], axis=0)).astype(bf16)
    idx = jnp.array(bit_reversed(S), jnp.int32) ^ s
    w_half = w_out.shape[0] // 2
    w_away = corner(jnp.stack([core, 0]).astype(jnp.int32), w_out, w_half, w_out.shape[1])
    received, packed_prompt, blocks, w_away = barrier((received, packed_prompt, blocks, w_away))

    w_a = swap(w_away, "fsdp", 2, 1)

    x = down_product(idx, packed, received, w_down)

    masks = [1 << b for b in range(S.bit_length() - 1)]
    image = None
    for n, mask in enumerate(masks):
        mid = x.shape[0] // 2
        got = swap(x[mid:], "seq", S, mask)
        if n == 1:
            x, qkv = barrier((x, qkv))
            image = image_part(qkv.reshape(S, 3, -1, LANES))
            got, image = barrier((got, image))
        if n == 2:
            got, w_a = barrier((got, w_a))
            w_b = swap(w_a, "seq", S, 1)
        x = (x[:mid].astype(f32) + got.astype(f32)).astype(bf16)
    pieces = [x]
    for n, mask in enumerate(reversed(masks)):
        last = mask == 1
        if not last and len(pieces) > 1:
            pieces = [jnp.concatenate(pieces, axis=0)]
        got = [swap(piece, "seq", S, mask) for piece in pieces]
        if n == 1:
            got[0], w_b = barrier((got[0], w_b))
        pieces = pieces + got

    gain_here = lax.dynamic_slice(gain_final, (f * cols,), (cols,))[None]
    ctx, sq = context_product(idx, packed_prompt, gain_here, w_context, pieces)
    ctx_other = swap(ctx, "fsdp", 2, 1)
    sq_other = swap(sq, "fsdp", 2, 1)
    inv = lax.rsqrt((sq + sq_other)[0] / width + norm_eps)
    ctx = ((ctx.astype(f32) + ctx_other.astype(f32)) * inv[:, None]).astype(bf16)
    ctx = dot_tn(select[:, :rows], ctx).astype(bf16)
    there = 2 * (1 - f)
    w_idx = jnp.stack([2 * f, 2 * f + 1, there + core, there + 1 - core]).astype(jnp.int32)
    return ctx, qkv.reshape(S, 3, -1, LANES), image, (w_out, w_a, w_b), w_idx


def rms_gain(values, gain):
    mean_sq = jnp.mean(values * values, axis=-1, keepdims=True)
    return values * lax.rsqrt(mean_sq + norm_eps) * gain


def encode_gathered(prompt, gain_ffn, w_gate, w_up, w_down, gain_final, w_context):
    gate_full = lax.all_gather(w_gate, "fsdp", axis=0, tiled=True)
    up_full = lax.all_gather(w_up, "fsdp", axis=0, tiled=True)
    down_full = lax.all_gather(w_down, "fsdp", axis=1, tiled=True)
    context_full = lax.all_gather(w_context, "fsdp", axis=0, tiled=True)
    prompt_f32 = prompt[0].astype(f32)
    normed = rms_gain(prompt_f32, gain_ffn).astype(bf16)
    hidden = (
        jax.nn.gelu(dot(normed, gate_full), approximate=True) * dot(normed, up_full)
    ).astype(bf16)
    summed = lax.psum(dot(hidden, down_full).astype(bf16), "seq").astype(f32)
    encoded = rms_gain(prompt_f32 + summed, gain_final).astype(bf16)
    return dot(encoded, context_full).astype(bf16)


def lanes_of(stream):
    return slice(stream * HEAD, (stream + 1) * HEAD)


def rows_of(ref):
    value = ref[...]
    return value.reshape(-1, LANES)


def with_ones(values):
    return jnp.concatenate([values, jnp.ones(values.shape, values.dtype)], axis=1)


def image_kernel(q_ref, k_ref, v_ref, e_ref, o_ref, m_ref, l_ref):
    q, k, v = rows_of(q_ref), rows_of(k_ref), rows_of(v_ref)
    rows = q.shape[0]
    outs, tops, sums = [], [], []
    for stream in range(2):
        at = lanes_of(stream)
        scores = dot_nt(q[:, at] * jnp.asarray(inv_root, bf16), k[:, at])
        top = jnp.max(scores, axis=-1, keepdims=True)
        e = jnp.exp(scores - top)
        eb = e.astype(bf16)
        e_ref[stream] = eb
        both = dot(eb, with_ones(v[:, at]))
        outs.append(both[:, :HEAD])
        tops.append(jnp.broadcast_to(top, (rows, HEAD)))
        sums.append(both[:, HEAD:])
    o_ref[...] = jnp.concatenate(outs, axis=1)
    m_ref[...] = jnp.concatenate(tops, axis=1)
    l_ref[...] = jnp.concatenate(sums, axis=1)


def q_blocks(S, tok):
    rows = min(256, S * tok)
    return rows // tok, S * tok // rows, rows


def image_part(qkv):
    S, _, tok, _ = qkv.shape
    group, steps, rows = q_blocks(S, tok)
    seq_len = S * tok
    whole = lambda n: pl.BlockSpec((S, None, tok, LANES), lambda i: (0, n, 0, 0))
    flat = pl.BlockSpec((rows, LANES), lambda i: (i, 0))
    return pl.pallas_call(
        image_kernel,
        grid=(steps,),
        out_shape=(pltpu.HBM((2, seq_len, seq_len), bf16),)
        + (pltpu.HBM((seq_len, LANES), f32),) * 3,
        in_specs=[
            pl.BlockSpec((group, None, tok, LANES), lambda i: (i, 0, 0, 0)),
            whole(1),
            whole(2),
        ],
        out_specs=(pl.BlockSpec((2, rows, seq_len), lambda i: (0, i, 0)), flat, flat, flat),
        compiler_params=params,
        cost_estimate=cost(16 * seq_len * seq_len * LANES, qkv, exps=2 * seq_len * seq_len),
        name="image_part",
    )(qkv, qkv, qkv)


def text_kernel(len_ref, q_ref, ctx_ref, o_ref, m_ref, l_ref, out_ref, p_ref, c_ref):
    q = rows_of(q_ref)
    ctx = ctx_ref[...]
    keys, values = ctx[:, :HEAD], ctx[:, HEAD:]
    keep = lax.broadcasted_iota(jnp.int32, (q.shape[0], ctx.shape[0]), 1) < len_ref[0]
    outs, scales = [], []
    for stream in range(2):
        at = lanes_of(stream)
        scores = dot_nt(q[:, at] * jnp.asarray(inv_root, bf16), keys)
        scores = jnp.where(keep, scores, -jnp.inf)
        top_image = m_ref[:, stream * HEAD : stream * HEAD + 1]
        top = jnp.maximum(top_image, jnp.max(scores, axis=-1, keepdims=True))
        e = jnp.exp(scores - top)
        eb = e.astype(bf16)
        both = dot(eb, with_ones(values))
        shrink = jnp.exp(m_ref[:, at] - top)
        inv = 1.0 / (l_ref[:, at] * shrink + both[:, HEAD:])
        scale = shrink * inv
        p_ref[stream] = (e * inv[:, :1]).astype(bf16)
        outs.append(o_ref[:, at] * scale + both[:, :HEAD] * inv)
        scales.append(scale)
    out = jnp.concatenate(outs, axis=1).astype(bf16)
    out_ref[...] = out.reshape(out_ref.shape)
    c_ref[...] = jnp.concatenate(scales, axis=1)


def text_part(lengths, qkv, ctx, o_img, m_img, l_img):
    S, _, tok, _ = qkv.shape
    group, steps, rows = q_blocks(S, tok)
    seq_len = S * tok
    text = ctx.shape[0]
    flat = pl.BlockSpec((rows, LANES), lambda i: (i, 0))
    return pl.pallas_call(
        text_kernel,
        grid=(steps,),
        out_shape=(
            pltpu.HBM((S, tok, LANES), bf16),
            pltpu.HBM((2, seq_len, text), bf16),
            pltpu.HBM((seq_len, LANES), f32),
        ),
        in_specs=[
            smem(),
            pl.BlockSpec((group, None, tok, LANES), lambda i: (i, 0, 0, 0)),
            pl.BlockSpec((text, LANES), lambda i: (0, 0)),
            flat,
            flat,
            flat,
        ],
        out_specs=(
            pl.BlockSpec((group, tok, LANES), lambda i: (i, 0, 0)),
            pl.BlockSpec((2, rows, text), lambda i: (0, i, 0)),
            flat,
        ),
        compiler_params=params,
        cost_estimate=cost(
            16 * seq_len * text * LANES, o_img, m_img, l_img, exps=2 * seq_len * text
        ),
        name="text_part",
    )(lengths, qkv, ctx, in_hbm(o_img), in_hbm(m_img), in_hbm(l_img))


def project_kernel(idx_ref, o_ref, target_hbm, *refs):
    counts = len(refs) - 5
    out_ref, a_ref, target_ref, buf_ref, sems = refs[counts:]
    block_rows = a_ref.shape[2]
    copies = []
    for ref in refs[:counts]:
        for n in range(ref.shape[0] // block_rows):
            slot = len(copies)
            at = pl.ds(n * block_rows, block_rows)
            copies.append(pltpu.make_async_copy(ref.at[at], buf_ref.at[slot], sems.at[slot]))
    target_copy = pltpu.make_async_copy(target_hbm, target_ref, sems.at[len(copies)])
    for copy in (*copies, target_copy):
        copy.start()
    heads, tok = o_ref.shape[0], o_ref.shape[1]
    _, _, block_rows = a_ref.shape
    pairs = block_rows // LANES
    for pair in range(heads // 2):
        a, b = o_ref[2 * pair], o_ref[2 * pair + 1]
        at = slice((pair % pairs) * LANES, (pair % pairs + 1) * LANES)
        a_ref[pair // pairs, :tok, at] = jnp.concatenate([a[:, :HEAD], b[:, :HEAD]], axis=1)
        a_ref[pair // pairs, tok:, at] = jnp.concatenate([a[:, HEAD:], b[:, HEAD:]], axis=1)
    pred = None
    for slot, copy in enumerate(copies):
        copy.wait()
        term = dot(a_ref[idx_ref[slot]], buf_ref[slot])
        pred = term if pred is None else pred + term
    target_copy.wait()
    target = target_ref[...].reshape(2 * tok, -1).astype(f32)
    residual = pred - target
    grad = residual.astype(bf16)
    for slot in range(len(copies)):
        g = dot_nt(grad, buf_ref[slot]).astype(bf16)
        head = idx_ref[slot] * (2 * pairs)
        for pair in range(pairs):
            a = g[:tok, pair * LANES : (pair + 1) * LANES]
            b = g[tok:, pair * LANES : (pair + 1) * LANES]
            out_ref[head + 2 * pair, :tok] = jnp.concatenate([a[:, :HEAD], b[:, :HEAD]], axis=1)
            out_ref[head + 2 * pair + 1, :tok] = jnp.concatenate(
                [a[:, HEAD:], b[:, HEAD:]], axis=1
            )
    squares = residual * residual
    parts = []
    for stream in range(2):
        part = squares[stream * tok : (stream + 1) * tok]
        rest = jnp.sum(jnp.sum(part, axis=0, keepdims=True), axis=1, keepdims=True)
        rest = jnp.broadcast_to(rest, (1, LANES))
        for _ in range(PARTS):
            piece = rest.astype(bf16).astype(f32)
            parts.append(piece)
            rest = rest - piece
    row = lax.broadcasted_iota(jnp.int32, (EXTRA, LANES), 0)
    tail = jnp.zeros((EXTRA, LANES), f32)
    for n, piece in enumerate(parts):
        tail = jnp.where(row == n, piece, tail)
    tail = tail.astype(bf16)
    for head in range(heads):
        out_ref[head, tok:] = tail


def project(idx, attended, target, weights):
    S, tok, _ = attended.shape
    blocks = idx.shape[0]
    block_rows = sum(w.shape[0] for w in weights) // blocks
    return pl.pallas_call(
        project_kernel,
        out_shape=jax.ShapeDtypeStruct((S, tok + EXTRA, LANES), bf16),
        in_specs=[smem(), vmem()] + [hbm()] * (1 + len(weights)),
        out_specs=vmem(),
        scratch_shapes=[
            pltpu.VMEM((blocks, 2 * tok, block_rows), bf16),
            pltpu.VMEM(target.shape, bf16),
            pltpu.VMEM((blocks, block_rows, target.shape[-1]), bf16),
            pltpu.SemaphoreType.DMA((blocks + 1,)),
        ],
        compiler_params=params,
        cost_estimate=cost(8 * attended.size // S * S * target.shape[-1], *weights),
        name="project",
    )(idx, attended, in_hbm(target), *[in_hbm(w) for w in weights])


def dpo_terms(err_ref, step_ref, ref_ref, count):
    parts = jnp.sum(err_ref[...].astype(f32), axis=0)
    totals = [
        jnp.sum(parts[n * PARTS : (n + 1) * PARTS], axis=0, keepdims=True) for n in range(2)
    ]
    errors = jnp.concatenate(totals, axis=0) / count
    step_index = jnp.full((1, LANES), step_ref[0], jnp.int32)
    sigma_t = noise_level(step_index)
    gap = (errors[0:1] - ref_ref[0, 0]) - (errors[1:2] - ref_ref[0, 1])
    logit = dpo_beta * sigma_t * gap
    small = jnp.exp(-jnp.abs(logit))
    loss = jnp.maximum(logit, 0.0) + jnp.log1p(small)
    return loss, sigma_t * jnp.where(logit >= 0, 1.0, small) / (1.0 + small)


def backward_kernel(
    count, err_ref, step_ref, ref_ref, q_ref, k_ref, v_ref, ctx_ref, e_ref, p_ref, c_ref, o_ref, g_ref,
    loss_ref, dq_ref, dk_ref, dv_ref, ka_ref, va_ref,
):
    step = pl.program_id(0)
    loss, weight = dpo_terms(err_ref, step_ref, ref_ref, count)
    coefs = (weight[:, :1], -weight[:, :1])
    q, k, v = rows_of(q_ref), rows_of(k_ref), rows_of(v_ref)
    o, g = rows_of(o_ref), g_ref[:, : o_ref.shape[1], :].reshape(-1, LANES)
    ctx = ctx_ref[...]
    keys, values = ctx[:, :HEAD], ctx[:, HEAD:]
    products = g.astype(f32) * o.astype(f32)

    @pl.when(step == 0)
    def _():
        loss_ref[...] = loss
        ka_ref[...] = jnp.zeros_like(ka_ref)
        va_ref[...] = jnp.zeros_like(va_ref)

    dqs = []
    for stream in range(2):
        at = lanes_of(stream)
        gs = g[:, at]
        delta = jnp.sum(products[:, at], axis=-1, keepdims=True)
        scale = c_ref[:, stream * HEAD : stream * HEAD + 1]
        e = e_ref[stream]
        probs = p_ref[stream]
        grad_image = dot_nt(gs, v[:, at])
        grad_text = dot_nt(gs, values)
        ds_image = (e.astype(f32) * ((grad_image - delta) * scale)).astype(bf16)
        ds_text = (probs.astype(f32) * (grad_text - delta)).astype(bf16)
        coef = coefs[stream]
        dq = dot(ds_image, k[:, at]) + dot(ds_text, keys)
        dqs.append(dq * (coef * inv_root))
        ka_ref[stream] += dot_tn(q[:, at], ds_image)
        va_ref[stream] += dot_tn((gs.astype(f32) * scale).astype(bf16), e)
    both = jnp.concatenate(dqs, axis=1).T.astype(bf16)
    dq_ref[0] = both[:HEAD]
    dq_ref[1] = both[HEAD:]

    @pl.when(step == pl.num_programs(0) - 1)
    def _():
        for stream in range(2):
            coef = coefs[stream]
            dk_ref[stream] = (ka_ref[stream] * (coef * inv_root)).astype(bf16)
            dv_ref[stream] = (va_ref[stream] * coef).astype(bf16)


def backward_part(count, steps_in, refs_in, qkv, ctx, e, probs, scale, attended, grads):
    S, _, tok, _ = qkv.shape
    group, steps, rows = q_blocks(S, tok)
    seq_len = S * tok
    text = ctx.shape[0]
    whole = lambda n: pl.BlockSpec((S, None, tok, LANES), lambda i: (0, n, 0, 0))
    block = pl.BlockSpec((group, tok, LANES), lambda i: (i, 0, 0))
    full = pl.BlockSpec((None, 2, HEAD, seq_len), lambda i: (0, 0, 0, 0))
    out = jax.ShapeDtypeStruct((1, 2, HEAD, seq_len), bf16)
    return pl.pallas_call(
        functools.partial(backward_kernel, count),
        grid=(steps,),
        out_shape=(jax.ShapeDtypeStruct((1, LANES), f32), out, out, out),
        in_specs=[
            pl.BlockSpec((S, EXTRA, LANES), lambda i: (0, tok // EXTRA, 0)),
            smem(),
            smem(),
            pl.BlockSpec((group, None, tok, LANES), lambda i: (i, 0, 0, 0)),
            whole(1),
            whole(2),
            pl.BlockSpec((text, LANES), lambda i: (0, 0)),
            pl.BlockSpec((2, rows, seq_len), lambda i: (0, i, 0)),
            pl.BlockSpec((2, rows, text), lambda i: (0, i, 0)),
            pl.BlockSpec((rows, LANES), lambda i: (i, 0)),
            block,
            pl.BlockSpec((group, tok + EXTRA, LANES), lambda i: (i, 0, 0)),
        ],
        out_specs=(
            pl.BlockSpec((1, LANES), lambda i: (0, 0)),
            pl.BlockSpec((None, 2, HEAD, rows), lambda i: (0, 0, 0, i)),
            full,
            full,
        ),
        scratch_shapes=[pltpu.VMEM((2, HEAD, seq_len), f32)] * 2,
        compiler_params=params,
        cost_estimate=cost(40 * seq_len * seq_len * LANES, e, probs, qkv),
        name="backward_part",
    )(
        grads, steps_in, refs_in, qkv, qkv, qkv, ctx, in_hbm(e), in_hbm(probs), in_hbm(scale),
        attended, grads,
    )


def on_device(
    S, F, prompt, lengths, timesteps, ref_errors, gain_ffn, w_in_gate, w_in_up, w_in_down,
    gain_final, w_context, image_q, image_k, image_v, w_out, target,
):
    tok = image_q.shape[2]
    seq_len = S * tok
    if F == 2 and w_in_down.shape[1] == S * LANES:
        ctx, qkv, image, weights, w_idx = encode_shared(
            S, prompt, lengths, gain_ffn, w_in_gate, w_in_up, w_in_down, gain_final, w_context,
            w_out, (image_q[0], image_k[0], image_v[0]),
        )
    else:
        qkv = exchange(pack_heads(image_q[0], image_k[0], image_v[0])).reshape(S, 3, tok, LANES)
        ctx = encode_gathered(
            prompt, gain_ffn, w_in_gate, w_in_up, w_in_down, gain_final, w_context
        )
        image = image_part(qkv)
        weights = (lax.all_gather(w_out, "fsdp", axis=0, tiled=True),)
        w_idx = jnp.arange(F, dtype=jnp.int32)
    e_img, o_img, m_img, l_img = image

    attended, probs, scale = text_part(lengths, qkv, ctx, o_img, m_img, l_img)
    tokens = exchange(attended)
    grads = exchange(project(w_idx, tokens, target[0], weights))
    loss, grad_q, grad_k, grad_v = backward_part(
        seq_len * target.shape[-1], timesteps, ref_errors, qkv, ctx, e_img, probs, scale, attended,
        grads,
    )
    turn = lambda x: jnp.swapaxes(x, 2, 3)
    return loss[0, :1], turn(grad_q), turn(grad_k), turn(grad_v)


def solution(mesh):
    S, F = mesh.shape["seq"], mesh.shape["fsdp"]

    def body(*args):
        return on_device(S, F, *args)

    return jax.shard_map(
        body,
        mesh=mesh,
        in_specs=(
            P("fsdp", None, None),
            P("fsdp"),
            P("fsdp"),
            P("fsdp", None),
            P(),
            P("fsdp", "seq"),
            P("fsdp", "seq"),
            P("seq", "fsdp"),
            P(),
            P("fsdp", "seq"),
            P("fsdp", None, "seq", None),
            P("fsdp", None, "seq", None),
            P("fsdp", None, "seq", None),
            P("fsdp", None),
            P("fsdp", None, "seq", None),
        ),
        out_specs=(
            P("fsdp"),
            P("fsdp", None, None, "seq"),
            P("fsdp", None, None, "seq"),
            P("fsdp", None, None, "seq"),
        ),
        check_vma=False,
    )
```

time: 205 us -> 162 us (0.79)
  local copies, waits for them, and re-layouts: 23.6 us -> 3.61 us
  waiting for transfers between devices: 85.5 us -> 67 us
  Pallas kernels: 29.2 us -> 46.1 us
  matrix products: 10 us -> 2.99 us
  other arithmetic: 7.6 us -> 2.56 us
  starting transfers between devices: 40.4 us -> 35.6 us
  between operations: 6.99 us -> 3.01 us
    ppermute x21 -> x18, waiting for transfers between devices: 75.6 us -> 46.4 us  [swap(): return lax.ppermute(x, axis, [(i, i ^ mask) for i in range(size)])]
    unnamed x68 -> x30, local copies, waits for them, and re-layouts: 17.8 us -> 1.93 us
    pallas_call x5 -> x9, Pallas kernels: 27.6 us -> 43 us  [the longest x1 8.86 us: backward_part(): pl.pallas_call(functools.partial(backward_kernel, count), grid=(steps,),...]
    all_to_all x3, waiting for transfers between devices: 9.93 us -> 20.6 us  [exchange(): return lax.all_to_all(x, 'seq', split_axis=0, concat_axis=0, tiled=True)]
    dot_general x8 -> x1, matrix products: 9.65 us -> 2.67 us  [dot(): return jnp.dot(a, b, preferred_element_type=f32)]
    ppermute x21 -> x18, starting transfers between devices: 24.3 us -> 19.4 us  [swap(): return lax.ppermute(x, axis, [(i, i ^ mask) for i in range(size)])]
    dynamic_slice x5 -> x0, local copies, waits for them, and re-layouts: 4.42 us -> none  [the longest x1 1.9 us: encode_shared(): away = lax.dynamic_slice(own, (core * half, (1 - f) * cols), (half, cols))]
    reduce_sum x1 -> x0, other arithmetic: 2.23 us -> none  [encode_shared(): scale = lax.rsqrt(jnp.mean(own_f32 * own_f32, axis=-1) + norm_eps)]
  transfers between devices with their start and end apart: 24 -> 21, of which waited for: 14 -> 17; matrix products, arithmetic and copies ran while one was open for 9% -> 4% of each run, Pallas kernels for 7% -> 11%
where the time goes in v2:
time: 162 us; the launch traced here: 161 us
  waiting for transfers between devices  67 us (41%)
  Pallas kernels  46.1 us (28%)
  starting transfers between devices  35.6 us (22%)
  local copies, waits for them, and re-layouts  3.61 us (2%)
  between operations  3.01 us (2%)
  matrix products  2.99 us (2%)
  other arithmetic  2.56 us (2%)
    ppermute x18, waiting for transfers between devices, swap(): return lax.ppermute(x, axis, [(i, i ^ mask) for i in range(size)])  46.4 us
    all_to_all x3, waiting for transfers between devices, exchange(): return lax.all_to_all(x, 'seq', split_axis=0, concat_axis=0, tiled=True)  20.6 us
    ppermute x18, starting transfers between devices, swap(): return lax.ppermute(x, axis, [(i, i ^ mask) for i in range(size)])  19.4 us
    all_to_all x3, starting transfers between devices, exchange(): return lax.all_to_all(x, 'seq', split_axis=0, concat_axis=0, tiled=True)  16.2 us
    pallas_call x1, Pallas kernels, backward_part(): pl.pallas_call(functools.partial(backward_kernel, count), grid=(steps,),...  8.86 us
    pallas_call x1, Pallas kernels, gate_up_own(): pl.pallas_call(gate_up_own_kernel, out_shape=(pltpu.HBM((rows, 2 * w_gate...  6.48 us
    pallas_call x1, Pallas kernels, text_part(): pl.pallas_call(text_kernel, grid=(steps,), out_shape=(pltpu.HBM((S, tok,...  6.48 us
    pallas_call x1, Pallas kernels, image_part(): pl.pallas_call(image_kernel, grid=(steps,), out_shape=(pltpu.HBM((2, seq_...  6.08 us
  transfers between devices with their start and end apart: 21, of which 17 were waited for; matrix products, arithmetic and copies ran while one was open for 4% of the time, Pallas kernels for 11%

profile of v2, /device:TPU:0, one launch (start us, length us, event | category | flops | bytes accessed | tf_op | source)
XLA Modules:
  0.0 160.9 jit_solution(13446830829465004249)
XLA Ops:
  0.6 0.1 pad_add_fusion.3.at_ref
  0.7 1.6 corner.2
  2.3 3.1 %collective-permute-start = (bf16[128,2048]{1,0:T(8,128)(2,1)S(1)}, bf16[128,2048]{1,0:T(8,128)(2,1)S(1)}, u32[]{:S(2)}, u32[]{:S(2)}) collective-permute-start(bf16[128,2048]{1,0:T(8,128)(2,1)S(1)} %corner.2), channel_id=1, source_target_pairs={{0,1},{1,0},{2,3},{3,2},{4,5},{5,4},{6,7},{7,6},{8,9},{9,8},{10,11... | collective-permute-start | bytes 1572872 | tf_op jit(solution)/shard_map/ppermute | solution.py:43
  5.4 0.1 pad_add_fusion.2.at_ref
  5.5 6.5 %gate_up_own.1 = (bf16[256,1024]{1,0:T(8,128)(2,1)}, f32[1,256]{1,0:T(1,128)S(1)}, bf16[256,2048]{1,0:T(8,128)(2,1)}) custom-call(s32[2]{0:T(128)S(1)} %pad_add_fusion.2.at_ref, bf16[256,4096]{1,0:T(8,128)(2,1)} %bitcast.39, f32[1,4096]{1,0:T(1,128)S(1)} %bitcast.35, bf16[2048,512]{1,0:T(8,128)(2,1)} %wg_ref.3, bf16[2048,512]{1,0:T(8,128)(2,1)} %wu_ref.3), custom_call_target="tpu_custom_call" | custom-call | flops 1073741824 | bytes 6291456 | tf_op jit(solution)/shard_map/gate_up_own/pallas_call | solution.py:239
  12.0 0.1 collective-permute-start.1
  12.0 2.0 %collective-permute-start.2 = (s32[1]{0:T(128)}, s32[1]{0:T(128)}, u32[]{:S(2)}, u32[]{:S(2)}) collective-permute-start(s32[1]{0:T(128)} %param.17), channel_id=1, source_target_pairs={{0,1},{1,0},{2,3},{3,2},{4,5},{5,4},{6,7},{7,6},{8,9},{9,8},{10,11... | collective-permute-start | bytes 20 | tf_op jit(solution)/shard_map/ppermute | solution.py:43
  14.8 2.6 %collective-permute-done.2 = s32[1]{0:T(128)} collective-permute-done((s32[1]{0:T(128)}, s32[1]{0:T(128)}, u32[]{:S(2)}, u32[]{:S(2)}) %collective-permute-start.2) | collective-permute-done | bytes 36 | tf_op jit(solution)/shard_map/ppermute | solution.py:43
  18.1 0.7 add_select_fusion
  18.8 0.1 fusion.5.select_ref
  18.9 0.0 copy-start.14
  18.9 0.1 collective-permute-start.3
  19.0 1.9 %collective-permute-done.3.b_ref = bf16[128,2048]{1,0:T(8,128)(2,1)S(1)} collective-permute-done((bf16[128,2048]{1,0:T(8,128)(2,1)S(1)}, bf16[128,2048]{1,0:T(8,128)(2,1)S(1)}, u32[]{:S(2)}, u32[]{:S(2)}) %collective-permute-start.3) | collective-permute-done | bytes 524320 | tf_op jit(solution)/shard_map/ppermute | solution.py:43
  20.9 4.7 %gate_up_other.1.mine_ref = bf16[384,1024]{1,0:T(8,128)(2,1)S(1)} custom-call(s32[2]{0:T(128)S(1)} %pad_add_fusion.2.at_ref, bf16[128,2048]{1,0:T(8,128)(2,1)} %copy-done.13, bf16[128,2048]{1,0:T(8,128)(2,1)S(1)} %collective-permute-done.3.b_ref, f32[1,256]{1,0:T(1,128)S(1)} %collective-permute-done.1.scale_ref, f32[1,4096]{1,0:T(1,128)S(1)} %bitcast.36, ...), custom_call_target="tpu_custom_call" | custom-call | flops 1610612736 | bytes 6291456 | tf_op jit(solution)/shard_map/gate_up_other/pallas_call | solution.py:291
  25.6 0.0 copy-start.6
  25.6 1.8 %collective-permute-start.4 = (bf16[384,1024]{1,0:T(8,128)(2,1)S(1)}, bf16[384,1024]{1,0:T(8,128)(2,1)}, u32[]{:S(2)}, u32[]{:S(2)}) collective-permute-start(bf16[384,1024]{1,0:T(8,128)(2,1)S(1)} %gate_up_other.1.mine_ref), channel_id=1, source_target_pairs={{0,1},{1,0},{2,3},{3,2},{4,5},{5,4},{6,7},{7,6},{8,9},{9,8},{10,11... | collective-permute-start | bytes 2359304 | tf_op jit(solution)/shard_map/ppermute | solution.py:43
  27.4 0.1 pad_add_fusion.4.at_ref
  27.5 1.6 %corner.3 = bf16[256,1280]{1,0:T(8,128)(2,1)S(1)} custom-call(s32[2]{0:T(128)S(1)} %pad_add_fusion.4.at_ref, bf16[512,1280]{1,0:T(8,128)(2,1)} %refs_0_.1), custom_call_target="tpu_custom_call" | custom-call | bytes 1310720 | tf_op jit(solution)/shard_map/corner/pallas_call | solution.py:175
  29.2 0.8 copy-done.1
  30.0 1.1 pack_heads.1
  31.2 5.9 %all-to-all-start = ((bf16[16,192,128]{2,1,0:T(8,128)(2,1)}), bf16[16,192,128]{2,1,0:T(8,128)(2,1)S(1)}, u32[]{:S(2)}, u32[]{:S(2)}) async-start(bf16[16,192,128]{2,1,0:T(8,128)(2,1)} %pack_heads.1), calls=%async_computation | async-start | bytes 1572864 | tf_op jit(solution)/shard_map/all_to_all | solution.py:74
  37.1 2.7 %convolution_convert_fusion.pp_ref = bf16[384,2048]{1,0:T(8,128)(2,1)S(1)} fusion(bf16[384,512]{1,0:T(8,128)(2,1)S(1)} %fusion.5.select_ref, bf16[128,2048]{1,0:T(8,128)(2,1)} %copy-done.3, bf16[128,2048]{1,0:T(8,128)(2,1)} %copy-done.13, bf16[256,2048]{1,0:T(8,128)(2,1)} %get-tuple-element.59), kind=kOutput, calls=%fused_computation | convolution fusion | flops 812384256 | bytes 4063232 | tf_op jit(solution)/shard_map/dot_general | solution.py:31
  39.8 5.6 %collective-permute-done.4.got_ref = bf16[384,1024]{1,0:T(8,128)(2,1)} collective-permute-done((bf16[384,1024]{1,0:T(8,128)(2,1)S(1)}, bf16[384,1024]{1,0:T(8,128)(2,1)}, u32[]{:S(2)}, u32[]{:S(2)}) %collective-permute-start.4) | collective-permute-done | bytes 786464 | tf_op jit(solution)/shard_map/ppermute | solution.py:43
  45.4 2.8 %down_product.1 = bf16[16,384,128]{2,1,0:T(8,128)(2,1)S(1)} custom-call(s32[16]{0:T(128)S(1)} %broadcast_xor_fusion.idx_ref, bf16[384,1024]{1,0:T(8,128)(2,1)S(1)} %gate_up_other.1.mine_ref, bf16[384,1024]{1,0:T(8,128)(2,1)} %collective-permute-done.4.got_ref, bf16[512,2048]{1,0:T(8,128)(2,1)S(1)} %copy-done), custom_call_target="tpu_custom_call" | custom-call | flops 805306368 | bytes 3670016 | tf_op jit(solution)/shard_map/down_product/pallas_call | solution.py:114
  48.2 0.1 slice.41
  48.2 0.1 collective-permute-start.5
  48.3 2.3 %collective-permute-done.5 = bf16[8,384,128]{2,1,0:T(8,128)(2,1)S(1)} collective-permute-done((bf16[8,384,128]{2,1,0:T(8,128)(2,1)S(1)}, bf16[8,384,128]{2,1,0:T(8,128)(2,1)S(1)}, u32[]{:S(2)}, u32[]{:S(2)}) %collective-permute-start.5) | collective-permute-done | bytes 786464 | tf_op jit(solution)/shard_map/ppermute | solution.py:43
  50.6 0.2 add_convert_fusion
  50.8 0.9 slice.42
  51.7 1.7 %collective-permute-start.6 = (bf16[4,384,128]{2,1,0:T(8,128)(2,1)}, bf16[4,384,128]{2,1,0:T(8,128)(2,1)}, u32[]{:S(2)}, u32[]{:S(2)}) collective-permute-start(bf16[4,384,128]{2,1,0:T(8,128)(2,1)} %slice.42), channel_id=1, source_target_pairs={{0,4},{2,6},{4,0},{6,2},{8,12},{10,14},{12,8},{14,10},{16,20},{18,... | collective-permute-start | bytes 1179656 | tf_op jit(solution)/shard_map/ppermute | solution.py:43
  53.4 1.5 collective-permute-start.8
  55.0 0.8 all-to-all-done
  55.8 6.1 %image_part.1 = (bf16[2,1024,1024]{2,1,0:T(8,128)(2,1)}, f32[1024,128]{1,0:T(8,128)}, f32[1024,128]{1,0:T(8,128)}, f32[1024,128]{1,0:T(8,128)}) custom-call(bf16[16,3,64,128]{3,2,1,0:T(8,128)(2,1)S(1)} %bitcast.25, bf16[16,3,64,128]{3,2,1,0:T(8,128)(2,1)S(1)} %bitcast.26, bf16[16,3,64,128]{3,2,1,0:T(8,128)(2,1)S(1)} %bitcast.27), custom_call_target="tpu_custom_call" | custom-call | flops 2147483648 | bytes 786432 | tf_op jit(solution)/shard_map/image_part/pallas_call | solution.py:463
  61.8 2.5 %collective-permute-done.6 = bf16[4,384,128]{2,1,0:T(8,128)(2,1)} collective-permute-done((bf16[4,384,128]{2,1,0:T(8,128)(2,1)}, bf16[4,384,128]{2,1,0:T(8,128)(2,1)}, u32[]{:S(2)}, u32[]{:S(2)}) %collective-permute-start.6) | collective-permute-done | bytes 393248 | tf_op jit(solution)/shard_map/ppermute | solution.py:43
  64.4 1.1 add_convert_fusion.1
  65.5 1.7 %collective-permute-start.7 = (bf16[2,384,128]{2,1,0:T(8,128)(2,1)S(1)}, bf16[2,384,128]{2,1,0:T(8,128)(2,1)S(1)}, u32[]{:S(2)}, u32[]{:S(2)}) collective-permute-start(bf16[2,384,128]{2,1,0:T(8,128)(2,1)S(1)} %slice.44), channel_id=1, source_target_pairs={{0,8},{2,10},{4,12},{6,14},{8,0},{10,2},{12,4},{14,6},{16,24},{18,... | collective-permute-start | bytes 589832 | tf_op jit(solution)/shard_map/ppermute | solution.py:43
  67.2 2.8 %collective-permute-done.8.refs_1_ = bf16[256,1280]{1,0:T(8,128)(2,1)} collective-permute-done((bf16[256,1280]{1,0:T(8,128)(2,1)S(1)}, bf16[256,1280]{1,0:T(8,128)(2,1)}, u32[]{:S(2)}, u32[]{:S(2)}) %collective-permute-start.8) | collective-permute-done | bytes 655392 | tf_op jit(solution)/shard_map/ppermute | solution.py:43
  70.0 2.3 %collective-permute-done.7 = bf16[2,384,128]{2,1,0:T(8,128)(2,1)S(1)} collective-permute-done((bf16[2,384,128]{2,1,0:T(8,128)(2,1)S(1)}, bf16[2,384,128]{2,1,0:T(8,128)(2,1)S(1)}, u32[]{:S(2)}, u32[]{:S(2)}) %collective-permute-start.7) | collective-permute-done | bytes 196640 | tf_op jit(solution)/shard_map/ppermute | solution.py:43
  72.3 0.1 add_convert_fusion.2
  72.4 2.3 %collective-permute-start.9 = (bf16[1,384,128]{2,1,0:T(8,128)(2,1)S(1)}, bf16[1,384,128]{2,1,0:T(8,128)(2,1)S(1)}, u32[]{:S(2)}, u32[]{:S(2)}) collective-permute-start(bf16[1,384,128]{2,1,0:T(8,128)(2,1)S(1)} %slice.46), channel_id=1, source_target_pairs={{0,16},{2,18},{4,20},{6,22},{8,24},{10,26},{12,28},{14,30},{16,0},... | collective-permute-start | bytes 294920 | tf_op jit(solution)/shard_map/ppermute | solution.py:43
  74.7 4.5 %collective-permute-done.9 = bf16[1,384,128]{2,1,0:T(8,128)(2,1)S(1)} collective-permute-done((bf16[1,384,128]{2,1,0:T(8,128)(2,1)S(1)}, bf16[1,384,128]{2,1,0:T(8,128)(2,1)S(1)}, u32[]{:S(2)}, u32[]{:S(2)}) %collective-permute-start.9) | collective-permute-done | bytes 98336 | tf_op jit(solution)/shard_map/ppermute | solution.py:43
  79.3 1.2 collective-permute-start.10
  80.4 5.1 %collective-permute-done.10 = bf16[1,384,128]{2,1,0:T(8,128)(2,1)S(1)} collective-permute-done((bf16[1,384,128]{2,1,0:T(8,128)(2,1)S(1)}, bf16[1,384,128]{2,1,0:T(8,128)(2,1)S(1)}, u32[]{:S(2)}, u32[]{:S(2)}) %collective-permute-start.10) | collective-permute-done | bytes 98336 | tf_op jit(solution)/shard_map/ppermute | solution.py:43
  85.6 0.1 collective-permute-start.11
  85.6 5.7 %collective-permute-done.11 = bf16[2,384,128]{2,1,0:T(8,128)(2,1)S(1)} collective-permute-done((bf16[2,384,128]{2,1,0:T(8,128)(2,1)S(1)}, bf16[2,384,128]{2,1,0:T(8,128)(2,1)S(1)}, u32[]{:S(2)}, u32[]{:S(2)}) %collective-permute-start.11) | collective-permute-done | bytes 196640 | tf_op jit(solution)/shard_map/ppermute | solution.py:43
  91.3 1.7 %collective-permute-start.13 = (bf16[4,384,128]{2,1,0:T(8,128)(2,1)S(1)}, bf16[4,384,128]{2,1,0:T(8,128)(2,1)S(1)}, u32[]{:S(2)}, u32[]{:S(2)}) collective-permute-start(bf16[4,384,128]{2,1,0:T(8,128)(2,1)S(1)} %pad_maximum_fusion.refs_0_), channel_id=1, source_target_pairs={{0,4},{2,6},{4,0},{6,2},{8,12},{10,14},{12,8},{14,10},{16,20},{18,... | collective-permute-start | bytes 1179656 | tf_op jit(solution)/shard_map/ppermute | solution.py:43
  93.1 6.1 %collective-permute-done.13.refs_1_ = bf16[4,384,128]{2,1,0:T(8,128)(2,1)S(1)} collective-permute-done((bf16[4,384,128]{2,1,0:T(8,128)(2,1)S(1)}, bf16[4,384,128]{2,1,0:T(8,128)(2,1)S(1)}, u32[]{:S(2)}, u32[]{:S(2)}) %collective-permute-start.13) | collective-permute-done | bytes 393248 | tf_op jit(solution)/shard_map/ppermute | solution.py:43
  99.2 0.7 dynamic_slice.3
  99.9 1.1 collective-permute-done.15.refs_3_
  101.0 1.0 copy-done.4
  102.1 2.0 %context_product.1 = (bf16[384,128]{1,0:T(8,128)(2,1)S(1)}, f32[1,384]{1,0:T(1,128)S(1)}) custom-call(s32[16]{0:T(128)S(1)} %broadcast_xor_fusion.idx_ref, bf16[384,2048]{1,0:T(8,128)(2,1)S(1)} %convolution_convert_fusion.pp_ref, f32[1,2048]{1,0:T(1,128)S(1)} %bitcast.37, bf16[2048,128]{1,0:T(8,128)(2,1)S(1)} %copy-done.4, ...), custom_call_target="tpu_custom_call" | custom-call | flops 402653184 | bytes 3670016 | tf_op jit(solution)/shard_map/context_product/pallas_call | solution.py:146
  104.0 1.3 collective-permute-start.17
  105.4 0.7 collective-permute-start.16
  106.1 1.6 collective-permute-done.17
  107.7 2.3 %collective-permute-done.16 = bf16[384,128]{1,0:T(8,128)(2,1)S(1)} collective-permute-done((bf16[384,128]{1,0:T(8,128)(2,1)S(1)}, bf16[384,128]{1,0:T(8,128)(2,1)S(1)}, u32[]{:S(2)}, u32[]{:S(2)}) %collective-permute-start.16) | collective-permute-done | bytes 98336 | tf_op jit(solution)/shard_map/ppermute | solution.py:43
  110.0 0.3 convolution_convert_fusion.1.ctx_ref
  110.3 6.5 %text_part.1 = (bf16[16,64,128]{2,1,0:T(8,128)(2,1)}, bf16[2,1024,256]{2,1,0:T(8,128)(2,1)}, f32[1024,128]{1,0:T(8,128)}) custom-call(s32[1]{0:T(128)} %copy.20.len_ref, bf16[16,3,64,128]{3,2,1,0:T(8,128)(2,1)S(1)} %bitcast.28, bf16[256,128]{1,0:T(8,128)(2,1)S(1)} %convolution_convert_fusion.1.ctx_ref, f32[1024,128]{1,0:T(8,128)} %get-tuple-element.80.o_ref, ...), custom_call_target="tpu_custom_call" | custom-call | flops 536870912 | bytes 1572864 | tf_op jit(solution)/shard_map/text_part/pallas_call | solution.py:512
  116.8 6.7 %all-to-all-start.1 = ((bf16[16,64,128]{2,1,0:T(8,128)(2,1)}), bf16[16,64,128]{2,1,0:T(8,128)(2,1)S(1)}, u32[]{:S(2)}, u32[]{:S(2)}) async-start(bf16[16,64,128]{2,1,0:T(8,128)(2,1)} %get-tuple-element.83.o_ref), calls=%async_computation.1 | async-start | bytes 524288 | tf_op jit(solution)/shard_map/all_to_all | solution.py:74
  123.5 0.1 pad_add_fusion.1.idx_ref
  123.6 9.9 %all-to-all-done.1.o_ref = bf16[16,64,128]{2,1,0:T(8,128)(2,1)S(1)} async-done(((bf16[16,64,128]{2,1,0:T(8,128)(2,1)}), bf16[16,64,128]{2,1,0:T(8,128)(2,1)S(1)}, u32[]{:S(2)}, u32[]{:S(2)}) %all-to-all-start.1) | async-done | bytes 262176 | tf_op jit(solution)/shard_map/all_to_all | solution.py:74
  133.5 4.4 %project.1 = bf16[16,72,128]{2,1,0:T(8,128)(2,1)} custom-call(s32[4]{0:T(128)S(1)} %pad_add_fusion.1.idx_ref, bf16[16,64,128]{2,1,0:T(8,128)(2,1)S(1)} %all-to-all-done.1.o_ref, bf16[2,64,1280]{2,1,0:T(8,128)(2,1)} %bitcast.40, bf16[512,1280]{1,0:T(8,128)(2,1)} %refs_0_.1, bf16[256,1280]{1,0:T(8,128)(2,1)} %collective-permute-done.8.refs_1_, ...), custom_call_target="tpu_custom_call" | custom-call | flops 1342177280 | bytes 2621440 | tf_op jit(solution)/shard_map/project/pallas_call | solution.py:604
  137.9 3.5 %all-to-all-start.2 = ((bf16[16,72,128]{2,1,0:T(8,128)(2,1)}), bf16[16,72,128]{2,1,0:T(8,128)(2,1)S(1)}, u32[]{:S(2)}, u32[]{:S(2)}) async-start(bf16[16,72,128]{2,1,0:T(8,128)(2,1)} %project.1), calls=%async_computation.2 | async-start | bytes 589824 | tf_op jit(solution)/shard_map/all_to_all | solution.py:74
  142.1 9.9 %all-to-all-done.2.err_ref.g_ref = bf16[16,72,128]{2,1,0:T(8,128)(2,1)S(1)} async-done(((bf16[16,72,128]{2,1,0:T(8,128)(2,1)}), bf16[16,72,128]{2,1,0:T(8,128)(2,1)S(1)}, u32[]{:S(2)}, u32[]{:S(2)}) %all-to-all-start.2) | async-done | bytes 294944 | tf_op jit(solution)/shard_map/all_to_all | solution.py:74
  152.0 8.9 %backward_part.1 = (f32[1,128]{1,0:T(1,128)}, bf16[1,2,64,1024]{3,2,1,0:T(8,128)(2,1)}, bf16[1,2,64,1024]{3,2,1,0:T(8,128)(2,1)}, bf16[1,2,64,1024]{3,2,1,0:T(8,128)(2,1)}) custom-call(bf16[16,72,128]{2,1,0:T(8,128)(2,1)S(1)} %all-to-all-done.2.err_ref.g_ref, s32[1]{0:T(128)S(6)} %copy.21.step_ref, f32[1,2]{1,0:T(1,128)S(1)} %copy-done.10, ...), custom_call_target="tpu_custom_call" | custom-call | flops 5368709120 | bytes 6029312 | tf_op jit(solution)/shard_map/backward_part/pallas_call | solution.py:693
  (43 shorter events, 0.2 us)
Async XLA Ops:
  0.6 4.8 %copy-start.9 = (f32[4096]{0:T(1024)S(1)}, f32[4096]{0:T(1024)}, u32[]{:S(2)}) copy-start(f32[4096]{0:T(1024)} %param.20) | copy-start | bytes 49156
  2.3 16.5 %collective-permute-start = (bf16[128,2048]{1,0:T(8,128)(2,1)S(1)}, bf16[128,2048]{1,0:T(8,128)(2,1)S(1)}, u32[]{:S(2)}, u32[]{:S(2)}) collective-permute-start(bf16[128,2048]{1,0:T(8,128)(2,1)S(1)} %corner.2), channel_id=1, source_target_pairs={{0,1},{1,0},{2,3},{3,2},{4,5},{5,4},{6,7},{7,6},{8,9},{9,8},{10,11... | collective-permute-start | bytes 1572872 | tf_op jit(solution)/shard_map/ppermute | solution.py:43
  12.0 6.9 %collective-permute-start.1 = (f32[1,256]{1,0:T(1,128)S(1)}, f32[1,256]{1,0:T(1,128)S(1)}, u32[]{:S(2)}, u32[]{:S(2)}) collective-permute-start(f32[1,256]{1,0:T(1,128)S(1)} %get-tuple-element.50), channel_id=1, source_target_pairs={{0,1},{1,0},{2,3},{3,2},{4,5},{5,4},{6,7},{7,6},{8,9},{9,8},{10,11... | collective-permute-start | bytes 3080 | tf_op jit(solution)/shard_map/ppermute | solution.py:43
  12.0 5.3 %collective-permute-start.2 = (s32[1]{0:T(128)}, s32[1]{0:T(128)}, u32[]{:S(2)}, u32[]{:S(2)}) collective-permute-start(s32[1]{0:T(128)} %param.17), channel_id=1, source_target_pairs={{0,1},{1,0},{2,3},{3,2},{4,5},{5,4},{6,7},{7,6},{8,9},{9,8},{10,11... | collective-permute-start | bytes 20 | tf_op jit(solution)/shard_map/ppermute | solution.py:43
  18.9 2.0 %copy-start.13 = (bf16[128,2048]{1,0:T(8,128)(2,1)}, bf16[128,2048]{1,0:T(8,128)(2,1)S(1)}, u32[]{:S(2)}) copy-start(bf16[128,2048]{1,0:T(8,128)(2,1)S(1)} %collective-permute-done.a_hbm) | copy-start | bytes 1572868
  18.9 11.1 %copy-start.14 = (s32[16]{0:T(128)S(1)}, s32[16]{0:T(128)}, u32[]{:S(2)}) copy-start(s32[16]{0:T(128)} %constant.34.clone) | copy-start | bytes 196
  18.9 2.0 %collective-permute-start.3 = (bf16[128,2048]{1,0:T(8,128)(2,1)S(1)}, bf16[128,2048]{1,0:T(8,128)(2,1)S(1)}, u32[]{:S(2)}, u32[]{:S(2)}) collective-permute-start(bf16[128,2048]{1,0:T(8,128)(2,1)S(1)} %collective-permute-done.a_hbm), channel_id=1, source_target_pairs={{0,2},{2,0},{4,6},{6,4},{8,10},{10,8},{12,14},{14,12},{16,18},{18,... | collective-permute-start | bytes 1572872 | tf_op jit(solution)/shard_map/ppermute | solution.py:43
  20.9 4.7 %copy-start.3 = (bf16[128,2048]{1,0:T(8,128)(2,1)}, bf16[128,2048]{1,0:T(8,128)(2,1)S(1)}, u32[]{:S(2)}) copy-start(bf16[128,2048]{1,0:T(8,128)(2,1)S(1)} %collective-permute-done.3.b_ref) | copy-start | bytes 1572868
  25.6 4.4 %copy-start.6 = (bf16[1,2,64,1024]{3,2,1,0:T(8,128)(2,1)S(1)}, bf16[1,2,64,1024]{3,2,1,0:T(8,128)(2,1)}, u32[]{:S(2)}) copy-start(bf16[1,2,64,1024]{3,2,1,0:T(8,128)(2,1)} %param.26) | copy-start | bytes 786436
  25.6 4.4 %copy-start.7 = (bf16[1,2,64,1024]{3,2,1,0:T(8,128)(2,1)S(1)}, bf16[1,2,64,1024]{3,2,1,0:T(8,128)(2,1)}, u32[]{:S(2)}) copy-start(bf16[1,2,64,1024]{3,2,1,0:T(8,128)(2,1)} %param.27) | copy-start | bytes 786436
  25.6 4.4 %copy-start.8 = (bf16[1,2,64,1024]{3,2,1,0:T(8,128)(2,1)S(1)}, bf16[1,2,64,1024]{3,2,1,0:T(8,128)(2,1)}, u32[]{:S(2)}) copy-start(bf16[1,2,64,1024]{3,2,1,0:T(8,128)(2,1)} %param.28) | copy-start | bytes 786436
  25.6 19.8 %collective-permute-start.4 = (bf16[384,1024]{1,0:T(8,128)(2,1)S(1)}, bf16[384,1024]{1,0:T(8,128)(2,1)}, u32[]{:S(2)}, u32[]{:S(2)}) collective-permute-start(bf16[384,1024]{1,0:T(8,128)(2,1)S(1)} %gate_up_other.1.mine_ref), channel_id=1, source_target_pairs={{0,1},{1,0},{2,3},{3,2},{4,5},{5,4},{6,7},{7,6},{8,9},{9,8},{10,11... | collective-permute-start | bytes 2359304 | tf_op jit(solution)/shard_map/ppermute | solution.py:43
  29.2 0.8 copy-start.1
  31.2 24.6 %all-to-all-start = ((bf16[16,192,128]{2,1,0:T(8,128)(2,1)}), bf16[16,192,128]{2,1,0:T(8,128)(2,1)S(1)}, u32[]{:S(2)}, u32[]{:S(2)}) async-start(bf16[16,192,128]{2,1,0:T(8,128)(2,1)} %pack_heads.1), calls=%async_computation | async-start | bytes 1572864 | tf_op jit(solution)/shard_map/all_to_all | solution.py:74
  37.1 8.3 %copy-start = (bf16[512,2048]{1,0:T(8,128)(2,1)S(1)}, bf16[512,2048]{1,0:T(8,128)(2,1)}, u32[]{:S(2)}) copy-start(bf16[512,2048]{1,0:T(8,128)(2,1)} %w_ref.2) | copy-start | bytes 6291460
  48.2 5.3 %copy-start.2 = (bf16[256,1280]{1,0:T(8,128)(2,1)S(1)}, bf16[256,1280]{1,0:T(8,128)(2,1)}, u32[]{:S(2)}) copy-start(bf16[256,1280]{1,0:T(8,128)(2,1)} %copy-done.1) | copy-start | bytes 1966084
  48.2 2.4 %collective-permute-start.5 = (bf16[8,384,128]{2,1,0:T(8,128)(2,1)S(1)}, bf16[8,384,128]{2,1,0:T(8,128)(2,1)S(1)}, u32[]{:S(2)}, u32[]{:S(2)}) collective-permute-start(bf16[8,384,128]{2,1,0:T(8,128)(2,1)S(1)} %slice.41), channel_id=1, source_target_pairs={{0,2},{2,0},{4,6},{6,4},{8,10},{10,8},{12,14},{14,12},{16,18},{18,... | collective-permute-start | bytes 2359304 | tf_op jit(solution)/shard_map/ppermute | solution.py:43
  50.8 2.6 %copy-start.11 = (bf16[8,384,128]{2,1,0:T(8,128)(2,1)}, bf16[8,384,128]{2,1,0:T(8,128)(2,1)S(1)}, u32[]{:S(2)}) copy-start(bf16[8,384,128]{2,1,0:T(8,128)(2,1)S(1)} %add_convert_fusion) | copy-start | bytes 2359300
  51.7 12.7 %collective-permute-start.6 = (bf16[4,384,128]{2,1,0:T(8,128)(2,1)}, bf16[4,384,128]{2,1,0:T(8,128)(2,1)}, u32[]{:S(2)}, u32[]{:S(2)}) collective-permute-start(bf16[4,384,128]{2,1,0:T(8,128)(2,1)} %slice.42), channel_id=1, source_target_pairs={{0,4},{2,6},{4,0},{6,2},{8,12},{10,14},{12,8},{14,10},{16,20},{18,... | collective-permute-start | bytes 1179656 | tf_op jit(solution)/shard_map/ppermute | solution.py:43
  53.4 16.6 %collective-permute-start.8 = (bf16[256,1280]{1,0:T(8,128)(2,1)S(1)}, bf16[256,1280]{1,0:T(8,128)(2,1)}, u32[]{:S(2)}, u32[]{:S(2)}) collective-permute-start(bf16[256,1280]{1,0:T(8,128)(2,1)S(1)} %copy-done.2), channel_id=1, source_target_pairs={{0,1},{1,0},{2,3},{3,2},{4,5},{5,4},{6,7},{7,6},{8,9},{9,8},{10,11... | collective-permute-start | bytes 1966088 | tf_op jit(solution)/shard_map/ppermute | solution.py:43
  55.8 8.6 %copy-start.12 = (bf16[8,384,128]{2,1,0:T(8,128)(2,1)S(1)}, bf16[8,384,128]{2,1,0:T(8,128)(2,1)}, u32[]{:S(2)}) copy-start(bf16[8,384,128]{2,1,0:T(8,128)(2,1)} %copy-done.11) | copy-start | bytes 2359300
  65.5 6.8 %collective-permute-start.7 = (bf16[2,384,128]{2,1,0:T(8,128)(2,1)S(1)}, bf16[2,384,128]{2,1,0:T(8,128)(2,1)S(1)}, u32[]{:S(2)}, u32[]{:S(2)}) collective-permute-start(bf16[2,384,128]{2,1,0:T(8,128)(2,1)S(1)} %slice.44), channel_id=1, source_target_pairs={{0,8},{2,10},{4,12},{6,14},{8,0},{10,2},{12,4},{14,6},{16,24},{18,... | collective-permute-start | bytes 589832 | tf_op jit(solution)/shard_map/ppermute | solution.py:43
  72.4 6.8 %collective-permute-start.9 = (bf16[1,384,128]{2,1,0:T(8,128)(2,1)S(1)}, bf16[1,384,128]{2,1,0:T(8,128)(2,1)S(1)}, u32[]{:S(2)}, u32[]{:S(2)}) collective-permute-start(bf16[1,384,128]{2,1,0:T(8,128)(2,1)S(1)} %slice.46), channel_id=1, source_target_pairs={{0,16},{2,18},{4,20},{6,22},{8,24},{10,26},{12,28},{14,30},{16,0},... | collective-permute-start | bytes 294920 | tf_op jit(solution)/shard_map/ppermute | solution.py:43
  74.7 16.6 %collective-permute-start.12 = (bf16[256,1280]{1,0:T(8,128)(2,1)}, bf16[256,1280]{1,0:T(8,128)(2,1)}, u32[]{:S(2)}, u32[]{:S(2)}) collective-permute-start(bf16[256,1280]{1,0:T(8,128)(2,1)} %collective-permute-done.8.refs_1_), channel_id=1, source_target_pairs={{0,2},{2,0},{4,6},{6,4},{8,10},{10,8},{12,14},{14,12},{16,18},{18,... | collective-permute-start | bytes 1966088 | tf_op jit(solution)/shard_map/ppermute | solution.py:43
  79.3 6.3 %collective-permute-start.10 = (bf16[1,384,128]{2,1,0:T(8,128)(2,1)S(1)}, bf16[1,384,128]{2,1,0:T(8,128)(2,1)S(1)}, u32[]{:S(2)}, u32[]{:S(2)}) collective-permute-start(bf16[1,384,128]{2,1,0:T(8,128)(2,1)S(1)} %add_convert_fusion.3), channel_id=1, source_target_pairs={{0,16},{2,18},{4,20},{6,22},{8,24},{10,26},{12,28},{14,30},{16,0},... | collective-permute-start | bytes 294920 | tf_op jit(solution)/shard_map/ppermute | solution.py:43
  85.6 5.7 %collective-permute-start.11 = (bf16[2,384,128]{2,1,0:T(8,128)(2,1)S(1)}, bf16[2,384,128]{2,1,0:T(8,128)(2,1)S(1)}, u32[]{:S(2)}, u32[]{:S(2)}) collective-permute-start(bf16[2,384,128]{2,1,0:T(8,128)(2,1)S(1)} %pad_maximum_fusion.1), channel_id=1, source_target_pairs={{0,8},{2,10},{4,12},{6,14},{8,0},{10,2},{12,4},{14,6},{16,24},{18,... | collective-permute-start | bytes 589832 | tf_op jit(solution)/shard_map/ppermute | solution.py:43
  91.3 7.8 %collective-permute-start.13 = (bf16[4,384,128]{2,1,0:T(8,128)(2,1)S(1)}, bf16[4,384,128]{2,1,0:T(8,128)(2,1)S(1)}, u32[]{:S(2)}, u32[]{:S(2)}) collective-permute-start(bf16[4,384,128]{2,1,0:T(8,128)(2,1)S(1)} %pad_maximum_fusion.refs_0_), channel_id=1, source_target_pairs={{0,4},{2,6},{4,0},{6,2},{8,12},{10,14},{12,8},{14,10},{16,20},{18,... | collective-permute-start | bytes 1179656 | tf_op jit(solution)/shard_map/ppermute | solution.py:43
  93.1 6.8 %collective-permute-start.14 = (bf16[4,384,128]{2,1,0:T(8,128)(2,1)S(1)}, bf16[4,384,128]{2,1,0:T(8,128)(2,1)}, u32[]{:S(2)}, u32[]{:S(2)}) collective-permute-start(bf16[4,384,128]{2,1,0:T(8,128)(2,1)S(1)} %pad_maximum_fusion.refs_0_), channel_id=1, source_target_pairs={{0,2},{2,0},{4,6},{6,4},{8,10},{10,8},{12,14},{14,12},{16,18},{18,... | collective-permute-start | bytes 1179656 | tf_op jit(solution)/shard_map/ppermute | solution.py:43
  99.2 1.9 %collective-permute-start.15 = (bf16[4,384,128]{2,1,0:T(8,128)(2,1)S(1)}, bf16[4,384,128]{2,1,0:T(8,128)(2,1)}, u32[]{:S(2)}, u32[]{:S(2)}) collective-permute-start(bf16[4,384,128]{2,1,0:T(8,128)(2,1)S(1)} %collective-permute-done.13.refs_1_), channel_id=1, source_target_pairs={{0,2},{2,0},{4,6},{6,4},{8,10},{10,8},{12,14},{14,12},{16,18},{18,... | collective-permute-start | bytes 1179656 | tf_op jit(solution)/shard_map/ppermute | solution.py:43
  101.0 1.0 copy-start.4
  104.0 3.6 %collective-permute-start.17 = (f32[1,384]{1,0:T(1,128)S(1)}, f32[1,384]{1,0:T(1,128)S(1)}, u32[]{:S(2)}, u32[]{:S(2)}) collective-permute-start(f32[1,384]{1,0:T(1,128)S(1)} %get-tuple-element.79), channel_id=1, source_target_pairs={{0,1},{1,0},{2,3},{3,2},{4,5},{5,4},{6,7},{7,6},{8,9},{9,8},{10,11... | collective-permute-start | bytes 4616 | tf_op jit(solution)/shard_map/ppermute | solution.py:43
  105.4 4.6 %collective-permute-start.16 = (bf16[384,128]{1,0:T(8,128)(2,1)S(1)}, bf16[384,128]{1,0:T(8,128)(2,1)S(1)}, u32[]{:S(2)}, u32[]{:S(2)}) collective-permute-start(bf16[384,128]{1,0:T(8,128)(2,1)S(1)} %get-tuple-element.78), channel_id=1, source_target_pairs={{0,1},{1,0},{2,3},{3,2},{4,5},{5,4},{6,7},{7,6},{8,9},{9,8},{10,11... | collective-permute-start | bytes 294920 | tf_op jit(solution)/shard_map/ppermute | solution.py:43
  116.8 16.7 %all-to-all-start.1 = ((bf16[16,64,128]{2,1,0:T(8,128)(2,1)}), bf16[16,64,128]{2,1,0:T(8,128)(2,1)S(1)}, u32[]{:S(2)}, u32[]{:S(2)}) async-start(bf16[16,64,128]{2,1,0:T(8,128)(2,1)} %get-tuple-element.83.o_ref), calls=%async_computation.1 | async-start | bytes 524288 | tf_op jit(solution)/shard_map/all_to_all | solution.py:74
  133.5 18.5 %copy-start.5 = (bf16[16,64,128]{2,1,0:T(8,128)(2,1)S(1)}, bf16[16,64,128]{2,1,0:T(8,128)(2,1)}, u32[]{:S(2)}) copy-start(bf16[16,64,128]{2,1,0:T(8,128)(2,1)} %get-tuple-element.83.o_ref) | copy-start | bytes 786436
  133.5 18.5 %copy-start.10 = (f32[1,2]{1,0:T(1,128)S(1)}, f32[1,2]{1,0:T(1,128)}, u32[]{:S(2)}) copy-start(f32[1,2]{1,0:T(1,128)} %ref_ref.1) | copy-start | bytes 28
  137.9 14.1 %all-to-all-start.2 = ((bf16[16,72,128]{2,1,0:T(8,128)(2,1)}), bf16[16,72,128]{2,1,0:T(8,128)(2,1)S(1)}, u32[]{:S(2)}, u32[]{:S(2)}) async-start(bf16[16,72,128]{2,1,0:T(8,128)(2,1)} %project.1), calls=%async_computation.2 | async-start | bytes 589824 | tf_op jit(solution)/shard_map/all_to_all | solution.py:74

commit v3 on v2

v3 whole, which is shorter than its diff:
```python
import functools
import math

import jax
import jax.numpy as jnp
from jax import lax
from jax.experimental import pallas as pl
from jax.experimental.pallas import tpu as pltpu
from jax.sharding import PartitionSpec as P


HEAD = 64
LANES = 128
CHUNKS = 2
TOKEN_CHUNKS = 2
IMAGE_PARTS = 2
PARTS = 3
EXTRA = 8
f32 = jnp.float32
bf16 = jnp.bfloat16


dpo_beta = 20.0
norm_eps = 1e-06
inv_root = 1.0 / math.sqrt(HEAD)


def noise_level(step_index):
    fraction = (step_index.astype(f32) + 1.0) / 1000.0
    return 3.0 * fraction / (1.0 + 2.0 * fraction)


def dot(a, b):
    return jnp.dot(a, b, preferred_element_type=f32)


def dot_nt(a, b):
    return lax.dot_general(a, b, (((1,), (1,)), ((), ())), preferred_element_type=f32)


def dot_tn(a, b):
    return lax.dot_general(a, b, (((0,), (0,)), ((), ())), preferred_element_type=f32)


def swap(x, axis, size, mask):
    return lax.ppermute(x, axis, [(i, i ^ mask) for i in range(size)])


barrier = lax.optimization_barrier


def cost(flops, *arrays, exps=0):
    moved = sum(math.prod(a.shape) * a.dtype.itemsize for a in arrays)
    return pl.CostEstimate(flops=int(flops), bytes_accessed=moved, transcendentals=int(exps))


def vmem():
    return pl.BlockSpec(memory_space=pltpu.VMEM)


def in_hbm(x):
    return pltpu.with_memory_space_constraint(x, pltpu.HBM)


def hbm():
    return pl.BlockSpec(memory_space=pltpu.HBM)


def smem():
    return pl.BlockSpec(memory_space=pltpu.SMEM)


params = pltpu.CompilerParams(vmem_limit_bytes=20 * 1024 * 1024)


def exchange(x):
    return lax.all_to_all(x, "seq", split_axis=0, concat_axis=0, tiled=True)


def pack_kernel(q_ref, k_ref, v_ref, out_ref):
    tok = q_ref.shape[1]
    for n, ref in enumerate((q_ref, k_ref, v_ref)):
        for pair in range(ref.shape[2] // LANES):
            a = ref[0, :, pair * LANES : (pair + 1) * LANES]
            b = ref[1, :, pair * LANES : (pair + 1) * LANES]
            rows = slice(n * tok, (n + 1) * tok)
            out_ref[2 * pair, rows, :] = jnp.concatenate([a[:, :HEAD], b[:, :HEAD]], axis=1)
            out_ref[2 * pair + 1, rows, :] = jnp.concatenate([a[:, HEAD:], b[:, HEAD:]], axis=1)


def pack_heads(q, k, v):
    tok, inner = q.shape[1], q.shape[2]
    return pl.pallas_call(
        pack_kernel,
        out_shape=jax.ShapeDtypeStruct((inner // HEAD, 3 * tok, LANES), bf16),
        in_specs=[vmem()] * 3,
        out_specs=vmem(),
        compiler_params=params,
        cost_estimate=cost(0, q, k, v, q, k, v),
        name="pack_heads",
    )(q, k, v)


def down_kernel(idx_ref, mine_ref, got_ref, w_ref, low_ref, high_ref, wide_ref):
    units = w_ref.shape[0]
    both = mine_ref[...].astype(f32) + got_ref[...].astype(f32)
    gate = both[:, :units]
    hidden = (jax.nn.gelu(gate, approximate=True) * both[:, units:]).astype(bf16)
    wide_ref[...] = dot(hidden, w_ref[...]).astype(bf16)
    blocks = low_ref.shape[0]
    for n, ref in enumerate((low_ref, high_ref)):
        for p in range(blocks):
            start = pl.multiple_of(idx_ref[n * blocks + p] * LANES, LANES)
            ref[p] = wide_ref[:, pl.ds(start, LANES)]


def down_product(idx, mine, got, w_down):
    blocks, rows = w_down.shape[1] // LANES, mine.shape[0]
    return pl.pallas_call(
        down_kernel,
        out_shape=(jax.ShapeDtypeStruct((blocks // 2, rows, LANES), bf16),) * 2,
        in_specs=[smem(), vmem(), vmem(), vmem()],
        out_specs=(vmem(), vmem()),
        scratch_shapes=[pltpu.VMEM((rows, w_down.shape[1]), bf16)],
        compiler_params=params,
        cost_estimate=cost(2 * rows * w_down.size, mine, got, w_down, exps=mine.size // 2),
        name="down_product",
    )(idx, mine, got, w_down)


def as_parts(values):
    parts = []
    for rest in values:
        for _ in range(PARTS):
            piece = rest.astype(bf16).astype(f32)
            parts.append(piece)
            rest = rest - piece
    assert len(parts) <= EXTRA
    row = lax.broadcasted_iota(jnp.int32, (EXTRA, LANES), 0)
    tail = jnp.zeros((EXTRA, LANES), f32)
    for n, piece in enumerate(parts):
        tail = jnp.where(row == n, piece, tail)
    return tail.astype(bf16)


def context_kernel(first, idx_ref, pp_ref, gain_ref, w_ref, *refs):
    y_refs, ctx_ref = refs[:-1], refs[-1]
    rows = y_refs[0].shape[1]
    acc = jnp.zeros((rows, w_ref.shape[1]), f32)
    sq = jnp.zeros((rows, LANES), f32)
    p = 0
    for ref in y_refs:
        for n in range(ref.shape[0]):
            start = pl.multiple_of(idx_ref[p] * LANES, LANES)
            base = pp_ref[first : first + rows, pl.ds(start, LANES)]
            state = ref[n].astype(f32) + base.astype(f32)
            sq = sq + state * state
            scaled = (state * gain_ref[:, pl.ds(start, LANES)]).astype(bf16)
            acc = acc + dot(scaled, w_ref[pl.ds(start, LANES), :])
            p += 1
    ctx_ref[:rows, :] = acc.astype(bf16)
    sums = jnp.sum(sq.T, axis=0, keepdims=True)
    lines = []
    for at in range(0, rows, LANES):
        line = sums[:, at : at + LANES]
        short = LANES - line.shape[1]
        if short:
            line = jnp.concatenate([line, jnp.zeros((1, short), f32)], axis=1)
        lines.append(line)
    ctx_ref[rows:, :] = as_parts(lines)


def context_product(first, idx, packed_prompt, gain, w_context, pieces):
    rows = pieces[0].shape[1]
    return pl.pallas_call(
        functools.partial(context_kernel, first),
        out_shape=jax.ShapeDtypeStruct((rows + EXTRA, w_context.shape[1]), bf16),
        in_specs=[smem()] + [vmem()] * (3 + len(pieces)),
        out_specs=vmem(),
        compiler_params=params,
        cost_estimate=cost(2 * rows * w_context.size, w_context, *pieces),
        name="context_product",
    )(idx, packed_prompt, gain, w_context, *pieces)


def finish_kernel(width, select_ref, *refs):
    out_ref = refs[-1]
    text = out_ref.shape[0]
    total = jnp.zeros(out_ref.shape, f32)
    first = 0
    for mine_ref, got_ref in zip(refs[:-1:2], refs[1:-1:2]):
        both = mine_ref[...].astype(f32) + got_ref[...].astype(f32)
        rows = both.shape[0] - EXTRA
        pieces = []
        for n, at in enumerate(range(0, rows, LANES)):
            tail = rows + n * PARTS
            sums = jnp.sum(both[tail : tail + PARTS], axis=0, keepdims=True)
            size = min(LANES, rows - at)
            inv = column(lax.rsqrt(sums / width + norm_eps))[:size]
            pieces.append((both[at : at + size] * inv).astype(bf16))
        ctx = jnp.concatenate(pieces, axis=0)
        total = total + dot_tn(select_ref[first : first + rows, :text], ctx)
        first += rows
    out_ref[...] = total.astype(bf16)


def finish_context(width, text, select, pairs):
    return pl.pallas_call(
        functools.partial(finish_kernel, width),
        out_shape=jax.ShapeDtypeStruct((text, pairs[0][0].shape[1]), bf16),
        in_specs=[vmem()] * (1 + 2 * len(pairs)),
        out_specs=vmem(),
        compiler_params=params,
        cost_estimate=cost(2 * text * select.shape[0] * LANES, select),
        name="finish_context",
    )(select, *[x for pair in pairs for x in pair])


def column(row):
    return jnp.broadcast_to(row, (LANES, row.shape[1])).T


def corner_kernel(at_ref, in_ref, out_ref, sem):
    rows, cols = out_ref.shape
    row = pl.multiple_of(at_ref[0] * rows, 16)
    col = pl.multiple_of(at_ref[1] * cols, LANES)
    copy = pltpu.make_async_copy(in_ref.at[pl.ds(row, rows), pl.ds(col, cols)], out_ref, sem)
    copy.start()
    copy.wait()


def corner(at, array, rows, cols):
    out = jax.ShapeDtypeStruct((rows, cols), array.dtype)
    return pl.pallas_call(
        corner_kernel,
        out_shape=out,
        in_specs=[smem(), hbm()],
        out_specs=vmem(),
        scratch_shapes=[pltpu.SemaphoreType.DMA(())],
        compiler_params=params,
        cost_estimate=cost(0, out, out),
        name="corner",
    )(at, in_hbm(array))


def weight_copies(w_refs, buf_ref, sems):
    copies = []
    rows = w_refs[0].shape[0] // CHUNKS
    for n, ref in enumerate(w_refs):
        for chunk in range(CHUNKS):
            at = pl.ds(chunk * rows, rows)
            copies.append(
                pltpu.make_async_copy(ref.at[at], buf_ref.at[n, at], sems.at[n * CHUNKS + chunk])
            )
    for copy in copies:
        copy.start()
    return copies


def norm_own_kernel(at_ref, prompt_ref, gain_ref, normed_ref, scale_ref):
    value = prompt_ref[...].astype(f32)
    scale = lax.rsqrt(jnp.mean(value * value, axis=-1, keepdims=True) + norm_eps)
    cols = normed_ref.shape[1]
    start = pl.multiple_of(at_ref[0] * cols, LANES)
    here = prompt_ref[:, pl.ds(start, cols)].astype(f32)
    normed_ref[...] = (here * scale * gain_ref[:, pl.ds(start, cols)]).astype(bf16)
    scale_ref[...] = jnp.broadcast_to(scale, (scale.shape[0], LANES)).T[:1]


def norm_own(at, prompt, gain, cols):
    rows = prompt.shape[0]
    return pl.pallas_call(
        norm_own_kernel,
        out_shape=(pltpu.HBM((rows, cols), bf16), jax.ShapeDtypeStruct((1, rows), f32)),
        in_specs=[smem(), vmem(), vmem()],
        out_specs=(vmem(), vmem()),
        compiler_params=params,
        cost_estimate=cost(0, prompt, prompt),
        name="norm_own",
    )(at, prompt, gain)


def gate_up_kernel(
    at_ref, a_hbm, b_ref, scale_ref, gain_ref, wg_ref, wu_ref, own_hbm, select_ref, *refs
):
    out_refs = refs[:-5]
    normed_ref, parts_ref, buf_ref, sems, a_ref = refs[-5:]
    half, cols = a_ref.shape
    rows = 2 * half
    a_copy = pltpu.make_async_copy(a_hbm, a_ref, sems.at[2 * CHUNKS])
    own_copy = pltpu.make_async_copy(own_hbm, normed_ref.at[pl.ds(0, rows)], sems.at[2 * CHUNKS + 1])
    a_copy.start()
    own_copy.start()
    copies = weight_copies((wg_ref, wu_ref), buf_ref, sems)
    start = pl.multiple_of(at_ref[0] * cols, LANES)
    gain = gain_ref[:, pl.ds(start, cols)]
    scales = column(scale_ref[...])
    swapped = at_ref[1] == 1
    low, high = scales[:half, :1], scales[half:, :1]
    scale_a = jnp.where(swapped, high, low)
    scale_b = jnp.where(swapped, low, high)
    normed_ref[rows + half :, :] = (b_ref[...].astype(f32) * scale_b * gain).astype(bf16)
    a_copy.wait()
    normed_ref[rows : rows + half, :] = (a_ref[...].astype(f32) * scale_a * gain).astype(bf16)
    own_copy.wait()
    units = buf_ref.shape[2]
    depth = cols // CHUNKS
    for n in range(2):
        acc = None
        for chunk in range(CHUNKS):
            copies[n * CHUNKS + chunk].wait()
            part = slice(chunk * depth, (chunk + 1) * depth)
            term = dot(normed_ref[:, part], buf_ref[n, part, :])
            acc = term if acc is None else acc + term
        parts_ref[:, n * units : (n + 1) * units] = acc.astype(bf16)
    for chunk, out_ref in enumerate(out_refs):
        size = out_ref.shape[0]
        select = select_ref[chunk * size : (chunk + 1) * size, :]
        out_ref[...] = dot(select, parts_ref[...]).astype(bf16)


def gate_up(at, a, b, scale, gain, w_gate, w_up, own, select):
    total, rows = select.shape
    cols, units = w_gate.shape
    size = total // TOKEN_CHUNKS
    return pl.pallas_call(
        gate_up_kernel,
        out_shape=(jax.ShapeDtypeStruct((size, 2 * units), bf16),) * TOKEN_CHUNKS,
        in_specs=[smem(), hbm()] + [vmem()] * 3 + [hbm()] * 3 + [vmem()],
        out_specs=(vmem(),) * TOKEN_CHUNKS,
        scratch_shapes=[
            pltpu.VMEM((rows, cols), bf16),
            pltpu.VMEM((rows, 2 * units), bf16),
            pltpu.VMEM((2, cols, units), bf16),
            pltpu.SemaphoreType.DMA((2 * CHUNKS + 2,)),
            pltpu.VMEM(a.shape, bf16),
        ],
        compiler_params=params,
        cost_estimate=cost(4 * rows * w_gate.size, a, b, w_gate, w_up, own),
        name="gate_up",
    )(at, in_hbm(a), b, scale, gain, in_hbm(w_gate), in_hbm(w_up), in_hbm(own), select)


def pack_rows_kernel(at_ref, prompt_hbm, a_ref, b_ref, select_ref, out_ref, rows_ref, sem):
    half, cols = a_ref.shape
    rows = 2 * half
    start = pl.multiple_of(at_ref[0] * cols, LANES)
    copy = pltpu.make_async_copy(
        prompt_hbm.at[:, pl.ds(start, cols)], rows_ref.at[pl.ds(0, rows)], sem
    )
    copy.start()
    rows_ref[rows : rows + half, :] = a_ref[...]
    rows_ref[rows + half :, :] = b_ref[...]
    copy.wait()
    out_ref[...] = dot(select_ref[...], rows_ref[...]).astype(bf16)


def pack_rows(at, prompt, a, b, select):
    cols = a.shape[1]
    return pl.pallas_call(
        pack_rows_kernel,
        out_shape=jax.ShapeDtypeStruct((select.shape[0], cols), bf16),
        in_specs=[smem(), hbm(), vmem(), vmem(), vmem()],
        out_specs=vmem(),
        scratch_shapes=[pltpu.VMEM((select.shape[1], cols), bf16), pltpu.SemaphoreType.DMA(())],
        compiler_params=params,
        cost_estimate=cost(2 * select.size * cols, a, b, a, b, a, b),
        name="pack_rows",
    )(at, in_hbm(prompt), a, b, select)


def encode_shared(
    S, prompt, lengths, gain_ffn, w_gate, w_up, w_down, gain_final, w_context, w_out, qkv_in
):
    s = lax.axis_index("seq")
    f = lax.axis_index("fsdp")
    own = prompt[0]
    rows, width = own.shape
    cols = width // 2
    half = rows // 2
    core = s & 1

    away = corner(jnp.stack([core, 1 - f]).astype(jnp.int32), own, half, cols)
    got_a = swap(away, "fsdp", 2, 1)
    other_len = swap(lengths, "fsdp", 2, 1)[0]
    away, own = barrier((away, own))
    at = jnp.stack([f, core]).astype(jnp.int32)
    normed_own, scale = norm_own(at, own, gain_ffn[None], cols)
    other_scale = swap(scale, "fsdp", 2, 1)
    normed_own, *qkv_in = barrier((normed_own, *qkv_in))
    blocks = pack_heads(*qkv_in)
    qkv = exchange(blocks)
    qkv = qkv.reshape(S, 3, -1, LANES)

    first = core * half
    own_len = lengths[0]
    own_start = jnp.where(f == 0, 0, other_len)
    other_start = jnp.where(f == 0, own_len, 0)
    row = jnp.arange(half, dtype=jnp.int32)
    source = jnp.concatenate([row, row + half, row + first, row + half - first])
    is_own = jnp.arange(2 * rows) < rows
    place = source + jnp.where(is_own, own_start, other_start)
    place = jnp.where(source < jnp.where(is_own, own_len, other_len), place, -1)
    total = rows * 3 // 2
    select = (jnp.arange(total)[:, None] == place[None, :]).astype(bf16)
    got_a, other_scale, select = barrier((got_a, other_scale, select))
    got_b = swap(got_a, "seq", S, 1)

    packed = gate_up(
        at, got_a, got_b, other_scale, gain_ffn[None], w_gate, w_up, normed_own, select
    )
    received = []
    for part in packed:
        received.append(swap(part, "fsdp", 2, 1))
    first_part, got_a, got_b = barrier((packed[0], got_a, got_b))
    packed = [first_part, *packed[1:]]
    packed_prompt = pack_rows(at, own, got_a, got_b, select)
    received[0], packed_prompt = barrier((received[0], packed_prompt))
    w_half = w_out.shape[0] // 2
    w_away = corner(jnp.stack([core, 0]).astype(jnp.int32), w_out, w_half, w_out.shape[1])
    w_a = swap(w_away, "fsdp", 2, 1)
    w_b = swap(w_a, "seq", S, 1)

    rest = S // 4
    order = [c + 2 * x + 4 * j for c in range(2) for x in range(2) for j in range(rest)]
    idx = jnp.array(order, jnp.int32) ^ s
    gain_here = lax.dynamic_slice(gain_final, (f * cols,), (cols,))[None]
    add = lambda *terms: sum(t.astype(f32) for t in terms).astype(bf16)
    pairs = []
    image = None
    for c in range(TOKEN_CHUNKS):

        def move(value, mask):
            return swap(value, "seq", S, mask)

        low, high = down_product(idx, packed[c], received[c], w_down)
        got = move(high, 1)
        send = add(low[rest:], got[rest:])
        got_x = move(send, 2)
        keep = add(low[:rest], got[:rest])
        mine = [add(keep[j : j + 1], got_x[j : j + 1]) for j in range(rest)]
        got_z = [move(mine[j], 4 * j) for j in range(1, rest)]
        block = add(mine[0], *got_z)
        near = [block] + [move(block, 4 * j) for j in range(1, rest)]
        near = jnp.concatenate(near, axis=0)
        far = move(near, 2)
        pieces = [near, far, move(near, 1), move(far, 1)]
        size = packed[c].shape[0]
        ctx = context_product(c * size, idx, packed_prompt, gain_here, w_context, pieces)
        pairs.append((ctx, swap(ctx, "fsdp", 2, 1)))
    for part in range(IMAGE_PARTS):
        image = image_part(qkv, part, IMAGE_PARTS, image)
    ctx = finish_context(width, rows, select, pairs)
    there = 2 * (1 - f)
    w_idx = jnp.stack([2 * f, 2 * f + 1, there + core, there + 1 - core]).astype(jnp.int32)
    return ctx, qkv, image, (w_out, w_a, w_b), w_idx


def rms_gain(values, gain):
    mean_sq = jnp.mean(values * values, axis=-1, keepdims=True)
    return values * lax.rsqrt(mean_sq + norm_eps) * gain


def encode_gathered(prompt, gain_ffn, w_gate, w_up, w_down, gain_final, w_context):
    gate_full = lax.all_gather(w_gate, "fsdp", axis=0, tiled=True)
    up_full = lax.all_gather(w_up, "fsdp", axis=0, tiled=True)
    down_full = lax.all_gather(w_down, "fsdp", axis=1, tiled=True)
    context_full = lax.all_gather(w_context, "fsdp", axis=0, tiled=True)
    prompt_f32 = prompt[0].astype(f32)
    normed = rms_gain(prompt_f32, gain_ffn).astype(bf16)
    hidden = (
        jax.nn.gelu(dot(normed, gate_full), approximate=True) * dot(normed, up_full)
    ).astype(bf16)
    summed = lax.psum(dot(hidden, down_full).astype(bf16), "seq").astype(f32)
    encoded = rms_gain(prompt_f32 + summed, gain_final).astype(bf16)
    return dot(encoded, context_full).astype(bf16)


def rows_of(ref):
    value = ref[...]
    return value.reshape(-1, LANES)


def first_lanes(x):
    return lax.broadcasted_iota(jnp.int32, x.shape, 1) < HEAD


def by_stream(first, second):
    return jnp.where(first_lanes(first), first, second)


def wide(first, second):
    shape = (first.shape[0], LANES)
    return by_stream(jnp.broadcast_to(first, shape), jnp.broadcast_to(second, shape))


def masked(x):
    none = jnp.zeros_like(x)
    return by_stream(x, none), by_stream(none, x)


def turned(x):
    return jnp.concatenate([x[:, HEAD:], x[:, :HEAD]], axis=1)


def with_sums(values):
    ones = masked(jnp.ones(values[0].shape, bf16))
    return [jnp.concatenate([v, one], axis=1) for v, one in zip(values, ones)]


def image_kernel(q_ref, k_ref, v_ref, *refs):
    e_ref, o_ref, m_ref, l_ref = refs[-4:]
    q = rows_of(q_ref) * jnp.asarray(inv_root, bf16)
    keys = masked(rows_of(k_ref))
    values = with_sums(masked(rows_of(v_ref)))
    both, tops = None, []
    for stream in range(2):
        scores = dot_nt(q, keys[stream])
        top = jnp.max(scores, axis=-1, keepdims=True)
        e = jnp.exp(scores - top).astype(bf16)
        e_ref[stream] = e
        term = dot(e, values[stream])
        both = term if both is None else both + term
        tops.append(top)
    o_ref[...] = both[:, :LANES]
    l_ref[...] = both[:, LANES:]
    m_ref[...] = wide(*tops)


def q_blocks(S, tok):
    rows = min(256, S * tok)
    return rows // tok, S * tok // rows, rows


def image_part(qkv, part, parts, previous=None):
    S, _, tok, _ = qkv.shape
    group, steps, rows = q_blocks(S, tok)
    seq_len = S * tok
    steps //= parts
    first = part * steps
    whole = lambda n: pl.BlockSpec((S, None, tok, LANES), lambda i: (0, n, 0, 0))
    flat = pl.BlockSpec((rows, LANES), lambda i: (first + i, 0))
    earlier = () if previous is None else previous
    return pl.pallas_call(
        image_kernel,
        grid=(steps,),
        out_shape=(pltpu.HBM((2, seq_len, seq_len), bf16),)
        + (pltpu.HBM((seq_len, LANES), f32),) * 3,
        in_specs=[
            pl.BlockSpec((group, None, tok, LANES), lambda i: (first + i, 0, 0, 0)),
            whole(1),
            whole(2),
        ]
        + [pl.BlockSpec(memory_space=pltpu.HBM)] * len(earlier),
        out_specs=(
            pl.BlockSpec((2, rows, seq_len), lambda i: (0, first + i, 0)), flat, flat, flat,
        ),
        input_output_aliases={3 + n: n for n in range(len(earlier))},
        compiler_params=params,
        cost_estimate=cost(
            16 * seq_len * seq_len * LANES // parts, qkv, exps=2 * seq_len * seq_len // parts
        ),
        name="image_part",
    )(qkv, qkv, qkv, *earlier)


def text_sides(ctx):
    other = turned(ctx)
    none = jnp.zeros_like(ctx)
    keys = (by_stream(ctx, none), by_stream(none, other))
    return keys, (by_stream(other, none), by_stream(none, ctx))


def text_kernel(len_ref, q_ref, ctx_ref, o_ref, m_ref, l_ref, out_ref, e_ref, ci_ref, ct_ref):
    q = rows_of(q_ref) * jnp.asarray(inv_root, bf16)
    keys, values = text_sides(ctx_ref[...])
    values = with_sums(values)
    keep = lax.broadcasted_iota(jnp.int32, (q.shape[0], ctx_ref.shape[0]), 1) < len_ref[0]
    both, tops = None, []
    for stream in range(2):
        scores = jnp.where(keep, dot_nt(q, keys[stream]), -jnp.inf)
        top = jnp.max(scores, axis=-1, keepdims=True)
        e = jnp.exp(scores - top).astype(bf16)
        e_ref[stream] = e
        term = dot(e, values[stream])
        both = term if both is None else both + term
        tops.append(top)
    top_text = wide(*tops)
    top_image = m_ref[...]
    top = jnp.maximum(top_image, top_text)
    shrink_image = jnp.exp(top_image - top)
    shrink_text = jnp.exp(top_text - top)
    inv = 1.0 / (l_ref[...] * shrink_image + both[:, LANES:] * shrink_text)
    scale_image = shrink_image * inv
    scale_text = shrink_text * inv
    out = o_ref[...] * scale_image + both[:, :LANES] * scale_text
    out_ref[...] = out.astype(bf16).reshape(out_ref.shape)
    ci_ref[...] = scale_image
    ct_ref[...] = scale_text


def text_part(lengths, qkv, ctx, o_img, m_img, l_img):
    S, _, tok, _ = qkv.shape
    group, steps, rows = q_blocks(S, tok)
    seq_len = S * tok
    text = ctx.shape[0]
    flat = pl.BlockSpec((rows, LANES), lambda i: (i, 0))
    return pl.pallas_call(
        text_kernel,
        grid=(steps,),
        out_shape=(
            pltpu.HBM((S, tok, LANES), bf16),
            pltpu.HBM((2, seq_len, text), bf16),
            pltpu.HBM((seq_len, LANES), f32),
            pltpu.HBM((seq_len, LANES), f32),
        ),
        in_specs=[
            smem(),
            pl.BlockSpec((group, None, tok, LANES), lambda i: (i, 0, 0, 0)),
            pl.BlockSpec((text, LANES), lambda i: (0, 0)),
            flat,
            flat,
            flat,
        ],
        out_specs=(
            pl.BlockSpec((group, tok, LANES), lambda i: (i, 0, 0)),
            pl.BlockSpec((2, rows, text), lambda i: (0, i, 0)),
            flat,
            flat,
        ),
        compiler_params=params,
        cost_estimate=cost(16 * seq_len * ctx.size, o_img, m_img, l_img, exps=2 * seq_len * text),
        name="text_part",
    )(lengths, qkv, ctx, in_hbm(o_img), in_hbm(m_img), in_hbm(l_img))


def load_kernel(target_hbm, *refs):
    counts = len(refs) - 3
    target_ref, buf_ref, sems = refs[counts:]
    block_rows = buf_ref.shape[1]
    copies = [pltpu.make_async_copy(target_hbm, target_ref, sems.at[0])]
    for ref in refs[:counts]:
        for n in range(ref.shape[0] // block_rows):
            slot = len(copies)
            at = pl.ds(n * block_rows, block_rows)
            copies.append(pltpu.make_async_copy(ref.at[at], buf_ref.at[slot - 1], sems.at[slot]))
    for copy in copies:
        copy.start()
    for copy in copies:
        copy.wait()


def load_weights(blocks, target, weights):
    rows = sum(w.shape[0] for w in weights) // blocks
    return pl.pallas_call(
        load_kernel,
        out_shape=(
            jax.ShapeDtypeStruct(target.shape, bf16),
            jax.ShapeDtypeStruct((blocks, rows, target.shape[-1]), bf16),
        ),
        in_specs=[hbm()] * (1 + len(weights)),
        out_specs=(vmem(), vmem()),
        scratch_shapes=[pltpu.SemaphoreType.DMA((blocks + 1,))],
        compiler_params=params,
        cost_estimate=cost(0, target, target, *weights, *weights),
        name="load_weights",
    )(in_hbm(target), *[in_hbm(w) for w in weights])


def project_kernel(idx_ref, o_ref, target_ref, w_ref, out_ref, a_ref):
    heads, tok = o_ref.shape[0], o_ref.shape[1]
    blocks, _, block_rows = a_ref.shape
    pairs = block_rows // LANES
    for pair in range(heads // 2):
        a, b = o_ref[2 * pair], o_ref[2 * pair + 1]
        at = slice((pair % pairs) * LANES, (pair % pairs + 1) * LANES)
        a_ref[pair // pairs, :tok, at] = jnp.concatenate([a[:, :HEAD], b[:, :HEAD]], axis=1)
        a_ref[pair // pairs, tok:, at] = jnp.concatenate([a[:, HEAD:], b[:, HEAD:]], axis=1)
    pred = None
    for slot in range(blocks):
        term = dot(a_ref[idx_ref[slot]], w_ref[slot])
        pred = term if pred is None else pred + term
    target = target_ref[...].reshape(2 * tok, -1).astype(f32)
    residual = pred - target
    grad = residual.astype(bf16)
    for slot in range(blocks):
        g = dot_nt(grad, w_ref[slot]).astype(bf16)
        head = idx_ref[slot] * (2 * pairs)
        for pair in range(pairs):
            a = g[:tok, pair * LANES : (pair + 1) * LANES]
            b = g[tok:, pair * LANES : (pair + 1) * LANES]
            out_ref[head + 2 * pair, :tok] = jnp.concatenate([a[:, :HEAD], b[:, :HEAD]], axis=1)
            out_ref[head + 2 * pair + 1, :tok] = jnp.concatenate(
                [a[:, HEAD:], b[:, HEAD:]], axis=1
            )
    squares = residual * residual
    totals = []
    for stream in range(2):
        part = squares[stream * tok : (stream + 1) * tok]
        total = jnp.sum(jnp.sum(part, axis=0, keepdims=True), axis=1, keepdims=True)
        totals.append(jnp.broadcast_to(total, (1, LANES)))
    tail = as_parts(totals)
    for head in range(heads):
        out_ref[head, tok:] = tail


def project(idx, attended, target, weights):
    S, tok, _ = attended.shape
    blocks, block_rows, _ = weights.shape
    return pl.pallas_call(
        project_kernel,
        out_shape=jax.ShapeDtypeStruct((S, tok + EXTRA, LANES), bf16),
        in_specs=[smem()] + [vmem()] * 3,
        out_specs=vmem(),
        scratch_shapes=[pltpu.VMEM((blocks, 2 * tok, block_rows), bf16)],
        compiler_params=params,
        cost_estimate=cost(8 * tok * weights.size, weights, attended, attended, target),
        name="project",
    )(idx, attended, target, weights)


def dpo_terms(err_ref, step_ref, ref_ref, count):
    parts = jnp.sum(err_ref[...].astype(f32), axis=0)
    totals = [
        jnp.sum(parts[n * PARTS : (n + 1) * PARTS], axis=0, keepdims=True) for n in range(2)
    ]
    errors = jnp.concatenate(totals, axis=0) / count
    step_index = jnp.full((1, LANES), step_ref[0], jnp.int32)
    sigma_t = noise_level(step_index)
    gap = (errors[0:1] - ref_ref[0, 0]) - (errors[1:2] - ref_ref[0, 1])
    logit = dpo_beta * sigma_t * gap
    small = jnp.exp(-jnp.abs(logit))
    loss = jnp.maximum(logit, 0.0) + jnp.log1p(small)
    return loss, sigma_t * jnp.where(logit >= 0, 1.0, small) / (1.0 + small)


def lane_in_half(x):
    return lax.broadcasted_iota(jnp.int32, x.shape, 1) % HEAD


def score_grads(g, delta, scale, values, weights):
    scaled = (g * scale).astype(bf16)
    term = -(delta * scale)
    term = jnp.concatenate([term[:, HEAD:], term[:, :HEAD]], axis=1)
    high = term.astype(bf16).astype(f32)
    place = lane_in_half(term)
    extra = jnp.where(place == 0, high, jnp.where(place == 1, term - high, 0.0)).astype(bf16)
    left = (by_stream(scaled, extra), by_stream(extra, scaled))
    grads = []
    for stream in range(2):
        product = dot_nt(left[stream], values[stream])
        grads.append((weights[stream].astype(f32) * product).astype(bf16))
    return grads, scaled


def with_marks(values):
    marks = (lane_in_half(values[0]) < 2).astype(bf16)
    return by_stream(values[0], marks), by_stream(marks, values[1])


def backward_kernel(
    count, err_ref, step_ref, ref_ref, q_ref, k_ref, v_ref, ctx_ref, e_ref, p_ref, ci_ref, ct_ref,
    o_ref, g_ref, loss_ref, dq_ref, dk_ref, dv_ref, ka_ref, va_ref,
):
    step = pl.program_id(0)
    loss, weight = dpo_terms(err_ref, step_ref, ref_ref, count)
    q = rows_of(q_ref)
    keys = masked(rows_of(k_ref))
    values = with_marks(masked(rows_of(v_ref)))
    text_keys, text_values = text_sides(ctx_ref[...])
    text_values = with_marks(text_values)
    o = rows_of(o_ref).astype(f32)
    g = g_ref[:, : o_ref.shape[1], :].reshape(-1, LANES).astype(f32)

    @pl.when(step == 0)
    def _():
        loss_ref[...] = loss
        ka_ref[...] = jnp.zeros_like(ka_ref)
        va_ref[...] = jnp.zeros_like(va_ref)

    delta = wide(*[jnp.sum(part, axis=-1, keepdims=True) for part in masked(g * o)])
    e = [e_ref[0], e_ref[1]]
    image, scaled = score_grads(g, delta, ci_ref[...], values, e)
    text, _ = score_grads(g, delta, ct_ref[...], text_values, [p_ref[0], p_ref[1]])
    dq = None
    for stream in range(2):
        term = dot(image[stream], keys[stream]) + dot(text[stream], text_keys[stream])
        dq = term if dq is None else dq + term
        at = slice(stream * HEAD, (stream + 1) * HEAD)
        ka_ref[stream] += dot_tn(q, image[stream])[at]
        va_ref[stream] += dot_tn(scaled, e[stream])[at]
    signed = wide(weight[:, :1], -weight[:, :1])
    turned_dq = (dq * (signed * inv_root)).T.astype(bf16)
    dq_ref[0] = turned_dq[:HEAD]
    dq_ref[1] = turned_dq[HEAD:]

    @pl.when(step == pl.num_programs(0) - 1)
    def _():
        for stream, coef in enumerate((weight[:, :1], -weight[:, :1])):
            dk_ref[stream] = (ka_ref[stream] * (coef * inv_root)).astype(bf16)
            dv_ref[stream] = (va_ref[stream] * coef).astype(bf16)


def backward_part(count, steps_in, refs_in, qkv, ctx, e, e_text, scales, attended, grads):
    S, _, tok, _ = qkv.shape
    group, steps, rows = q_blocks(S, tok)
    seq_len = S * tok
    text = ctx.shape[0]
    whole = lambda n: pl.BlockSpec((S, None, tok, LANES), lambda i: (0, n, 0, 0))
    block = pl.BlockSpec((group, tok, LANES), lambda i: (i, 0, 0))
    full = pl.BlockSpec((None, 2, HEAD, seq_len), lambda i: (0, 0, 0, 0))
    out = jax.ShapeDtypeStruct((1, 2, HEAD, seq_len), bf16)
    return pl.pallas_call(
        functools.partial(backward_kernel, count),
        grid=(steps,),
        out_shape=(jax.ShapeDtypeStruct((1, LANES), f32), out, out, out),
        in_specs=[
            pl.BlockSpec((S, EXTRA, LANES), lambda i: (0, tok // EXTRA, 0)),
            smem(),
            smem(),
            pl.BlockSpec((group, None, tok, LANES), lambda i: (i, 0, 0, 0)),
            whole(1),
            whole(2),
            pl.BlockSpec((text, LANES), lambda i: (0, 0)),
            pl.BlockSpec((2, rows, seq_len), lambda i: (0, i, 0)),
            pl.BlockSpec((2, rows, text), lambda i: (0, i, 0)),
            pl.BlockSpec((rows, LANES), lambda i: (i, 0)),
            pl.BlockSpec((rows, LANES), lambda i: (i, 0)),
            block,
            pl.BlockSpec((group, tok + EXTRA, LANES), lambda i: (i, 0, 0)),
        ],
        out_specs=(
            pl.BlockSpec((1, LANES), lambda i: (0, 0)),
            pl.BlockSpec((None, 2, HEAD, rows), lambda i: (0, 0, 0, i)),
            full,
            full,
        ),
        scratch_shapes=[pltpu.VMEM((2, HEAD, seq_len), f32)] * 2,
        compiler_params=params,
        cost_estimate=cost(40 * seq_len * seq_len * LANES, e, e_text, qkv),
        name="backward_part",
    )(
        grads, steps_in, refs_in, qkv, qkv, qkv, ctx, in_hbm(e), in_hbm(e_text),
        *[in_hbm(x) for x in scales], attended, grads,
    )


def on_device(
    S, F, prompt, lengths, timesteps, ref_errors, gain_ffn, w_in_gate, w_in_up, w_in_down,
    gain_final, w_context, image_q, image_k, image_v, w_out, target,
):
    tok = image_q.shape[2]
    seq_len = S * tok
    if F == 2 and w_in_down.shape[1] == S * LANES:
        ctx, qkv, image, weights, w_idx = encode_shared(
            S, prompt, lengths, gain_ffn, w_in_gate, w_in_up, w_in_down, gain_final, w_context,
            w_out, (image_q[0], image_k[0], image_v[0]),
        )
    else:
        qkv = exchange(pack_heads(image_q[0], image_k[0], image_v[0])).reshape(S, 3, tok, LANES)
        ctx = encode_gathered(
            prompt, gain_ffn, w_in_gate, w_in_up, w_in_down, gain_final, w_context
        )
        image = image_part(qkv, 0, 1)
        weights = (lax.all_gather(w_out, "fsdp", axis=0, tiled=True),)
        w_idx = jnp.arange(F, dtype=jnp.int32)
    e_img, o_img, m_img, l_img = image

    attended, e_text, *scales = text_part(lengths, qkv, ctx, o_img, m_img, l_img)
    tokens = exchange(attended)
    loaded, blocks = load_weights(w_idx.shape[0], target[0], weights)
    grads = exchange(project(w_idx, tokens, loaded, blocks))
    loss, grad_q, grad_k, grad_v = backward_part(
        seq_len * target.shape[-1], timesteps, ref_errors, qkv, ctx, e_img, e_text, scales,
        attended, grads,
    )
    turn = lambda x: jnp.swapaxes(x, 2, 3)
    return loss[0, :1], turn(grad_q), turn(grad_k), turn(grad_v)


def solution(mesh):
    S, F = mesh.shape["seq"], mesh.shape["fsdp"]

    def body(*args):
        return on_device(S, F, *args)

    return jax.shard_map(
        body,
        mesh=mesh,
        in_specs=(
            P("fsdp", None, None),
            P("fsdp"),
            P("fsdp"),
            P("fsdp", None),
            P(),
            P("fsdp", "seq"),
            P("fsdp", "seq"),
            P("seq", "fsdp"),
            P(),
            P("fsdp", "seq"),
            P("fsdp", None, "seq", None),
            P("fsdp", None, "seq", None),
            P("fsdp", None, "seq", None),
            P("fsdp", None),
            P("fsdp", None, "seq", None),
        ),
        out_specs=(
            P("fsdp"),
            P("fsdp", None, None, "seq"),
            P("fsdp", None, None, "seq"),
            P("fsdp", None, None, "seq"),
        ),
        check_vma=False,
    )
```

time: 162 us -> 166 us (1.025)
  starting transfers between devices: 35.6 us -> 48 us
  waiting for transfers between devices: 67 us -> 54.7 us
  Pallas kernels: 46.1 us -> 51.1 us
  matrix products: 2.99 us -> 0 us
    ppermute x18 -> x32, starting transfers between devices: 19.4 us -> 34 us  [swap(): return lax.ppermute(x, axis, [(i, i ^ mask) for i in range(size)])]
    ppermute x18 -> x32, waiting for transfers between devices: 46.4 us -> 37.5 us  [swap(): return lax.ppermute(x, axis, [(i, i ^ mask) for i in range(size)])]
    pallas_call x4 -> x9, Pallas kernels: 15.9 us -> 21.3 us  [the longest x1 5.68 us: gate_up(): pl.pallas_call(gate_up_kernel, out_shape=(jax.ShapeDtypeStruct((size, 2 *...]
    all_to_all x3, waiting for transfers between devices: 20.6 us -> 17.2 us  [exchange(): return lax.all_to_all(x, 'seq', split_axis=0, concat_axis=0, tiled=True)]
    dot_general x2 -> x0, matrix products: 2.99 us -> none  [the longest x1 2.67 us: dot(): return jnp.dot(a, b, preferred_element_type=f32)]
    all_to_all x3, starting transfers between devices: 16.2 us -> 14 us  [exchange(): return lax.all_to_all(x, 'seq', split_axis=0, concat_axis=0, tiled=True)]
    pallas_call x1 -> x2, Pallas kernels: 6.08 us -> 8.12 us  [image_part(): pl.pallas_call(image_kernel, grid=(steps,), out_shape=(pltpu.HBM((2, seq_...]
    pallas_call x1, Pallas kernels: 4.39 us -> 2.46 us  [project(): pl.pallas_call(project_kernel, out_shape=jax.ShapeDtypeStruct((S, tok + E...]
  transfers between devices with their start and end apart: 21 -> 35, of which waited for: 17 -> 16; matrix products, arithmetic and copies ran while one was open for 4% -> 3% of each run, Pallas kernels for 11% -> 20%
where the time goes in v3:
time: 166 us; the launch traced here: 165 us
  waiting for transfers between devices  54.7 us (33%)
  Pallas kernels  51.1 us (31%)
  starting transfers between devices  48 us (29%)
  other arithmetic  4.19 us (3%)
  local copies, waits for them, and re-layouts  4.1 us (2%)
  between operations  3.02 us (2%)
    ppermute x32, waiting for transfers between devices, swap(): return lax.ppermute(x, axis, [(i, i ^ mask) for i in range(size)])  37.5 us
    ppermute x32, starting transfers between devices, swap(): return lax.ppermute(x, axis, [(i, i ^ mask) for i in range(size)])  34 us
    all_to_all x3, waiting for transfers between devices, exchange(): return lax.all_to_all(x, 'seq', split_axis=0, concat_axis=0, tiled=True)  17.2 us
    all_to_all x3, starting transfers between devices, exchange(): return lax.all_to_all(x, 'seq', split_axis=0, concat_axis=0, tiled=True)  14 us
    pallas_call x1, Pallas kernels, backward_part(): pl.pallas_call(functools.partial(backward_kernel, count), grid=(steps,),...  9 us
    pallas_call x2, Pallas kernels, image_part(): pl.pallas_call(image_kernel, grid=(steps,), out_shape=(pltpu.HBM((2, seq_...  8.12 us
    pallas_call x1, Pallas kernels, gate_up(): pl.pallas_call(gate_up_kernel, out_shape=(jax.ShapeDtypeStruct((size, 2 *...  5.68 us
    pallas_call x1, Pallas kernels, text_part(): pl.pallas_call(text_kernel, grid=(steps,), out_shape=(pltpu.HBM((S, tok,...  4.95 us
  transfers between devices with their start and end apart: 35, of which 16 were waited for; matrix products, arithmetic and copies ran while one was open for 3% of the time, Pallas kernels for 20%

profile of v3, /device:TPU:0, one launch (start us, length us, event | category | flops | bytes accessed | tf_op | source)
XLA Modules:
  0.0 165.1 jit_solution(15841732569756977572)
XLA Ops:
  0.7 1.6 corner.2
  2.3 3.1 %collective-permute-start = (bf16[128,2048]{1,0:T(8,128)(2,1)S(1)}, bf16[128,2048]{1,0:T(8,128)(2,1)}, u32[]{:S(2)}, u32[]{:S(2)}) collective-permute-start(bf16[128,2048]{1,0:T(8,128)(2,1)S(1)} %corner.2), channel_id=1, source_target_pairs={{0,1},{1,0},{2,3},{3,2},{4,5},{5,4},{6,7},{7,6},{8,9},{9,8},{10,11... | collective-permute-start | bytes 1572872 | tf_op jit(solution)/shard_map/ppermute | solution.py:46
  5.5 2.3 %norm_own.1 = (bf16[256,2048]{1,0:T(8,128)(2,1)}, f32[1,256]{1,0:T(1,128)S(1)}) custom-call(s32[2]{0:T(128)S(1)} %pad_add_fusion.2.at_ref, bf16[256,4096]{1,0:T(8,128)(2,1)S(1)} %bitcast.36, f32[1,4096]{1,0:T(1,128)S(1)} %bitcast.42), custom_call_target="tpu_custom_call" | custom-call | bytes 4194304 | tf_op jit(solution)/shard_map/norm_own/pallas_call | solution.py:272
  7.8 2.0 %collective-permute-start.2 = (s32[1]{0:T(128)}, s32[1]{0:T(128)}, u32[]{:S(2)}, u32[]{:S(2)}) collective-permute-start(s32[1]{0:T(128)} %param.17), channel_id=1, source_target_pairs={{0,1},{1,0},{2,3},{3,2},{4,5},{5,4},{6,7},{7,6},{8,9},{9,8},{10,11... | collective-permute-start | bytes 20 | tf_op jit(solution)/shard_map/ppermute | solution.py:46
  10.5 7.0 %collective-permute-done.2 = s32[1]{0:T(128)} collective-permute-done((s32[1]{0:T(128)}, s32[1]{0:T(128)}, u32[]{:S(2)}, u32[]{:S(2)}) %collective-permute-start.2) | collective-permute-done | bytes 36 | tf_op jit(solution)/shard_map/ppermute | solution.py:46
  18.1 0.6 add_select_fusion
  19.0 2.1 %collective-permute-done.3.b_ref = bf16[128,2048]{1,0:T(8,128)(2,1)S(1)} collective-permute-done((bf16[128,2048]{1,0:T(8,128)(2,1)}, bf16[128,2048]{1,0:T(8,128)(2,1)S(1)}, u32[]{:S(2)}, u32[]{:S(2)}) %collective-permute-start.3) | collective-permute-done | bytes 524320 | tf_op jit(solution)/shard_map/ppermute | solution.py:46
  21.0 5.7 %gate_up.1 = (bf16[192,1024]{1,0:T(8,128)(2,1)S(1)}, bf16[192,1024]{1,0:T(8,128)(2,1)S(1)}) custom-call(s32[2]{0:T(128)S(1)} %pad_add_fusion.2.at_ref, bf16[128,2048]{1,0:T(8,128)(2,1)} %collective-permute-done.a_hbm.a_ref, bf16[128,2048]{1,0:T(8,128)(2,1)S(1)} %collective-permute-done.3.b_ref, f32[1,256]{1,0:T(1,128)S(1)} %collective-permute-done.1.scale_ref, ...), custom_call_target="tpu_custom_call" | custom-call | flops 2147483648 | bytes 6291456 | tf_op jit(solution)/shard_map/gate_up/pallas_call | solution.py:326
  26.7 1.8 %collective-permute-start.4 = (bf16[192,1024]{1,0:T(8,128)(2,1)S(1)}, bf16[192,1024]{1,0:T(8,128)(2,1)S(1)}, u32[]{:S(2)}, u32[]{:S(2)}) collective-permute-start(bf16[192,1024]{1,0:T(8,128)(2,1)S(1)} %get-tuple-element.57.mine_ref), channel_id=1, source_target_pairs={{0,1},{1,0},{2,3},{3,2},{4,5},{5,4},{6,7},{7,6},{8,9},{9,8},{10,11... | collective-permute-start | bytes 1179656 | tf_op jit(solution)/shard_map/ppermute | solution.py:46
  28.5 0.3 collective-permute-start.17
  28.8 3.4 %pack_rows.1.pp_ref = bf16[384,2048]{1,0:T(8,128)(2,1)S(1)} custom-call(s32[2]{0:T(128)S(1)} %pad_add_fusion.2.at_ref, bf16[256,4096]{1,0:T(8,128)(2,1)} %bitcast.35, bf16[128,2048]{1,0:T(8,128)(2,1)} %collective-permute-done.a_hbm.a_ref, bf16[128,2048]{1,0:T(8,128)(2,1)S(1)} %collective-permute-done.3.b_ref, bf16[384,512]{1,0:T(8,128)(2,1)S(1)} %fusion.select_ref), custom_call_target="tpu_custom_call" | custom-call | flops 805306368 | bytes 3145728 | tf_op jit(solution)/shard_map/pack_rows/pallas_call | solution.py:360
  32.3 6.5 %collective-permute-done.4.got_ref = bf16[192,1024]{1,0:T(8,128)(2,1)S(1)} collective-permute-done((bf16[192,1024]{1,0:T(8,128)(2,1)S(1)}, bf16[192,1024]{1,0:T(8,128)(2,1)S(1)}, u32[]{:S(2)}, u32[]{:S(2)}) %collective-permute-start.4) | collective-permute-done | bytes 393248 | tf_op jit(solution)/shard_map/ppermute | solution.py:46
  38.8 2.2 %down_product.2 = (bf16[8,192,128]{2,1,0:T(8,128)(2,1)S(1)}, bf16[8,192,128]{2,1,0:T(8,128)(2,1)}) custom-call(s32[16]{0:T(128)S(1)} %broadcast_xor_fusion.idx_ref, bf16[192,1024]{1,0:T(8,128)(2,1)S(1)} %get-tuple-element.57.mine_ref, bf16[192,1024]{1,0:T(8,128)(2,1)S(1)} %collective-permute-done.4.got_ref, bf16[512,2048]{1,0:T(8,128)(2,1)S(1)} %copy-done.1), custom_call_target="tpu_custom_call" | custom-call | flops 402653184 | bytes 2883584 | tf_op jit(solution)/shard_map/down_product/pallas_call | solution.py:119
  41.0 5.4 %collective-permute-done.17.got_ref = bf16[192,1024]{1,0:T(8,128)(2,1)S(1)} collective-permute-done((bf16[192,1024]{1,0:T(8,128)(2,1)S(1)}, bf16[192,1024]{1,0:T(8,128)(2,1)S(1)}, u32[]{:S(2)}, u32[]{:S(2)}) %collective-permute-start.17) | collective-permute-done | bytes 393248 | tf_op jit(solution)/shard_map/ppermute | solution.py:46
  46.4 2.2 %down_product.3 = (bf16[8,192,128]{2,1,0:T(8,128)(2,1)S(1)}, bf16[8,192,128]{2,1,0:T(8,128)(2,1)}) custom-call(s32[16]{0:T(128)S(1)} %broadcast_xor_fusion.idx_ref, bf16[192,1024]{1,0:T(8,128)(2,1)S(1)} %get-tuple-element.61.mine_ref, bf16[192,1024]{1,0:T(8,128)(2,1)S(1)} %collective-permute-done.17.got_ref, bf16[512,2048]{1,0:T(8,128)(2,1)S(1)} %copy-done.1), custom_call_target="tpu_custom_call" | custom-call | flops 402653184 | bytes 2883584 | tf_op jit(solution)/shard_map/down_product/pallas_call | solution.py:119
  48.6 1.2 pack_heads.1
  49.8 6.2 %all-to-all-start = ((bf16[16,192,128]{2,1,0:T(8,128)(2,1)}), bf16[16,192,128]{2,1,0:T(8,128)(2,1)S(1)}, u32[]{:S(2)}, u32[]{:S(2)}) async-start(bf16[16,192,128]{2,1,0:T(8,128)(2,1)} %pack_heads.1), calls=%async_computation | async-start | bytes 1572864 | tf_op jit(solution)/shard_map/all_to_all | solution.py:77
  56.1 2.5 %corner.3 = bf16[256,1280]{1,0:T(8,128)(2,1)} custom-call(s32[2]{0:T(128)S(1)} %pad_add_fusion.4.at_ref, bf16[512,1280]{1,0:T(8,128)(2,1)} %refs_0_.1), custom_call_target="tpu_custom_call" | custom-call | bytes 1310720 | tf_op jit(solution)/shard_map/corner/pallas_call | solution.py:234
  58.6 1.6 collective-permute-start.30
  60.2 1.1 add_convert_fusion.3
  61.3 2.0 %collective-permute-start.6 = (bf16[4,192,128]{2,1,0:T(8,128)(2,1)S(1)}, bf16[4,192,128]{2,1,0:T(8,128)(2,1)S(1)}, u32[]{:S(2)}, u32[]{:S(2)}) collective-permute-start(bf16[4,192,128]{2,1,0:T(8,128)(2,1)S(1)} %get-tuple-element.85), channel_id=1, source_target_pairs={{0,4},{2,6},{4,0},{6,2},{8,12},{10,14},{12,8},{14,10},{16,20},{18,... | collective-permute-start | bytes 589832 | tf_op jit(solution)/shard_map/ppermute | solution.py:46
  63.3 1.1 add_convert_fusion.1
  64.6 6.6 %collective-permute-done.6 = bf16[4,192,128]{2,1,0:T(8,128)(2,1)S(1)} collective-permute-done((bf16[4,192,128]{2,1,0:T(8,128)(2,1)S(1)}, bf16[4,192,128]{2,1,0:T(8,128)(2,1)S(1)}, u32[]{:S(2)}, u32[]{:S(2)}) %collective-permute-start.6) | collective-permute-done | bytes 196640 | tf_op jit(solution)/shard_map/ppermute | solution.py:46
  71.3 3.9 %collective-permute-start.9 = (bf16[1,192,128]{2,1,0:T(8,128)(2,1)S(1)}, bf16[1,192,128]{2,1,0:T(8,128)(2,1)S(1)}, u32[]{:S(2)}, u32[]{:S(2)}) collective-permute-start(bf16[1,192,128]{2,1,0:T(8,128)(2,1)S(1)} %get-tuple-element.90), channel_id=1, source_target_pairs={{0,24},{2,26},{4,28},{6,30},{8,16},{10,18},{12,20},{14,22},{16,8},... | collective-permute-start | bytes 147464 | tf_op jit(solution)/shard_map/ppermute | solution.py:46
  75.1 0.7 collective-permute-start.8
  75.9 1.0 collective-permute-done.19
  76.9 2.9 %collective-permute-start.22 = (bf16[1,192,128]{2,1,0:T(8,128)(2,1)S(1)}, bf16[1,192,128]{2,1,0:T(8,128)(2,1)S(1)}, u32[]{:S(2)}, u32[]{:S(2)}) collective-permute-start(bf16[1,192,128]{2,1,0:T(8,128)(2,1)S(1)} %get-tuple-element.87), channel_id=1, source_target_pairs={{0,24},{2,26},{4,28},{6,30},{8,16},{10,18},{12,20},{14,22},{16,8},... | collective-permute-start | bytes 147464 | tf_op jit(solution)/shard_map/ppermute | solution.py:46
  79.7 1.5 collective-permute-start.21
  81.2 0.6 collective-permute-done.8
  81.8 2.4 %collective-permute-start.12 = (bf16[1,192,128]{2,1,0:T(8,128)(2,1)S(1)}, bf16[1,192,128]{2,1,0:T(8,128)(2,1)S(1)}, u32[]{:S(2)}, u32[]{:S(2)}) collective-permute-start(bf16[1,192,128]{2,1,0:T(8,128)(2,1)S(1)} %add_convert_fusion.9), channel_id=1, source_target_pairs={{0,24},{2,26},{4,28},{6,30},{8,16},{10,18},{12,20},{14,22},{16,8},... | collective-permute-start | bytes 147464 | tf_op jit(solution)/shard_map/ppermute | solution.py:46
  84.2 1.3 collective-permute-start.11
  85.5 1.5 collective-permute-done.21
  87.1 2.1 %collective-permute-start.25 = (bf16[1,192,128]{2,1,0:T(8,128)(2,1)S(1)}, bf16[1,192,128]{2,1,0:T(8,128)(2,1)S(1)}, u32[]{:S(2)}, u32[]{:S(2)}) collective-permute-start(bf16[1,192,128]{2,1,0:T(8,128)(2,1)S(1)} %add_convert_fusion.4), channel_id=1, source_target_pairs={{0,24},{2,26},{4,28},{6,30},{8,16},{10,18},{12,20},{14,22},{16,8},... | collective-permute-start | bytes 147464 | tf_op jit(solution)/shard_map/ppermute | solution.py:46
  89.2 1.5 collective-permute-start.24
  90.6 0.7 collective-permute-done.11
  91.5 0.4 collective-permute-done.10
  92.0 1.6 collective-permute-start.13
  93.6 0.6 collective-permute-done.24
  94.1 1.3 collective-permute-done.23
  95.4 0.7 pad_maximum_fusion.1.refs_0_
  96.1 1.6 collective-permute-start.26
  97.7 1.9 %collective-permute-done.13.refs_1_ = bf16[4,192,128]{2,1,0:T(8,128)(2,1)} collective-permute-done((bf16[4,192,128]{2,1,0:T(8,128)(2,1)S(1)}, bf16[4,192,128]{2,1,0:T(8,128)(2,1)}, u32[]{:S(2)}, u32[]{:S(2)}) %collective-permute-start.13) | collective-permute-done | bytes 196640 | tf_op jit(solution)/shard_map/ppermute | solution.py:46
  99.6 0.5 collective-permute-start.27
  100.1 2.0 %collective-permute-done.26.refs_1_ = bf16[4,192,128]{2,1,0:T(8,128)(2,1)} collective-permute-done((bf16[4,192,128]{2,1,0:T(8,128)(2,1)}, bf16[4,192,128]{2,1,0:T(8,128)(2,1)}, u32[]{:S(2)}, u32[]{:S(2)}) %collective-permute-start.26) | collective-permute-done | bytes 196640 | tf_op jit(solution)/shard_map/ppermute | solution.py:46
  102.1 0.7 dynamic_slice.3
  102.8 0.5 collective-permute-start.31
  103.3 4.0 %image_part.2 = (bf16[2,1024,1024]{2,1,0:T(8,128)(2,1)}, f32[1024,128]{1,0:T(8,128)}, f32[1024,128]{1,0:T(8,128)}, f32[1024,128]{1,0:T(8,128)}) custom-call(bf16[16,3,64,128]{3,2,1,0:T(8,128)(2,1)S(1)} %bitcast.24, bf16[16,3,64,128]{3,2,1,0:T(8,128)(2,1)S(1)} %bitcast.25, bf16[16,3,64,128]{3,2,1,0:T(8,128)(2,1)S(1)} %bitcast.26), custom_call_target="tpu_custom_call" | custom-call | flops 1073741824 | bytes 786432 | tf_op jit(solution)/shard_map/image_part/pallas_call | solution.py:544
  107.4 1.6 context_product.2.refs_0_
  109.0 2.3 %collective-permute-start.16 = (bf16[200,128]{1,0:T(8,128)(2,1)S(1)}, bf16[200,128]{1,0:T(8,128)(2,1)S(1)}, u32[]{:S(2)}, u32[]{:S(2)}) collective-permute-start(bf16[200,128]{1,0:T(8,128)(2,1)S(1)} %context_product.2.refs_0_), channel_id=1, source_target_pairs={{0,1},{1,0},{2,3},{3,2},{4,5},{5,4},{6,7},{7,6},{8,9},{9,8},{10,11... | collective-permute-start | bytes 153608 | tf_op jit(solution)/shard_map/ppermute | solution.py:46
  111.3 1.7 %context_product.3.refs_2_ = bf16[200,128]{1,0:T(8,128)(2,1)S(1)} custom-call(s32[16]{0:T(128)S(1)} %broadcast_xor_fusion.idx_ref, bf16[384,2048]{1,0:T(8,128)(2,1)S(1)} %pack_rows.1.pp_ref, f32[1,2048]{1,0:T(1,128)S(1)} %bitcast.41, bf16[2048,128]{1,0:T(8,128)(2,1)S(1)} %copy-done.2, bf16[4,192,128]{2,1,0:T(8,128)(2,1)} %pad_maximum_fusion.1.refs_0_, ...), custom_call_target="tpu_custom_call" | custom-call | flops 100663296 | bytes 1310720 | tf_op jit(solution)/shard_map/context_product/pallas_call | solution.py:175
  113.1 4.1 %image_part.3 = (bf16[2,1024,1024]{2,1,0:T(8,128)(2,1)}, f32[1024,128]{1,0:T(8,128)}, f32[1024,128]{1,0:T(8,128)}, f32[1024,128]{1,0:T(8,128)}) custom-call(bf16[16,3,64,128]{3,2,1,0:T(8,128)(2,1)S(1)} %bitcast.27, bf16[16,3,64,128]{3,2,1,0:T(8,128)(2,1)S(1)} %bitcast.28, ...), custom_call_target="tpu_custom_call", output_to_operand_aliasing={{0}: (3, {}), {1}: (4, {}), {2}: (5, {}), {3}: (6, {})} | custom-call | flops 1073741824 | bytes 786432 | tf_op jit(solution)/shard_map/image_part/pallas_call | solution.py:544
  117.2 0.4 finish_context.1.ctx_ref
  117.6 5.0 %text_part.1 = (bf16[16,64,128]{2,1,0:T(8,128)(2,1)}, bf16[2,1024,256]{2,1,0:T(8,128)(2,1)}, f32[1024,128]{1,0:T(8,128)}, f32[1024,128]{1,0:T(8,128)}) custom-call(s32[1]{0:T(128)} %copy.28.len_ref, bf16[16,3,64,128]{3,2,1,0:T(8,128)(2,1)S(1)} %bitcast.30, bf16[256,128]{1,0:T(8,128)(2,1)S(1)} %finish_context.1.ctx_ref, f32[1024,128]{1,0:T(8,128)} %get-tuple-element.68.o_ref, ...), custom_call_target="tpu_custom_call" | custom-call | flops 536870912 | bytes 1572864 | tf_op jit(solution)/shard_map/text_part/pallas_call | solution.py:608
  122.6 4.2 %all-to-all-start.1 = ((bf16[16,64,128]{2,1,0:T(8,128)(2,1)}), bf16[16,64,128]{2,1,0:T(8,128)(2,1)}, u32[]{:S(2)}, u32[]{:S(2)}) async-start(bf16[16,64,128]{2,1,0:T(8,128)(2,1)} %get-tuple-element.71.o_ref), calls=%async_computation.1 | async-start | bytes 524288 | tf_op jit(solution)/shard_map/all_to_all | solution.py:77
  126.9 1.8 %load_weights.1 = (bf16[2,64,1280]{2,1,0:T(8,128)(2,1)S(1)}, bf16[4,256,1280]{2,1,0:T(8,128)(2,1)S(1)}) custom-call(bf16[2,64,1280]{2,1,0:T(8,128)(2,1)} %bitcast.44, bf16[512,1280]{1,0:T(8,128)(2,1)} %refs_0_.1, bf16[256,1280]{1,0:T(8,128)(2,1)} %collective-permute-done.30.refs_1_, bf16[256,1280]{1,0:T(8,128)(2,1)} %collective-permute-done.31.refs_2_), custom_call_target="tpu_custom_call" | custom-call | bytes 5898240 | tf_op jit(solution)/shard_map/load_weights/pallas_call | solution.py:655
  128.7 0.7 copy-done.4
  129.4 7.4 %all-to-all-done.1.o_ref = bf16[16,64,128]{2,1,0:T(8,128)(2,1)} async-done(((bf16[16,64,128]{2,1,0:T(8,128)(2,1)}), bf16[16,64,128]{2,1,0:T(8,128)(2,1)}, u32[]{:S(2)}, u32[]{:S(2)}) %all-to-all-start.1) | async-done | bytes 262176 | tf_op jit(solution)/shard_map/all_to_all | solution.py:77
  136.8 1.0 copy-done.5
  137.8 2.5 %project.1 = bf16[16,72,128]{2,1,0:T(8,128)(2,1)S(1)} custom-call(s32[4]{0:T(128)S(1)} %pad_add_fusion.1.idx_ref, bf16[16,64,128]{2,1,0:T(8,128)(2,1)} %all-to-all-done.1.o_ref, bf16[2,64,1280]{2,1,0:T(8,128)(2,1)S(1)} %copy-done.5, bf16[4,256,1280]{2,1,0:T(8,128)(2,1)S(1)} %get-tuple-element.73.w_ref), custom_call_target="tpu_custom_call" | custom-call | flops 671088640 | bytes 3473408 | tf_op jit(solution)/shard_map/project/pallas_call | solution.py:710
  140.2 0.7 copy-done.3
  141.0 3.5 %all-to-all-start.2 = ((bf16[16,72,128]{2,1,0:T(8,128)(2,1)}), bf16[16,72,128]{2,1,0:T(8,128)(2,1)S(1)}, u32[]{:S(2)}, u32[]{:S(2)}) async-start(bf16[16,72,128]{2,1,0:T(8,128)(2,1)} %copy-done.3), calls=%async_computation.2 | async-start | bytes 589824 | tf_op jit(solution)/shard_map/all_to_all | solution.py:77
  145.2 9.9 %all-to-all-done.2.err_ref.g_ref = bf16[16,72,128]{2,1,0:T(8,128)(2,1)S(1)} async-done(((bf16[16,72,128]{2,1,0:T(8,128)(2,1)}), bf16[16,72,128]{2,1,0:T(8,128)(2,1)S(1)}, u32[]{:S(2)}, u32[]{:S(2)}) %all-to-all-start.2) | async-done | bytes 294944 | tf_op jit(solution)/shard_map/all_to_all | solution.py:77
  155.0 0.9 copy-done.6
  156.0 9.0 %backward_part.1 = (f32[1,128]{1,0:T(1,128)}, bf16[1,2,64,1024]{3,2,1,0:T(8,128)(2,1)}, bf16[1,2,64,1024]{3,2,1,0:T(8,128)(2,1)}, bf16[1,2,64,1024]{3,2,1,0:T(8,128)(2,1)}) custom-call(bf16[16,72,128]{2,1,0:T(8,128)(2,1)S(1)} %all-to-all-done.2.err_ref.g_ref, s32[1]{0:T(128)S(6)} %copy.29.step_ref, f32[1,2]{1,0:T(1,128)S(1)} %copy-done.11, ...), custom_call_target="tpu_custom_call" | custom-call | flops 5368709120 | bytes 6029312 | tf_op jit(solution)/shard_map/backward_part/pallas_call | solution.py:813
  (68 shorter events, 1.3 us)
Async XLA Ops:
  0.6 4.8 %copy-start = (bf16[1,256,4096]{2,1,0:T(8,128)(2,1)S(1)}, bf16[1,256,4096]{2,1,0:T(8,128)(2,1)}, u32[]{:S(2)}) copy-start(bf16[1,256,4096]{2,1,0:T(8,128)(2,1)} %param.16) | copy-start | bytes 6291460
  0.6 4.8 %copy-start.10 = (f32[4096]{0:T(1024)S(1)}, f32[4096]{0:T(1024)}, u32[]{:S(2)}) copy-start(f32[4096]{0:T(1024)} %param.20) | copy-start | bytes 49156
  2.3 16.5 %collective-permute-start = (bf16[128,2048]{1,0:T(8,128)(2,1)S(1)}, bf16[128,2048]{1,0:T(8,128)(2,1)}, u32[]{:S(2)}, u32[]{:S(2)}) collective-permute-start(bf16[128,2048]{1,0:T(8,128)(2,1)S(1)} %corner.2), channel_id=1, source_target_pairs={{0,1},{1,0},{2,3},{3,2},{4,5},{5,4},{6,7},{7,6},{8,9},{9,8},{10,11... | collective-permute-start | bytes 1572872 | tf_op jit(solution)/shard_map/ppermute | solution.py:46
  7.7 11.1 %collective-permute-start.1 = (f32[1,256]{1,0:T(1,128)S(1)}, f32[1,256]{1,0:T(1,128)S(1)}, u32[]{:S(2)}, u32[]{:S(2)}) collective-permute-start(f32[1,256]{1,0:T(1,128)S(1)} %get-tuple-element.48), channel_id=1, source_target_pairs={{0,1},{1,0},{2,3},{3,2},{4,5},{5,4},{6,7},{7,6},{8,9},{9,8},{10,11... | collective-permute-start | bytes 3080 | tf_op jit(solution)/shard_map/ppermute | solution.py:46
  7.8 9.7 %collective-permute-start.2 = (s32[1]{0:T(128)}, s32[1]{0:T(128)}, u32[]{:S(2)}, u32[]{:S(2)}) collective-permute-start(s32[1]{0:T(128)} %param.17), channel_id=1, source_target_pairs={{0,1},{1,0},{2,3},{3,2},{4,5},{5,4},{6,7},{7,6},{8,9},{9,8},{10,11... | collective-permute-start | bytes 20 | tf_op jit(solution)/shard_map/ppermute | solution.py:46
  18.9 2.2 %collective-permute-start.3 = (bf16[128,2048]{1,0:T(8,128)(2,1)}, bf16[128,2048]{1,0:T(8,128)(2,1)S(1)}, u32[]{:S(2)}, u32[]{:S(2)}) collective-permute-start(bf16[128,2048]{1,0:T(8,128)(2,1)} %collective-permute-done.a_hbm.a_ref), channel_id=1, source_target_pairs={{0,2},{2,0},{4,6},{6,4},{8,10},{10,8},{12,14},{14,12},{16,18},{18,... | collective-permute-start | bytes 1572872 | tf_op jit(solution)/shard_map/ppermute | solution.py:46
  18.9 9.9 %copy-start.12 = (s32[16]{0:T(128)S(1)}, s32[16]{0:T(128)}, u32[]{:S(2)}) copy-start(s32[16]{0:T(128)} %constant.29.clone) | copy-start | bytes 196
  26.7 12.1 %collective-permute-start.4 = (bf16[192,1024]{1,0:T(8,128)(2,1)S(1)}, bf16[192,1024]{1,0:T(8,128)(2,1)S(1)}, u32[]{:S(2)}, u32[]{:S(2)}) collective-permute-start(bf16[192,1024]{1,0:T(8,128)(2,1)S(1)} %get-tuple-element.57.mine_ref), channel_id=1, source_target_pairs={{0,1},{1,0},{2,3},{3,2},{4,5},{5,4},{6,7},{7,6},{8,9},{9,8},{10,11... | collective-permute-start | bytes 1179656 | tf_op jit(solution)/shard_map/ppermute | solution.py:46
  28.5 17.8 %collective-permute-start.17 = (bf16[192,1024]{1,0:T(8,128)(2,1)S(1)}, bf16[192,1024]{1,0:T(8,128)(2,1)S(1)}, u32[]{:S(2)}, u32[]{:S(2)}) collective-permute-start(bf16[192,1024]{1,0:T(8,128)(2,1)S(1)} %get-tuple-element.61.mine_ref), channel_id=1, source_target_pairs={{0,1},{1,0},{2,3},{3,2},{4,5},{5,4},{6,7},{7,6},{8,9},{9,8},{10,11... | collective-permute-start | bytes 1179656 | tf_op jit(solution)/shard_map/ppermute | solution.py:46
  28.8 10.0 %copy-start.1 = (bf16[512,2048]{1,0:T(8,128)(2,1)S(1)}, bf16[512,2048]{1,0:T(8,128)(2,1)}, u32[]{:S(2)}) copy-start(bf16[512,2048]{1,0:T(8,128)(2,1)} %w_ref.6) | copy-start | bytes 6291460
  41.0 7.6 %copy-start.7 = (bf16[1,2,64,1024]{3,2,1,0:T(8,128)(2,1)S(1)}, bf16[1,2,64,1024]{3,2,1,0:T(8,128)(2,1)}, u32[]{:S(2)}) copy-start(bf16[1,2,64,1024]{3,2,1,0:T(8,128)(2,1)} %param.26) | copy-start | bytes 786436
  41.0 7.6 %copy-start.8 = (bf16[1,2,64,1024]{3,2,1,0:T(8,128)(2,1)S(1)}, bf16[1,2,64,1024]{3,2,1,0:T(8,128)(2,1)}, u32[]{:S(2)}) copy-start(bf16[1,2,64,1024]{3,2,1,0:T(8,128)(2,1)} %param.27) | copy-start | bytes 786436
  41.0 7.6 %copy-start.9 = (bf16[1,2,64,1024]{3,2,1,0:T(8,128)(2,1)S(1)}, bf16[1,2,64,1024]{3,2,1,0:T(8,128)(2,1)}, u32[]{:S(2)}) copy-start(bf16[1,2,64,1024]{3,2,1,0:T(8,128)(2,1)} %param.28) | copy-start | bytes 786436
  41.0 19.2 %collective-permute-start.5 = (bf16[8,192,128]{2,1,0:T(8,128)(2,1)}, bf16[8,192,128]{2,1,0:T(8,128)(2,1)}, u32[]{:S(2)}, u32[]{:S(2)}) collective-permute-start(bf16[8,192,128]{2,1,0:T(8,128)(2,1)} %get-tuple-element.60), channel_id=1, source_target_pairs={{0,2},{2,0},{4,6},{6,4},{8,10},{10,8},{12,14},{14,12},{16,18},{18,... | collective-permute-start | bytes 1179656 | tf_op jit(solution)/shard_map/ppermute | solution.py:46
  48.6 14.7 %collective-permute-start.18 = (bf16[8,192,128]{2,1,0:T(8,128)(2,1)}, bf16[8,192,128]{2,1,0:T(8,128)(2,1)}, u32[]{:S(2)}, u32[]{:S(2)}) collective-permute-start(bf16[8,192,128]{2,1,0:T(8,128)(2,1)} %get-tuple-element.63), channel_id=1, source_target_pairs={{0,2},{2,0},{4,6},{6,4},{8,10},{10,8},{12,14},{14,12},{16,18},{18,... | collective-permute-start | bytes 1179656 | tf_op jit(solution)/shard_map/ppermute | solution.py:46
  49.8 53.5 %all-to-all-start = ((bf16[16,192,128]{2,1,0:T(8,128)(2,1)}), bf16[16,192,128]{2,1,0:T(8,128)(2,1)S(1)}, u32[]{:S(2)}, u32[]{:S(2)}) async-start(bf16[16,192,128]{2,1,0:T(8,128)(2,1)} %pack_heads.1), calls=%async_computation | async-start | bytes 1572864 | tf_op jit(solution)/shard_map/all_to_all | solution.py:77
  58.6 44.2 %collective-permute-start.30 = (bf16[256,1280]{1,0:T(8,128)(2,1)}, bf16[256,1280]{1,0:T(8,128)(2,1)}, u32[]{:S(2)}, u32[]{:S(2)}) collective-permute-start(bf16[256,1280]{1,0:T(8,128)(2,1)} %corner.3), channel_id=1, source_target_pairs={{0,1},{1,0},{2,3},{3,2},{4,5},{5,4},{6,7},{7,6},{8,9},{9,8},{10,11... | collective-permute-start | bytes 1966088 | tf_op jit(solution)/shard_map/ppermute | solution.py:46
  61.3 9.9 %collective-permute-start.6 = (bf16[4,192,128]{2,1,0:T(8,128)(2,1)S(1)}, bf16[4,192,128]{2,1,0:T(8,128)(2,1)S(1)}, u32[]{:S(2)}, u32[]{:S(2)}) collective-permute-start(bf16[4,192,128]{2,1,0:T(8,128)(2,1)S(1)} %get-tuple-element.85), channel_id=1, source_target_pairs={{0,4},{2,6},{4,0},{6,2},{8,12},{10,14},{12,8},{14,10},{16,20},{18,... | collective-permute-start | bytes 589832 | tf_op jit(solution)/shard_map/ppermute | solution.py:46
  64.5 12.4 %collective-permute-start.19 = (bf16[4,192,128]{2,1,0:T(8,128)(2,1)S(1)}, bf16[4,192,128]{2,1,0:T(8,128)(2,1)S(1)}, u32[]{:S(2)}, u32[]{:S(2)}) collective-permute-start(bf16[4,192,128]{2,1,0:T(8,128)(2,1)S(1)} %get-tuple-element.83), channel_id=1, source_target_pairs={{0,4},{2,6},{4,0},{6,2},{8,12},{10,14},{12,8},{14,10},{16,20},{18,... | collective-permute-start | bytes 589832 | tf_op jit(solution)/shard_map/ppermute | solution.py:46
  71.3 8.5 %collective-permute-start.9 = (bf16[1,192,128]{2,1,0:T(8,128)(2,1)S(1)}, bf16[1,192,128]{2,1,0:T(8,128)(2,1)S(1)}, u32[]{:S(2)}, u32[]{:S(2)}) collective-permute-start(bf16[1,192,128]{2,1,0:T(8,128)(2,1)S(1)} %get-tuple-element.90), channel_id=1, source_target_pairs={{0,24},{2,26},{4,28},{6,30},{8,16},{10,18},{12,20},{14,22},{16,8},... | collective-permute-start | bytes 147464 | tf_op jit(solution)/shard_map/ppermute | solution.py:46
  75.1 6.6 %collective-permute-start.8 = (bf16[1,192,128]{2,1,0:T(8,128)(2,1)S(1)}, bf16[1,192,128]{2,1,0:T(8,128)(2,1)S(1)}, u32[]{:S(2)}, u32[]{:S(2)}) collective-permute-start(bf16[1,192,128]{2,1,0:T(8,128)(2,1)S(1)} %get-tuple-element.91), channel_id=1, source_target_pairs={{0,16},{2,18},{4,20},{6,22},{8,24},{10,26},{12,28},{14,30},{16,0},... | collective-permute-start | bytes 147464 | tf_op jit(solution)/shard_map/ppermute | solution.py:46
  75.9 5.9 %collective-permute-start.7 = (bf16[1,192,128]{2,1,0:T(8,128)(2,1)S(1)}, bf16[1,192,128]{2,1,0:T(8,128)(2,1)S(1)}, u32[]{:S(2)}, u32[]{:S(2)}) collective-permute-start(bf16[1,192,128]{2,1,0:T(8,128)(2,1)S(1)} %get-tuple-element.89), channel_id=1, source_target_pairs={{0,8},{2,10},{4,12},{6,14},{8,0},{10,2},{12,4},{14,6},{16,24},{18,... | collective-permute-start | bytes 147464 | tf_op jit(solution)/shard_map/ppermute | solution.py:46
  76.9 7.4 %collective-permute-start.22 = (bf16[1,192,128]{2,1,0:T(8,128)(2,1)S(1)}, bf16[1,192,128]{2,1,0:T(8,128)(2,1)S(1)}, u32[]{:S(2)}, u32[]{:S(2)}) collective-permute-start(bf16[1,192,128]{2,1,0:T(8,128)(2,1)S(1)} %get-tuple-element.87), channel_id=1, source_target_pairs={{0,24},{2,26},{4,28},{6,30},{8,16},{10,18},{12,20},{14,22},{16,8},... | collective-permute-start | bytes 147464 | tf_op jit(solution)/shard_map/ppermute | solution.py:46
  79.7 7.3 %collective-permute-start.21 = (bf16[1,192,128]{2,1,0:T(8,128)(2,1)S(1)}, bf16[1,192,128]{2,1,0:T(8,128)(2,1)S(1)}, u32[]{:S(2)}, u32[]{:S(2)}) collective-permute-start(bf16[1,192,128]{2,1,0:T(8,128)(2,1)S(1)} %get-tuple-element.88), channel_id=1, source_target_pairs={{0,16},{2,18},{4,20},{6,22},{8,24},{10,26},{12,28},{14,30},{16,0},... | collective-permute-start | bytes 147464 | tf_op jit(solution)/shard_map/ppermute | solution.py:46
  81.7 5.3 %collective-permute-start.20 = (bf16[1,192,128]{2,1,0:T(8,128)(2,1)S(1)}, bf16[1,192,128]{2,1,0:T(8,128)(2,1)S(1)}, u32[]{:S(2)}, u32[]{:S(2)}) collective-permute-start(bf16[1,192,128]{2,1,0:T(8,128)(2,1)S(1)} %get-tuple-element.86), channel_id=1, source_target_pairs={{0,8},{2,10},{4,12},{6,14},{8,0},{10,2},{12,4},{14,6},{16,24},{18,... | collective-permute-start | bytes 147464 | tf_op jit(solution)/shard_map/ppermute | solution.py:46
  81.8 7.4 %collective-permute-start.12 = (bf16[1,192,128]{2,1,0:T(8,128)(2,1)S(1)}, bf16[1,192,128]{2,1,0:T(8,128)(2,1)S(1)}, u32[]{:S(2)}, u32[]{:S(2)}) collective-permute-start(bf16[1,192,128]{2,1,0:T(8,128)(2,1)S(1)} %add_convert_fusion.9), channel_id=1, source_target_pairs={{0,24},{2,26},{4,28},{6,30},{8,16},{10,18},{12,20},{14,22},{16,8},... | collective-permute-start | bytes 147464 | tf_op jit(solution)/shard_map/ppermute | solution.py:46
  84.2 7.1 %collective-permute-start.11 = (bf16[1,192,128]{2,1,0:T(8,128)(2,1)S(1)}, bf16[1,192,128]{2,1,0:T(8,128)(2,1)S(1)}, u32[]{:S(2)}, u32[]{:S(2)}) collective-permute-start(bf16[1,192,128]{2,1,0:T(8,128)(2,1)S(1)} %add_convert_fusion.9), channel_id=1, source_target_pairs={{0,16},{2,18},{4,20},{6,22},{8,24},{10,26},{12,28},{14,30},{16,0},... | collective-permute-start | bytes 147464 | tf_op jit(solution)/shard_map/ppermute | solution.py:46
  87.0 4.9 %collective-permute-start.10 = (bf16[1,192,128]{2,1,0:T(8,128)(2,1)S(1)}, bf16[1,192,128]{2,1,0:T(8,128)(2,1)S(1)}, u32[]{:S(2)}, u32[]{:S(2)}) collective-permute-start(bf16[1,192,128]{2,1,0:T(8,128)(2,1)S(1)} %add_convert_fusion.9), channel_id=1, source_target_pairs={{0,8},{2,10},{4,12},{6,14},{8,0},{10,2},{12,4},{14,6},{16,24},{18,... | collective-permute-start | bytes 147464 | tf_op jit(solution)/shard_map/ppermute | solution.py:46
  87.1 6.5 %collective-permute-start.25 = (bf16[1,192,128]{2,1,0:T(8,128)(2,1)S(1)}, bf16[1,192,128]{2,1,0:T(8,128)(2,1)S(1)}, u32[]{:S(2)}, u32[]{:S(2)}) collective-permute-start(bf16[1,192,128]{2,1,0:T(8,128)(2,1)S(1)} %add_convert_fusion.4), channel_id=1, source_target_pairs={{0,24},{2,26},{4,28},{6,30},{8,16},{10,18},{12,20},{14,22},{16,8},... | collective-permute-start | bytes 147464 | tf_op jit(solution)/shard_map/ppermute | solution.py:46
  89.2 5.0 %collective-permute-start.24 = (bf16[1,192,128]{2,1,0:T(8,128)(2,1)S(1)}, bf16[1,192,128]{2,1,0:T(8,128)(2,1)S(1)}, u32[]{:S(2)}, u32[]{:S(2)}) collective-permute-start(bf16[1,192,128]{2,1,0:T(8,128)(2,1)S(1)} %add_convert_fusion.4), channel_id=1, source_target_pairs={{0,16},{2,18},{4,20},{6,22},{8,24},{10,26},{12,28},{14,30},{16,0},... | collective-permute-start | bytes 147464 | tf_op jit(solution)/shard_map/ppermute | solution.py:46
  91.3 4.1 %collective-permute-start.23 = (bf16[1,192,128]{2,1,0:T(8,128)(2,1)S(1)}, bf16[1,192,128]{2,1,0:T(8,128)(2,1)S(1)}, u32[]{:S(2)}, u32[]{:S(2)}) collective-permute-start(bf16[1,192,128]{2,1,0:T(8,128)(2,1)S(1)} %add_convert_fusion.4), channel_id=1, source_target_pairs={{0,8},{2,10},{4,12},{6,14},{8,0},{10,2},{12,4},{14,6},{16,24},{18,... | collective-permute-start | bytes 147464 | tf_op jit(solution)/shard_map/ppermute | solution.py:46
  92.0 7.6 %collective-permute-start.13 = (bf16[4,192,128]{2,1,0:T(8,128)(2,1)S(1)}, bf16[4,192,128]{2,1,0:T(8,128)(2,1)}, u32[]{:S(2)}, u32[]{:S(2)}) collective-permute-start(bf16[4,192,128]{2,1,0:T(8,128)(2,1)S(1)} %pad_maximum_fusion.refs_0_), channel_id=1, source_target_pairs={{0,4},{2,6},{4,0},{6,2},{8,12},{10,14},{12,8},{14,10},{16,20},{18,... | collective-permute-start | bytes 589832 | tf_op jit(solution)/shard_map/ppermute | solution.py:46
  96.1 11.2 %copy-start.2 = (bf16[2048,128]{1,0:T(8,128)(2,1)S(1)}, bf16[2048,128]{1,0:T(8,128)(2,1)}, u32[]{:S(2)}) copy-start(bf16[2048,128]{1,0:T(8,128)(2,1)} %w_ref.7) | copy-start | bytes 1572868
  96.1 6.0 %collective-permute-start.26 = (bf16[4,192,128]{2,1,0:T(8,128)(2,1)}, bf16[4,192,128]{2,1,0:T(8,128)(2,1)}, u32[]{:S(2)}, u32[]{:S(2)}) collective-permute-start(bf16[4,192,128]{2,1,0:T(8,128)(2,1)} %pad_maximum_fusion.1.refs_0_), channel_id=1, source_target_pairs={{0,4},{2,6},{4,0},{6,2},{8,12},{10,14},{12,8},{14,10},{16,20},{18,... | collective-permute-start | bytes 589832 | tf_op jit(solution)/shard_map/ppermute | solution.py:46
  97.7 9.6 %collective-permute-start.14 = (bf16[4,192,128]{2,1,0:T(8,128)(2,1)S(1)}, bf16[4,192,128]{2,1,0:T(8,128)(2,1)}, u32[]{:S(2)}, u32[]{:S(2)}) collective-permute-start(bf16[4,192,128]{2,1,0:T(8,128)(2,1)S(1)} %pad_maximum_fusion.refs_0_), channel_id=1, source_target_pairs={{0,2},{2,0},{4,6},{6,4},{8,10},{10,8},{12,14},{14,12},{16,18},{18,... | collective-permute-start | bytes 589832 | tf_op jit(solution)/shard_map/ppermute | solution.py:46
  99.6 7.8 %collective-permute-start.15 = (bf16[4,192,128]{2,1,0:T(8,128)(2,1)}, bf16[4,192,128]{2,1,0:T(8,128)(2,1)}, u32[]{:S(2)}, u32[]{:S(2)}) collective-permute-start(bf16[4,192,128]{2,1,0:T(8,128)(2,1)} %collective-permute-done.13.refs_1_), channel_id=1, source_target_pairs={{0,2},{2,0},{4,6},{6,4},{8,10},{10,8},{12,14},{14,12},{16,18},{18,... | collective-permute-start | bytes 589832 | tf_op jit(solution)/shard_map/ppermute | solution.py:46
  99.6 11.7 %collective-permute-start.27 = (bf16[4,192,128]{2,1,0:T(8,128)(2,1)}, bf16[4,192,128]{2,1,0:T(8,128)(2,1)}, u32[]{:S(2)}, u32[]{:S(2)}) collective-permute-start(bf16[4,192,128]{2,1,0:T(8,128)(2,1)} %pad_maximum_fusion.1.refs_0_), channel_id=1, source_target_pairs={{0,2},{2,0},{4,6},{6,4},{8,10},{10,8},{12,14},{14,12},{16,18},{18,... | collective-permute-start | bytes 589832 | tf_op jit(solution)/shard_map/ppermute | solution.py:46
  102.1 9.2 %collective-permute-start.28 = (bf16[4,192,128]{2,1,0:T(8,128)(2,1)}, bf16[4,192,128]{2,1,0:T(8,128)(2,1)}, u32[]{:S(2)}, u32[]{:S(2)}) collective-permute-start(bf16[4,192,128]{2,1,0:T(8,128)(2,1)} %collective-permute-done.26.refs_1_), channel_id=1, source_target_pairs={{0,2},{2,0},{4,6},{6,4},{8,10},{10,8},{12,14},{14,12},{16,18},{18,... | collective-permute-start | bytes 589832 | tf_op jit(solution)/shard_map/ppermute | solution.py:46
  102.8 24.0 %collective-permute-start.31 = (bf16[256,1280]{1,0:T(8,128)(2,1)}, bf16[256,1280]{1,0:T(8,128)(2,1)}, u32[]{:S(2)}, u32[]{:S(2)}) collective-permute-start(bf16[256,1280]{1,0:T(8,128)(2,1)} %collective-permute-done.30.refs_1_), channel_id=1, source_target_pairs={{0,2},{2,0},{4,6},{6,4},{8,10},{10,8},{12,14},{14,12},{16,18},{18,... | collective-permute-start | bytes 1966088 | tf_op jit(solution)/shard_map/ppermute | solution.py:46
  109.0 8.2 %collective-permute-start.16 = (bf16[200,128]{1,0:T(8,128)(2,1)S(1)}, bf16[200,128]{1,0:T(8,128)(2,1)S(1)}, u32[]{:S(2)}, u32[]{:S(2)}) collective-permute-start(bf16[200,128]{1,0:T(8,128)(2,1)S(1)} %context_product.2.refs_0_), channel_id=1, source_target_pairs={{0,1},{1,0},{2,3},{3,2},{4,5},{5,4},{6,7},{7,6},{8,9},{9,8},{10,11... | collective-permute-start | bytes 153608 | tf_op jit(solution)/shard_map/ppermute | solution.py:46
  113.0 4.2 %collective-permute-start.29 = (bf16[200,128]{1,0:T(8,128)(2,1)S(1)}, bf16[200,128]{1,0:T(8,128)(2,1)S(1)}, u32[]{:S(2)}, u32[]{:S(2)}) collective-permute-start(bf16[200,128]{1,0:T(8,128)(2,1)S(1)} %context_product.3.refs_2_), channel_id=1, source_target_pairs={{0,1},{1,0},{2,3},{3,2},{4,5},{5,4},{6,7},{7,6},{8,9},{9,8},{10,11... | collective-permute-start | bytes 153608 | tf_op jit(solution)/shard_map/ppermute | solution.py:46
  122.6 14.2 %all-to-all-start.1 = ((bf16[16,64,128]{2,1,0:T(8,128)(2,1)}), bf16[16,64,128]{2,1,0:T(8,128)(2,1)}, u32[]{:S(2)}, u32[]{:S(2)}) async-start(bf16[16,64,128]{2,1,0:T(8,128)(2,1)} %get-tuple-element.71.o_ref), calls=%async_computation.1 | async-start | bytes 524288 | tf_op jit(solution)/shard_map/all_to_all | solution.py:77
  128.7 0.7 copy-start.4
  129.4 25.6 %copy-start.11 = (f32[1,2]{1,0:T(1,128)S(1)}, f32[1,2]{1,0:T(1,128)}, u32[]{:S(2)}) copy-start(f32[1,2]{1,0:T(1,128)} %ref_ref.1) | copy-start | bytes 28
  136.8 1.0 copy-start.5
  140.2 0.7 copy-start.3
  141.0 14.1 %all-to-all-start.2 = ((bf16[16,72,128]{2,1,0:T(8,128)(2,1)}), bf16[16,72,128]{2,1,0:T(8,128)(2,1)S(1)}, u32[]{:S(2)}, u32[]{:S(2)}) async-start(bf16[16,72,128]{2,1,0:T(8,128)(2,1)} %copy-done.3), calls=%async_computation.2 | async-start | bytes 589824 | tf_op jit(solution)/shard_map/all_to_all | solution.py:77
  155.0 1.0 copy-start.6
